TPU v7x, 512 devices: a whole 4x8x8 slice. The times are simulated.
512 devices in a mesh: dp: 64 (over z_hi, y, x), blk: 8 (over z_lo, core).
Axes of the slice: x: 4, y: 8, z: 8 (z_hi: 2, z_lo: 4; z = z_hi * 4 + z_lo), core: 2. Of those that a mesh axis runs over, the one named last changes fastest.
Arguments:
- train_act: bfloat16 [2048, 4096], P(('dp', 'blk')), may hold values from -3 to 3
- train_grad: bfloat16 [2048, 8192], P(('dp', 'blk')), may hold values from -3 to 3
- query_act: bfloat16 [256, 4096], P('dp', 'blk'), may hold values from -3 to 3
- query_grad: bfloat16 [256, 8192], P('dp'), may hold values from -3 to 3
- act_basis: bfloat16 [4096, 512], P('blk'), may hold values from -0.25 to 0.25
- grad_basis: bfloat16 [512, 8192], P(None, 'dp'), may hold values from -0.25 to 0.25
- eigenvalues: float32 [4096, 8192], P('blk', 'dp'), may hold values from 0.05 to 5
- example_ids: int32 [2048], replicated, may hold values from 0 to 127, never falling along the last dimension, each value on 1 to 48 neighbouring positions
- query_ids: int32 [256], replicated, may hold values from 0 to 15, never falling along the last dimension, each value on 1 to 48 neighbouring positions
Outputs:
- influence: float32 [128, 16], P('dp')
Inputs may be any that keep to these rules, and one draw needn't show every extreme that they name: `example_ids`: the tokens of one training example are contiguous and ids never fall; every example has a token. `query_ids`: the tokens of one query are contiguous and ids never fall; every query has a token.
All inputs are finite; a program needn't handle non-finite values.
Results may differ from a plain program's by a relative error of at most 0.0007.
The roundings to bfloat16 on the way count: a program that leaves them out, or rounds other values in their place, can miss the bound.
Values may be sent and summed in bfloat16 or wider, within the bound.
No kernel may reach another device: no remote copies, remote signals or barrier semaphores. Data moves between devices by JAX's collectives and lax.ppermute only.
A program may use at most 64 MiB of HBM per device.

v0:
```python
import jax
import jax.numpy as jnp
from jax import lax
from jax.sharding import PartitionSpec as P

D = 4096
FF = 8192
QUERIES = 16
EX_DP = 2


def partner(block, axis, stride):
    count = lax.axis_size(axis)
    route = []
    for low in range(count):
        high = low | 1 << stride
        if high != low and high < count:
            route += [(low, high), (high, low)]
    return lax.ppermute(block, axis, route)


def rotate_blocks(row_data, basis):
    row_count = row_data.shape[0]
    block_size = basis.shape[1]
    count_blocks = basis.shape[0] // block_size
    turned = jnp.einsum(
        "tnk,nkl->tnl",
        row_data.reshape(row_count, count_blocks, block_size),
        basis.reshape(count_blocks, block_size, block_size),
        preferred_element_type=jnp.float32,
    )
    return turned.reshape(row_count, count_blocks * block_size).astype(jnp.bfloat16)


def rotate_columns(row_data, basis):
    row_count = row_data.shape[0]
    full_width = row_data.shape[1]
    block_size = basis.shape[0]
    col_width = basis.shape[1]
    count_blocks = full_width // block_size
    turned = jnp.einsum(
        "tmk,kml->tml",
        row_data.reshape(row_count, count_blocks, block_size),
        basis.reshape(block_size, count_blocks, col_width // count_blocks),
        preferred_element_type=jnp.float32,
    )
    return turned.reshape(row_count, col_width).astype(jnp.bfloat16)


def join_pair(mine, other, is_upper):
    return jnp.where(is_upper, jnp.concatenate([other, mine], 1), jnp.concatenate([mine, other], 1))


def shards(
    train_act,
    train_grad,
    query_act,
    query_grad,
    act_basis,
    grad_basis,
    eigenvalues,
    example_ids,
    query_ids,
):
    devices_dp = lax.axis_size("dp")
    block_size = grad_basis.shape[0]
    col_width = grad_basis.shape[1]
    owned_width = act_basis.shape[0]
    eigen_sum = lax.psum(jnp.sum(eigenvalues), ("dp", "blk"))
    damping = 0.1 * eigen_sum / (D * FF)
    owned_rows = lax.all_to_all(train_act, "blk", split_axis=1, concat_axis=0, tiled=True)
    query_all = lax.all_gather(rotate_blocks(query_act, act_basis), "dp", axis=0, tiled=True)
    train_cols, query_cols = (
        lax.all_to_all(train_grad, "dp", split_axis=1, concat_axis=0, tiled=True),
        lax.all_to_all(query_grad, "dp", split_axis=1, concat_axis=0, tiled=True),
    )
    position = lax.axis_index("dp")
    for bit_index in range((block_size // col_width).bit_length() - 1):
        other_train, other_query = partner((train_cols, query_cols), "dp", bit_index)
        is_upper = position >> bit_index & 1 == 1
        train_cols = join_pair(train_cols, other_train, is_upper)
        query_cols = join_pair(query_cols, other_query, is_upper)
    grad_mine = rotate_columns(train_cols, grad_basis)
    query_grad_rot = rotate_columns(query_cols, grad_basis)
    grad_all = lax.all_gather(
        grad_mine.reshape(devices_dp, 1, grad_mine.shape[0] // devices_dp, col_width),
        "blk",
        axis=1,
        tiled=True,
    )
    grad_all = grad_all.reshape(
        grad_all.shape[0] * grad_all.shape[1] * grad_all.shape[2], col_width
    )
    one_query = (query_ids[:, None] == jnp.arange(QUERIES, dtype=jnp.int32)[None, :]).astype(
        jnp.bfloat16
    )
    weighted = one_query.T[:, :, None] * query_all[None, :, :]
    query_gram = jnp.einsum(
        "qti,tj->iqj", weighted, query_grad_rot, preferred_element_type=jnp.float32
    )
    norm_scale = float(D * FF) ** (-0.5)
    precond = (query_gram / (eigenvalues[:, None, :] + damping) * norm_scale).astype(jnp.bfloat16)
    precond = precond.reshape(owned_width, QUERIES * col_width)
    shard_rows = lax.all_gather(rotate_blocks(owned_rows, act_basis), "dp", axis=0, tiled=True)
    row_count = shard_rows.shape[0]
    mixed_rows = jnp.dot(shard_rows, precond, preferred_element_type=jnp.float32).reshape(
        row_count, QUERIES, col_width
    )
    token_score = jnp.sum(mixed_rows * grad_all[:, None, :].astype(jnp.float32), axis=2)
    example_count = EX_DP * devices_dp
    one_example = (
        example_ids[:, None] == jnp.arange(example_count, dtype=jnp.int32)[None, :]
    ).astype(jnp.float32)
    partial_scores = jnp.dot(one_example.T, token_score, precision=lax.Precision.HIGHEST)
    all_scores = lax.psum(partial_scores, ("dp", "blk"))
    return lax.dynamic_slice_in_dim(all_scores, lax.axis_index("dp") * EX_DP, EX_DP, 0)


def solution(mesh):
    placed = (
        P(("dp", "blk"), None),
        P(("dp", "blk"), None),
        P("dp", "blk"),
        P("dp", None),
        P("blk", None),
        P(None, "dp"),
        P("blk", "dp"),
        P(),
        P(),
    )
    return jax.shard_map(
        shards, mesh=mesh, in_specs=placed, out_specs=P("dp", None), check_vma=False
    )
```

profile of v0, /device:TPU:1, one launch (start us, length us, event | category | flops | bytes accessed | tf_op | source)
XLA Modules:
  0.0 528.6 jit_solution(4616958831097814002)
XLA Ops:
  6.5 15.2 %all_to_all.54 = bf16[4,8,512]{2,0,1:T(4,128)(2,1)S(1)} all-to-all(bf16[4,8,512]{2,0,1:T(4,128)(2,1)} %bitcast.73), channel_id=1, replica_groups=mesh['dp'=64,'blk'=8] {'blk'}, dimensions={1} | all-to-all | bytes 65536 | tf_op jit(solution)/shard_map/all_to_all | solution.py:71
  21.8 0.8 fusion.10
  22.6 1.6 reduce_sum.18
  24.2 14.7 %all-to-all-start.2 = ((bf16[4,64,128]{2,0,1:T(4,128)(2,1)}), bf16[4,64,128]{2,0,1:T(4,128)(2,1)S(1)}, u32[]{:S(2)}, u32[]{:S(2)}) async-start(bf16[4,64,128]{2,0,1:T(4,128)(2,1)} %bitcast.71), calls=%async_computation.2 | async-start | bytes 131072 | tf_op jit(solution)/shard_map/all_to_all | solution.py:74
  38.9 104.2 %psum.14 = f32[]{:T(128)} all-reduce(f32[]{:T(128)} %reduce_sum.18), channel_id=1, replica_groups=mesh['dp'=64,'blk'=8] {'dp','blk'}, use_global_device_ids=true, to_apply=%region_1.0 | all-reduce | flops 1 | bytes 8 | tf_op jit(solution)/shard_map/psum | solution.py:69
  143.7 1.0 broadcast_add_fusion
  144.7 0.7 fusion.34
  145.4 10.7 %all-to-all-start.1 = ((bf16[4,64,128]{2,0,1:T(4,128)(2,1)}), bf16[4,64,128]{2,0,1:T(4,128)(2,1)S(1)}, u32[]{:S(2)}, u32[]{:S(2)}) async-start(bf16[4,64,128]{2,0,1:T(4,128)(2,1)} %bitcast.72), calls=%async_computation.1 | async-start | bytes 131072 | tf_op jit(solution)/shard_map/all_to_all | solution.py:75
  156.1 2.9 collective-permute-start.2
  159.0 0.9 fusion.11
  159.9 9.7 %all-to-all-done.1 = bf16[4,64,128]{2,0,1:T(4,128)(2,1)S(1)} async-done(((bf16[4,64,128]{2,0,1:T(4,128)(2,1)}), bf16[4,64,128]{2,0,1:T(4,128)(2,1)S(1)}, u32[]{:S(2)}, u32[]{:S(2)}) %all-to-all-start.1) | async-done | bytes 65568 | tf_op jit(solution)/shard_map/all_to_all | solution.py:75
  169.6 2.2 collective-permute-start
  171.9 3.9 collective-permute-start.3
  175.9 189.5 %all-gather.1 = bf16[256,1,512]{2,1,0:T(2,128)(2,1)S(1)} all-gather(bf16[4,1,512]{2,1,0:T(2,128)(2,1)S(1)} %copy.34), channel_id=3, replica_groups=mesh['dp'=64,'blk'=8] {'dp'}, dimensions={0}, use_global_device_ids=true | all-gather | bytes 266240 | tf_op jit(solution)/shard_map/all_gather | solution.py:72
  365.3 0.1 copy.36
  365.5 1.9 collective-permute-start.1
  367.5 0.2 convolution_convert_fusion
  367.7 45.3 %all_gather.11 = bf16[64,8,4,128]{3,2,1,0:T(4,128)(2,1)S(1)} all-gather(bf16[64,1,4,128]{3,2,1,0:T(4,128)(2,1)S(1)} %bitcast.70), channel_id=1, replica_groups=mesh['dp'=64,'blk'=8] {'blk'}, dimensions={1}, use_global_device_ids=true | all-gather | bytes 589824 | tf_op jit(solution)/shard_map/all_gather | solution.py:85
  413.0 0.2 copy.39
  413.3 3.0 fusion.2
  416.2 7.7 %multiply_reduce_fusion = f32[2048,16]{0,1:T(8,128)S(1)} fusion(f32[2048,128]{0,1:T(8,128)S(1)} %copy.39, bf16[2048,1,512]{2,0,1:T(8,128)(2,1)} %all-gather.4.cloned.1.call-done, f32[128,16,512]{2,0,1:T(8,128)} %fusion.2, f32[512,128]{0,1:T(8,128)S(1)} %copy.36), kind=kOutput, calls=%fused_computation | convolution fusion | flops 4306468864 | bytes 7733248 | tf_op jit(solution)/shard_map/dot_general | solution.py:106
  424.0 1.1 fusion.13
  425.1 96.1 %psum.15 = f32[128,16]{1,0:T(8,128)S(1)} all-reduce(f32[128,16]{1,0:T(8,128)S(1)} %fusion.13), channel_id=1, replica_groups=mesh['dp'=64,'blk'=8] {'dp','blk'}, use_global_device_ids=true, to_apply=%region_3.4 | all-reduce | flops 2048 | bytes 16384 | tf_op jit(solution)/shard_map/psum | solution.py:115
  521.1 0.6 constant_dynamic-slice_fusion
  (19 shorter events, 0.2 us)
Async XLA Ops:
  6.5 15.2 %copy-start = (bf16[512,512]{1,0:T(8,128)(2,1)S(1)}, bf16[512,512]{1,0:T(8,128)(2,1)}, u32[]{:S(2)}) copy-start(bf16[512,512]{1,0:T(8,128)(2,1)} %param.13) | copy-start | bytes 1572868
  6.5 360.9 %copy-start.1 = (bf16[512,128]{1,0:T(8,128)(2,1)S(1)}, bf16[512,128]{1,0:T(8,128)(2,1)}, u32[]{:S(2)}) copy-start(bf16[512,128]{1,0:T(8,128)(2,1)} %param.14) | copy-start | bytes 393220
  6.5 409.7 %all-gather.4.cloned.1.call-start = ((), (), s32[]{:S(2)}) async-start(), calls=%async_computation.3 | async-start | bytes 2129920 | tf_op jit(solution)/shard_map/all_gather | solution.py:104
  24.2 121.2 %all-to-all-start.2 = ((bf16[4,64,128]{2,0,1:T(4,128)(2,1)}), bf16[4,64,128]{2,0,1:T(4,128)(2,1)S(1)}, u32[]{:S(2)}, u32[]{:S(2)}) async-start(bf16[4,64,128]{2,0,1:T(4,128)(2,1)} %bitcast.71), calls=%async_computation.2 | async-start | bytes 131072 | tf_op jit(solution)/shard_map/all_to_all | solution.py:74
  145.4 24.2 %all-to-all-start.1 = ((bf16[4,64,128]{2,0,1:T(4,128)(2,1)}), bf16[4,64,128]{2,0,1:T(4,128)(2,1)S(1)}, u32[]{:S(2)}, u32[]{:S(2)}) async-start(bf16[4,64,128]{2,0,1:T(4,128)(2,1)} %bitcast.72), calls=%async_computation.1 | async-start | bytes 131072 | tf_op jit(solution)/shard_map/all_to_all | solution.py:75
  156.1 15.7 %collective-permute-start.2 = (bf16[256,128]{1,0:T(8,128)(2,1)S(1)}, bf16[256,128]{1,0:T(8,128)(2,1)S(1)}, u32[]{:S(2)}, u32[]{:S(2)}) collective-permute-start(bf16[256,128]{1,0:T(8,128)(2,1)S(1)} %bitcast.67), channel_id=1, source_target_pairs={{0,8},{8,0},{16,24},{24,16},{32,40},{40,32},{48,56},{56,48},{64,72... | collective-permute-start | bytes 196616 | tf_op jit(solution)/shard_map/ppermute | solution.py:19
  169.6 195.8 %collective-permute-start = (bf16[256,128]{1,0:T(8,128)(2,1)S(1)}, bf16[256,128]{1,0:T(8,128)(2,1)S(1)}, u32[]{:S(2)}, u32[]{:S(2)}) collective-permute-start(bf16[256,128]{1,0:T(8,128)(2,1)S(1)} %bitcast.65), channel_id=1, source_target_pairs={{0,8},{8,0},{16,24},{24,16},{32,40},{40,32},{48,56},{56,48},{64,72... | collective-permute-start | bytes 196616 | tf_op jit(solution)/shard_map/ppermute | solution.py:19
  171.9 195.6 %collective-permute-start.3 = (bf16[256,256]{1,0:T(8,128)(2,1)S(1)}, bf16[256,256]{1,0:T(8,128)(2,1)S(1)}, u32[]{:S(2)}, u32[]{:S(2)}) collective-permute-start(bf16[256,256]{1,0:T(8,128)(2,1)S(1)} %maximum_select_fusion.6), channel_id=1, source_target_pairs={{0,16},{16,0},{8,24},{24,8},{32,48},{48,32},{40,56},{56,40},{64,80... | collective-permute-start | bytes 393224 | tf_op jit(solution)/shard_map/ppermute | solution.py:19
  365.5 47.7 %collective-permute-start.1 = (bf16[256,256]{1,0:T(8,128)(2,1)S(1)}, bf16[256,256]{1,0:T(8,128)(2,1)S(1)}, u32[]{:S(2)}, u32[]{:S(2)}) collective-permute-start(bf16[256,256]{1,0:T(8,128)(2,1)S(1)} %maximum_select_fusion.5), channel_id=1, source_target_pairs={{0,16},{16,0},{8,24},{24,8},{32,48},{48,32},{40,56},{56,40},{64,80... | collective-permute-start | bytes 393224 | tf_op jit(solution)/shard_map/ppermute | solution.py:19
  416.2 7.7 %copy-start.2 = (s32[2048]{0:T(1024)S(1)}, s32[2048]{0:T(1024)}, u32[]{:S(2)}) copy-start(s32[2048]{0:T(1024)} %param.16) | copy-start | bytes 24580
Sparse Core Ops, SparseCore 0:
  22.7 136.6 all-gather.3
where the time goes:
time: 529 us
  blocking collectives  450 us (85%)
  starting transfers between devices  36.4 us (7%)
  between operations  14.2 us (3%)
  matrix products  13.6 us (3%)
  waiting for transfers between devices  9.75 us (2%)
    all_gather x1, blocking collectives, shards(): lax.all_gather(rotate_blocks(query_act, act_basis), 'dp', axis=0, tiled=T...  189 us
    psum x1, blocking collectives, shards(): eigen_sum = lax.psum(jnp.sum(eigenvalues), ('dp', 'blk'))  104 us
    psum x1, blocking collectives, shards(): all_scores = lax.psum(partial_scores, ('dp', 'blk'))  96.1 us
    all_gather x1, blocking collectives, shards(): lax.all_gather(grad_mine.reshape(devices_dp, 1, grad_mine.shape[0] // dev...  45.3 us
    all_to_all x1, blocking collectives, shards(): lax.all_to_all(train_act, 'blk', split_axis=1, concat_axis=0, tiled=True)  15.2 us
    all_to_all x1, starting transfers between devices, shards(): lax.all_to_all(train_grad, 'dp', split_axis=1, concat_axis=0, tiled=True)  14.7 us
    ppermute x4, starting transfers between devices, partner(): return lax.ppermute(block, axis, route)  11 us
    all_to_all x1, starting transfers between devices, shards(): lax.all_to_all(query_grad, 'dp', split_axis=1, concat_axis=0, tiled=True)  10.7 us
  transfers between devices with their start and end apart: 7, of which 1 were waited for; matrix products, arithmetic and copies ran while one was open for 1% of the time, Pallas kernels for 0%

commit v1 on v0

v1 whole, which is shorter than its diff:
```python
import functools

import jax
import jax.numpy as jnp
import numpy as np
from jax import lax
from jax.experimental import pallas as pl
from jax.experimental.pallas import tpu as pltpu
from jax.sharding import Mesh, PartitionSpec as P

D = 4096
FF = 8192
QUERIES = 16
EXAMPLES = 128
BF = jnp.bfloat16
F32 = jnp.float32
DP = ("zh", "y", "x")
BLK = ("zl", "c")
SIZES = (2, 8, 4, 4, 2)


def swap_all(block, axes):
    return lax.all_to_all(block, axes, split_axis=0, concat_axis=0, tiled=True)


def three_parts(value):
    high = lax.reduce_precision(value, 8, 7)
    rest = value - high
    mid = lax.reduce_precision(rest, 8, 7)
    low = rest - mid
    lane = lax.broadcasted_iota(jnp.int32, (1, 128), 1)
    row = jnp.where(lane == 0, high, jnp.where(lane == 1, mid, jnp.where(lane == 2, low, 0.0)))
    return row.astype(BF)


def score_kernel(
    core, act_own, grad_own, other, queries, act_basis, grad_basis, eigen, ids, query_ids, out, scale, grads
):
    mine = core[0]
    total = 0.0
    for peer in range(8):
        total += jnp.sum(queries[peer, 64:65, :].astype(F32))
    damping = 0.1 * total / (D * FF)
    norm = float(D * FF) ** (-0.5)
    for part in range(4):
        cols = pl.ds(part * 128, 128)
        scale[:, cols] = norm / (eigen[part] + damping)
    basis = act_basis[...]
    columns = jnp.concatenate([grad_basis[part] for part in range(4)], axis=1)

    def rotated(rows, by):
        return jnp.dot(rows, by, preferred_element_type=F32)

    acts = jnp.concatenate(
        [rotated(act_own[...], basis), rotated(other[:, 0:512], basis)], axis=0
    ).astype(BF)
    grads[0:256, :] = rotated(grad_own[...], columns).astype(BF).astype(F32)
    grads[256:512, :] = rotated(other[:, 512:1024], columns).astype(BF).astype(F32)
    query_act = jnp.concatenate([queries[2 * x + mine, 0:64, :] for x in range(4)], axis=0)
    query_grad = jnp.concatenate([queries[2 * x + 1 - mine, 0:64, :] for x in range(4)], axis=0)
    query_turned = rotated(query_act, basis).T.astype(BF)
    query_cols = rotated(query_grad, columns).astype(BF)
    lane = lax.broadcasted_iota(jnp.int32, (512, QUERIES), 1)
    scores = jnp.zeros((512, QUERIES), F32)
    for q in range(QUERIES):
        chosen = (query_ids[...] == q).astype(F32).astype(BF)
        gram = rotated(query_turned * chosen, query_cols)
        precond = (gram * scale[...]).astype(BF)
        mixed = rotated(acts, precond)
        score = jnp.sum(mixed * grads[...], axis=1, keepdims=True)
        scores = jnp.where(lane == q, score, scores)
    row = lax.broadcasted_iota(jnp.int32, (EXAMPLES, 512), 0)
    chosen = (ids[...] == row).astype(F32)
    out[...] = jnp.dot(chosen, scores, precision=lax.Precision.HIGHEST, preferred_element_type=F32)


def shards(
    train_act,
    train_grad,
    query_act,
    query_grad,
    act_basis,
    grad_basis,
    eigenvalues,
    example_ids,
    query_ids,
):
    x = lax.axis_index("x")
    zl = lax.axis_index("zl")
    c = lax.axis_index("c")
    eigen_all = lax.all_gather(eigenvalues, "x", axis=0)
    basis_all = lax.all_gather(grad_basis, "x", axis=0)
    sum_row = three_parts(jnp.sum(eigenvalues))

    acts = jnp.transpose(train_act.reshape(4, 4, 1024), (1, 0, 2))
    cols = jnp.transpose(train_grad.reshape(4, 16, 512), (1, 0, 2))
    query_part = lax.dynamic_index_in_dim(query_grad.reshape(4, 16, 4, 128), zl, 2, keepdims=False)
    query_part = jnp.transpose(query_part, (1, 0, 2))
    wide = (16, 4, 4)
    message = jnp.concatenate(
        [
            jnp.broadcast_to(acts[None], wide + (1024,)),
            jnp.broadcast_to(cols[:, None], wide + (512,)),
            jnp.broadcast_to(query_act[None, None], wide + (512,)),
            jnp.broadcast_to(query_part[:, None], wide + (128,)),
            jnp.broadcast_to(sum_row[None, None], wide + (128,)),
        ],
        axis=3,
    ).reshape(64, 4, 2304)
    got = swap_all(message, ("zh", "y", "zl"))

    pair = got[:, :, 0:1024].reshape(64, 4, 2, 512)
    act_own = lax.dynamic_index_in_dim(pair, c, 2, keepdims=False).reshape(256, 512)
    act_away = lax.dynamic_index_in_dim(pair, 1 - c, 2, keepdims=False).reshape(256, 512)
    grad_own = got[:, :, 1024:1536].reshape(256, 512)
    other = lax.ppermute(jnp.concatenate([act_away, grad_own], axis=1), "c", [(0, 1), (1, 0)])

    by_zl = got.reshape(16, 4, 4, 2304)
    query_rows = lax.dynamic_index_in_dim(by_zl, zl, 1, keepdims=False)[:, :, 1536:2048].reshape(64, 512)
    query_cols = jnp.transpose(by_zl[:, :, :, 2048:2176], (0, 2, 1, 3)).reshape(64, 512)
    partial = three_parts(jnp.sum(got[:, 0, 2176:2304].astype(F32)))
    partial = jnp.pad(partial, ((0, 7), (0, 384)))
    to_same = jnp.concatenate([query_rows, partial], axis=0)
    to_other = jnp.concatenate([query_cols, partial], axis=0)
    first = jnp.where(c == 0, to_same, to_other)
    second = jnp.where(c == 0, to_other, to_same)
    queries = jnp.broadcast_to(jnp.stack([first, second])[None], (4, 2, 72, 512)).reshape(8, 72, 512)
    queries = swap_all(queries, ("x", "c"))

    ids = lax.dynamic_index_in_dim(example_ids.reshape(16, 4, 4, 2, 4), x, 1, keepdims=False)
    ids_own = lax.dynamic_index_in_dim(ids, c, 2, keepdims=False).reshape(1, 256)
    ids_other = lax.dynamic_index_in_dim(ids, 1 - c, 2, keepdims=False).reshape(1, 256)
    ids = jnp.concatenate([ids_own, ids_other], axis=1)
    ids = (ids % 64) // 2 * 4 + ids // 64 * 2 + ids % 2
    query_order = jnp.transpose(query_ids.reshape(16, 4, 4), (1, 0, 2)).reshape(1, 256)

    vmem = pl.BlockSpec(memory_space=pltpu.VMEM)
    partial_scores = pl.pallas_call(
        score_kernel,
        out_shape=jax.ShapeDtypeStruct((EXAMPLES, QUERIES), F32),
        in_specs=[pl.BlockSpec(memory_space=pltpu.SMEM)] + [vmem] * 9,
        out_specs=vmem,
        scratch_shapes=[pltpu.VMEM((512, 512), F32), pltpu.VMEM((512, 512), F32)],
        compiler_params=pltpu.CompilerParams(vmem_limit_bytes=40 << 20),
    )(
        c.reshape(1).astype(jnp.int32),
        act_own,
        grad_own,
        other,
        queries,
        act_basis,
        basis_all,
        eigen_all,
        ids,
        query_order,
    )
    got = swap_all(partial_scores.reshape(32, 4, 16), ("y", "x"))
    sums = jnp.sum(got, axis=0).reshape(2, 1, 2, 16)
    got = swap_all(jnp.broadcast_to(sums, (2, 8, 2, 16)).reshape(16, 2, 16), ("zh", "zl", "c"))
    return jnp.sum(got, axis=0)


def solution(mesh):
    fine = Mesh(np.asarray(mesh.devices).reshape(SIZES), DP + BLK)
    placed = (
        P(DP + BLK, None),
        P(DP + BLK, None),
        P(DP, BLK),
        P(DP, None),
        P(BLK, None),
        P(None, DP),
        P(BLK, DP),
        P(),
        P(),
    )
    return jax.shard_map(
        shards, mesh=fine, in_specs=placed, out_specs=P(DP, None), check_vma=False
    )
```

time: 529 us -> 149 us (0.28)
  blocking collectives: 450 us -> 45.1 us
  waiting for transfers between devices: 9.75 us -> 28.9 us
  matrix products: 13.6 us -> 0 us
  local copies, waits for them, and re-layouts: 0.99 us -> 13.3 us
  starting transfers between devices: 36.4 us -> 25.4 us
  Pallas kernels: 0 us -> 9.28 us
  between operations: 14.2 us -> 21 us
    all_gather x2 -> x1, blocking collectives: 235 us -> 11.7 us  [shards(): basis_all = lax.all_gather(grad_basis, 'x', axis=0)]
    psum x2 -> x0, blocking collectives: 200 us -> none  [the longest x1 104 us: shards(): eigen_sum = lax.psum(jnp.sum(eigenvalues), ('dp', 'blk'))]
    all_to_all x2, waiting for transfers between devices: 9.72 us -> 28.2 us  [swap_all(): return lax.all_to_all(block, axes, split_axis=0, concat_axis=0, tiled=True)]
    all_to_all x1 -> x2, blocking collectives: 15.2 us -> 33.5 us  [swap_all(): return lax.all_to_all(block, axes, split_axis=0, concat_axis=0, tiled=True)]
    dot_general x6 -> x0, matrix products: 13.6 us -> none  [the longest x1 7.71 us: shards(): jnp.dot(shard_rows, precond, preferred_element_type=jnp.float32)]
    pallas_call x0 -> x1, Pallas kernels: none -> 9.28 us  [shards(): pl.pallas_call(score_kernel, out_shape=jax.ShapeDtypeStruct((EXAMPLES, QU...]
    ppermute x4 -> x1, starting transfers between devices: 11 us -> 2.05 us  [shards(): lax.ppermute(jnp.concatenate([act_away, grad_own], axis=1), 'c', [(0, 1),...]
  transfers between devices with their start and end apart: 7 -> 4, of which waited for: 1 -> 1; matrix products, arithmetic and copies ran while one was open for 1% -> 6% of each run, Pallas kernels for 0% -> 0%
where the time goes in v1:
time: 149 us
  blocking collectives  45.1 us (30%)
  waiting for transfers between devices  28.9 us (19%)
  starting transfers between devices  25.4 us (17%)
  between operations  21 us (14%)
  local copies, waits for them, and re-layouts  13.3 us (9%)
  Pallas kernels  9.28 us (6%)
  other arithmetic  5.67 us (4%)
    all_to_all x2, blocking collectives, swap_all(): return lax.all_to_all(block, axes, split_axis=0, concat_axis=0, tiled=True)  33.5 us
    all_to_all x2, waiting for transfers between devices, swap_all(): return lax.all_to_all(block, axes, split_axis=0, concat_axis=0, tiled=True)  28.2 us
    all_to_all x2, starting transfers between devices, swap_all(): return lax.all_to_all(block, axes, split_axis=0, concat_axis=0, tiled=True)  23.4 us
    all_gather x1, blocking collectives, shards(): basis_all = lax.all_gather(grad_basis, 'x', axis=0)  11.7 us
    pallas_call x1, Pallas kernels, shards(): pl.pallas_call(score_kernel, out_shape=jax.ShapeDtypeStruct((EXAMPLES, QU...  9.28 us
    unnamed x21, local copies, waits for them, and re-layouts  4.63 us
    dynamic_slice x1, local copies, waits for them, and re-layouts, shards(): lax.dynamic_index_in_dim(pair, 1 - c, 2, keepdims=False).reshape(256, 512)  3.3 us
  transfers between devices with their start and end apart: 4, of which 1 were waited for; matrix products, arithmetic and copies ran while one was open for 6% of the time, Pallas kernels for 0%

profile of v1, /device:TPU:1, one launch (start us, length us, event | category | flops | bytes accessed | tf_op | source)
XLA Modules:
  0.0 148.7 jit_solution(15862165880621527321)
XLA Ops:
  6.5 1.7 %reduce_sum.36 = f32[]{:T(128)} reduce(f32[512,128]{1,0:T(8,128)} %param.15, f32[]{:T(128)} %constant.134.clone.1), dimensions={0,1}, to_apply=%region_0.0 | reduce | flops 65535 | bytes 262152 | tf_op jit(solution)/shard_map/reduce_sum | solution.py:93
  11.9 1.3 fusion.2
  13.3 0.9 reshape.657
  14.3 0.8 reshape.655
  15.1 1.0 broadcast_dynamic-update-slice_fusion
  16.2 0.8 broadcast_dynamic-update-slice_fusion.2
  17.0 0.8 broadcast_dynamic-update-slice_fusion.1
  17.9 0.7 broadcast_dynamic-update-slice_fusion.4
  18.6 0.7 broadcast_dynamic-update-slice_fusion.3
  19.2 17.3 %all-to-all-start = ((bf16[64,4,2304]{2,1,0:T(4,128)(2,1)}), bf16[64,4,2304]{2,1,0:T(4,128)(2,1)S(1)}, u32[]{:S(2)}, u32[]{:S(2)}) async-start(bf16[64,4,2304]{2,1,0:T(4,128)(2,1)} %bitcast.4), calls=%async_computation | async-start | bytes 2359296 | tf_op jit(solution)/shard_map/all_to_all | solution.py:23
  36.6 0.7 all-gather.4.cloned.1.call-update
  38.4 28.2 %all-to-all-done = bf16[64,4,2304]{2,1,0:T(4,128)(2,1)S(1)} async-done(((bf16[64,4,2304]{2,1,0:T(4,128)(2,1)}), bf16[64,4,2304]{2,1,0:T(4,128)(2,1)S(1)}, u32[]{:S(2)}, u32[]{:S(2)}) %all-to-all-start) | async-done | bytes 1179680 | tf_op jit(solution)/shard_map/all_to_all | solution.py:23
  66.7 0.7 fusion
  71.0 1.3 fusion.3
  72.4 0.9 broadcast_in_dim.83
  73.2 6.1 %all-to-all-start.1 = ((bf16[8,72,512]{2,1,0:T(8,128)(2,1)}), bf16[8,72,512]{2,1,0:T(8,128)(2,1)S(1)}, u32[]{:S(2)}, u32[]{:S(2)}) async-start(bf16[8,72,512]{2,1,0:T(8,128)(2,1)} %bitcast.9), calls=%async_computation.1 | async-start | bytes 1179648 | tf_op jit(solution)/shard_map/all_to_all | solution.py:23
  79.7 3.3 %dynamic-slice_reduce_fusion = (bf16[64,4,512]{2,1,0:T(4,128)(2,1)S(1)}, bf16[64,4,512]{2,1,0:T(4,128)(2,1)S(1)}) fusion(bf16[64,4,2,512]{3,2,1,0:T(2,128)(2,1)S(1)} %reshape.659, s32[]{:T(128)S(6)} %select_n.170, s32[]{:T(128)S(6)} %select_n.169), kind=kLoop, calls=%fused_computation.1 | loop fusion | bytes 1048584 | tf_op jit(solution)/shard_map/jit(dynamic_index_in_dim)/dynamic_slice | solution.py:114
  83.3 2.1 %collective-permute-start = (bf16[256,1024]{1,0:T(8,128)(2,1)S(1)}, bf16[256,1024]{1,0:T(8,128)(2,1)S(1)}, u32[]{:S(2)}, u32[]{:S(2)}) collective-permute-start(bf16[256,1024]{1,0:T(8,128)(2,1)S(1)} %pad_maximum_fusion), channel_id=1, source_target_pairs={{0,1},{1,0},{2,3},{3,2},{4,5},{5,4},{6,7},{7,6},{8,9},{9,8},{10,11... | collective-permute-start | bytes 1572872 | tf_op jit(solution)/shard_map/ppermute | solution.py:116
  85.4 11.7 %all-gather = bf16[2048,128]{1,0:T(8,128)(2,1)S(1)} all-gather(bf16[512,128]{1,0:T(8,128)(2,1)S(1)} %copy-done.2), channel_id=2, replica_groups=mesh['zh'=2,'y'=8,'x'=4,'zl'=4,'c'=2] {'x'}, dimensions={0}, use_global_device_ids=true | all-gather | bytes 655360 | tf_op jit(solution)/shard_map/all_gather | solution.py:92
  97.2 1.2 copy-done
  98.5 9.3 %shard_map.91 = f32[128,16]{1,0:T(8,128)S(1)} custom-call(s32[1]{0:T(128)} %bitcast.core, bf16[256,512]{1,0:T(8,128)(2,1)S(1)} %reshape.660.act_own, bf16[256,512]{1,0:T(8,128)(2,1)S(1)} %reshape.661.grad_own, bf16[256,1024]{1,0:T(8,128)(2,1)S(1)} %collective-permute-done.other, bf16[8,72,512]{2,1,0:T(8,128)(2,1)S(1)} %all-to-all-done.1.queries, ...), custom_call_target="tpu_custom_call" | custom-call | tf_op jit(solution)/shard_map/pallas_call | solution.py:138
  107.8 18.0 %all_to_all.20 = f32[32,4,16]{2,1,0:T(4,128)S(1)} all-to-all(f32[32,4,16]{2,1,0:T(4,128)S(1)} %bitcast.31), channel_id=1, replica_groups=mesh['zh'=2,'y'=8,'x'=4,'zl'=4,'c'=2] {'y','x'}, dimensions={0} | all-to-all | bytes 16384 | tf_op jit(solution)/shard_map/all_to_all | solution.py:23
  125.8 15.5 %all_to_all.21 = f32[16,2,16]{2,1,0:T(2,128)S(1)} all-to-all(f32[16,2,16]{2,1,0:T(2,128)S(1)} %bitcast.39), channel_id=1, replica_groups=mesh['zh'=2,'y'=8,'x'=4,'zl'=4,'c'=2] {'zh','zl','c'}, dimensions={0} | all-to-all | bytes 4096 | tf_op jit(solution)/shard_map/all_to_all | solution.py:23
  141.3 0.6 reduce_sum.39
  (51 shorter events, 2.4 us)
Async XLA Ops:
  6.5 9.6 %copy-start.3 = (bf16[4,8192]{1,0:T(4,128)(2,1)S(1)}, bf16[4,8192]{1,0:T(4,128)(2,1)}, u32[]{:S(2)}) copy-start(bf16[4,8192]{1,0:T(4,128)(2,1)} %param.10) | copy-start | bytes 196612
  6.5 10.5 %copy-start.5 = (bf16[4,512]{1,0:T(4,128)(2,1)S(1)}, bf16[4,512]{1,0:T(4,128)(2,1)}, u32[]{:S(2)}) copy-start(bf16[4,512]{1,0:T(4,128)(2,1)} %param.11) | copy-start | bytes 12292
  19.2 18.0 %copy-start.4 = (s32[2048]{0:T(1024)S(1)}, s32[2048]{0:T(1024)}, u32[]{:S(2)}) copy-start(s32[2048]{0:T(1024)} %param.16) | copy-start | bytes 24580
  19.2 18.9 %copy-start.6 = (s32[256]{0:T(256)S(1)}, s32[256]{0:T(256)}, u32[]{:S(2)}) copy-start(s32[256]{0:T(256)} %param.17) | copy-start | bytes 3076
  19.2 47.4 %all-to-all-start = ((bf16[64,4,2304]{2,1,0:T(4,128)(2,1)}), bf16[64,4,2304]{2,1,0:T(4,128)(2,1)S(1)}, u32[]{:S(2)}, u32[]{:S(2)}) async-start(bf16[64,4,2304]{2,1,0:T(4,128)(2,1)} %bitcast.4), calls=%async_computation | async-start | bytes 2359296 | tf_op jit(solution)/shard_map/all_to_all | solution.py:23
  36.5 60.7 %all-gather.4.cloned.1.call-start = ((), (), s32[]{:S(2)}) async-start(), calls=%async_computation.4 | async-start | bytes 1310720 | tf_op jit(solution)/shard_map/all_gather | solution.py:91
  73.2 24.0 %all-to-all-start.1 = ((bf16[8,72,512]{2,1,0:T(8,128)(2,1)}), bf16[8,72,512]{2,1,0:T(8,128)(2,1)S(1)}, u32[]{:S(2)}, u32[]{:S(2)}) async-start(bf16[8,72,512]{2,1,0:T(8,128)(2,1)} %bitcast.9), calls=%async_computation.1 | async-start | bytes 1179648 | tf_op jit(solution)/shard_map/all_to_all | solution.py:23
  83.2 2.2 %copy-start.2 = (bf16[512,128]{1,0:T(8,128)(2,1)S(1)}, bf16[512,128]{1,0:T(8,128)(2,1)}, u32[]{:S(2)}) copy-start(bf16[512,128]{1,0:T(8,128)(2,1)} %param.14) | copy-start | bytes 393220
  83.3 14.0 %copy-start.1 = (bf16[512,512]{1,0:T(8,128)(2,1)S(1)}, bf16[512,512]{1,0:T(8,128)(2,1)}, u32[]{:S(2)}) copy-start(bf16[512,512]{1,0:T(8,128)(2,1)} %act_basis.1) | copy-start | bytes 1572868
  83.3 13.9 %collective-permute-start = (bf16[256,1024]{1,0:T(8,128)(2,1)S(1)}, bf16[256,1024]{1,0:T(8,128)(2,1)S(1)}, u32[]{:S(2)}, u32[]{:S(2)}) collective-permute-start(bf16[256,1024]{1,0:T(8,128)(2,1)S(1)} %pad_maximum_fusion), channel_id=1, source_target_pairs={{0,1},{1,0},{2,3},{3,2},{4,5},{5,4},{6,7},{7,6},{8,9},{9,8},{10,11... | collective-permute-start | bytes 1572872 | tf_op jit(solution)/shard_map/ppermute | solution.py:116
  97.2 1.2 copy-start
Sparse Core Ops, SparseCore 0:
  39.5 29.5 all-gather.3

commit v2 on v1

v2 whole, which is shorter than its diff:
```python
import jax
import jax.numpy as jnp
import numpy as np
from jax import lax
from jax.experimental import pallas as pl
from jax.experimental.pallas import tpu as pltpu
from jax.sharding import Mesh, PartitionSpec as P

D = 4096
FF = 8192
QUERIES = 16
EXAMPLES = 128
BF = jnp.bfloat16
F32 = jnp.float32
DP = ("zh", "y", "x")
BLK = ("zl", "c")
SIZES = (2, 8, 4, 4, 2)


def swap_all(block, axes):
    return lax.all_to_all(block, axes, split_axis=0, concat_axis=0, tiled=True)


def three_parts(rows):
    high = rows.astype(BF).astype(F32)
    rest = rows - high
    mid = rest.astype(BF).astype(F32)
    return high, mid, rest - mid


def pack_kernel(place, act, grad, query_act, query_grad, eigen, out):
    zl, c = place[0], place[1]
    sums = jnp.sum(jnp.sum(eigen[...].reshape(64, 8, 128), axis=0), axis=0, keepdims=True)
    sums = jnp.concatenate([*three_parts(sums), jnp.zeros((1, 128), F32)], axis=0).astype(BF)
    for z in range(4):
        own = act[:, pl.ds(pl.multiple_of(z * 1024 + c * 512, 128), 512)]
        away = act[:, pl.ds(pl.multiple_of(z * 1024 + 512 - c * 512, 128), 512)]
        for m in range(16):
            to = m * 4 + z
            for t in range(4):
                part = slice(t * 128, t * 128 + 128)
                cols = slice(m * 512 + t * 128, m * 512 + t * 128 + 128)
                out[to, t] = own[:, part]
                out[to, 4 + t] = away[:, part]
                out[to, 8 + t] = grad[:, cols]
                out[to, 12 + t] = query_grad[:, cols]
            out[to, 16] = sums
    for m in range(16):
        for t in range(4):
            out[m * 4 + zl, 12 + t] = query_act[:, t * 128 : t * 128 + 128]


def relay_kernel(place, got, out):
    zl, c = place[0], place[1]
    sums = jnp.sum(jnp.sum(got[:, 16].astype(F32), axis=0), axis=0, keepdims=True)
    sums = jnp.concatenate([*three_parts(sums), jnp.zeros((5, 128), F32)], axis=0).astype(BF)
    for core in range(2):
        source = zl + jnp.where(c == core, 0, 1 - 2 * (zl % 2))
        for t in range(4):
            for s in range(16):
                out[core, t * 64 + s * 4 : t * 64 + s * 4 + 4, :] = got[s * 4 + source, 12 + t]
        out[core, 256:264, :] = sums
        for x in range(1, 4):
            out[2 * x + core] = out[core]


def score_kernel(
    place, own, other, queries, act_basis, basis0, basis1, basis2, basis3, eigen, ids, query_ids, out,
    scale, columns, grads
):
    c, x = place[1], place[2]
    total = 0.0
    for peer in range(8):
        total += jnp.sum(queries[peer, 256:264, :].astype(F32))
    damping = 0.1 * total / (D * FF)
    norm = float(D * FF) ** (-0.5)
    for part in range(4):
        scale[:, part * 128 : part * 128 + 128] = norm / (eigen[part] + damping)
    for step, part in enumerate((basis0, basis1, basis2, basis3)):
        at = pl.multiple_of(lax.rem(x + 4 - step, 4) * 128, 128)
        columns[:, pl.ds(at, 128)] = part[...]
    basis = act_basis[...]

    def rotated(rows, by):
        return jnp.dot(rows, by, preferred_element_type=F32)

    def tiles(ref, first):
        return jnp.concatenate([ref[first + t] for t in range(4)], axis=1)

    def query_rows(core):
        rows = [
            jnp.concatenate([queries[2 * p + core, t * 64 : t * 64 + 64, :] for t in range(4)], axis=1)
            for p in range(4)
        ]
        return jnp.concatenate(rows, axis=0)

    acts = jnp.concatenate([rotated(tiles(own, 0), basis), rotated(tiles(other, 0), basis)], axis=0)
    acts = acts.astype(BF)
    grads[0:256, :] = rotated(tiles(own, 8), columns[...]).astype(BF).astype(F32)
    grads[256:512, :] = rotated(tiles(other, 4), columns[...]).astype(BF).astype(F32)
    query_turned = rotated(query_rows(c), basis).T.astype(BF)
    query_cols = rotated(query_rows(1 - c), columns[...]).astype(BF)
    lane = lax.broadcasted_iota(jnp.int32, (512, QUERIES), 1)
    scores = jnp.zeros((512, QUERIES), F32)
    for q in range(QUERIES):
        chosen = (query_ids[...] == q).astype(F32).astype(BF)
        gram = rotated(query_turned * chosen, query_cols)
        precond = (gram * scale[...]).astype(BF)
        mixed = rotated(acts, precond)
        score = jnp.sum(mixed * grads[...], axis=1, keepdims=True)
        scores = jnp.where(lane == q, score, scores)
    row = lax.broadcasted_iota(jnp.int32, (EXAMPLES, 512), 0)
    chosen = (ids[...] == row).astype(F32)
    out[...] = jnp.dot(chosen, scores, precision=lax.Precision.HIGHEST, preferred_element_type=F32)


def local_call(kernel, out_shape, dtype, place, arrays, scratch=()):
    vmem = pl.BlockSpec(memory_space=pltpu.VMEM)
    return pl.pallas_call(
        kernel,
        out_shape=jax.ShapeDtypeStruct(out_shape, dtype),
        in_specs=[pl.BlockSpec(memory_space=pltpu.SMEM)] + [vmem] * len(arrays),
        out_specs=vmem,
        scratch_shapes=list(scratch),
        compiler_params=pltpu.CompilerParams(vmem_limit_bytes=40 << 20),
    )(place, *arrays)


def shards(
    train_act,
    train_grad,
    query_act,
    query_grad,
    act_basis,
    grad_basis,
    eigenvalues,
    example_ids,
    query_ids,
):
    x = lax.axis_index("x")
    c = lax.axis_index("c")
    place = jnp.stack([lax.axis_index("zl"), c, x]).astype(jnp.int32)

    message = local_call(
        pack_kernel, (64, 17, 4, 128), BF, place, (train_act, train_grad, query_act, query_grad, eigenvalues)
    )
    message, eigenvalues, grad_basis = lax.optimization_barrier((message, eigenvalues, grad_basis))
    eigen_all = lax.all_gather(eigenvalues, "x", axis=0)
    bases = [lax.ppermute(grad_basis, "x", [(p, (p + step) % 4) for p in range(4)]) for step in (1, 2, 3)]
    got = swap_all(message, ("zh", "y", "zl"))

    ids = lax.dynamic_index_in_dim(example_ids.reshape(16, 4, 4, 2, 4), x, 1, keepdims=False)
    ids_own = lax.dynamic_index_in_dim(ids, c, 2, keepdims=False).reshape(1, 256)
    ids_other = lax.dynamic_index_in_dim(ids, 1 - c, 2, keepdims=False).reshape(1, 256)
    ids = jnp.concatenate([ids_own, ids_other], axis=1)
    ids = (ids % 64) // 2 * 4 + ids // 64 * 2 + ids % 2
    query_order = jnp.transpose(query_ids.reshape(16, 4, 4), (1, 0, 2)).reshape(1, 256)
    got, bases, ids, query_order = lax.optimization_barrier((got, bases, ids, query_order))

    queries = local_call(relay_kernel, (8, 264, 128), BF, place, (got,))
    queries = swap_all(queries, ("x", "c"))
    own = jnp.transpose(got[:, 0:12], (1, 0, 2, 3)).reshape(12, 256, 128)
    other = lax.ppermute(own[4:12], "c", [(0, 1), (1, 0)])

    partial_scores = local_call(
        score_kernel,
        (EXAMPLES, QUERIES),
        F32,
        place,
        (own, other, queries, act_basis, grad_basis, *bases, eigen_all, ids, query_order),
        (pltpu.VMEM((512, 512), F32), pltpu.VMEM((512, 512), BF), pltpu.VMEM((512, 512), F32)),
    )
    got = swap_all(partial_scores.reshape(32, 4, 16), ("y", "x"))
    sums = jnp.sum(got, axis=0).reshape(2, 1, 2, 16)
    got = swap_all(jnp.broadcast_to(sums, (2, 8, 2, 16)).reshape(16, 2, 16), ("zh", "zl", "c"))
    return jnp.sum(got, axis=0)


def solution(mesh):
    fine = Mesh(np.asarray(mesh.devices).reshape(SIZES), DP + BLK)
    placed = (
        P(DP + BLK, None),
        P(DP + BLK, None),
        P(DP, BLK),
        P(DP, None),
        P(BLK, None),
        P(None, DP),
        P(BLK, DP),
        P(),
        P(),
    )
    return jax.shard_map(
        shards, mesh=fine, in_specs=placed, out_specs=P(DP, None), check_vma=False
    )
```

time: 149 us -> 128 us (0.86)
  blocking collectives: 45.1 us -> 29.8 us
  starting transfers between devices: 25.4 us -> 36 us
  between operations: 21 us -> 13.6 us
  other arithmetic: 5.67 us -> 0.75 us
  local copies, waits for them, and re-layouts: 13.3 us -> 9.05 us
  waiting for transfers between devices: 28.9 us -> 24.9 us
  Pallas kernels: 9.28 us -> 13.2 us
    ppermute x1 -> x4, starting transfers between devices: 2.05 us -> 14.2 us  [the longest x3 10.5 us: shards(): lax.ppermute(grad_basis, 'x', [(p, (p + step) % 4) for p in range(4)])]
    all_gather x1 -> x0, blocking collectives: 11.7 us -> none  [shards(): basis_all = lax.all_gather(grad_basis, 'x', axis=0)]
    all_to_all x2, waiting for transfers between devices: 28.2 us -> 22.5 us  [swap_all(): return lax.all_to_all(block, axes, split_axis=0, concat_axis=0, tiled=True)]
    pallas_call x1 -> x3, Pallas kernels: 9.28 us -> 13.2 us  [local_call(): pl.pallas_call(kernel, out_shape=jax.ShapeDtypeStruct(out_shape, dtype),...]
    all_to_all x2, blocking collectives: 33.5 us -> 29.8 us  [swap_all(): return lax.all_to_all(block, axes, split_axis=0, concat_axis=0, tiled=True)]
    dynamic_slice x2 -> x0, local copies, waits for them, and re-layouts: 3.34 us -> none  [the longest x1 3.3 us: shards(): lax.dynamic_index_in_dim(pair, 1 - c, 2, keepdims=False).reshape(256, 512)]
    convert_element_type x2 -> x0, other arithmetic: 2.59 us -> none  [three_parts(): return row.astype(BF)]
    reduce_sum x2 -> x0, other arithmetic: 2.31 us -> none  [the longest x1 1.65 us: shards(): sum_row = three_parts(jnp.sum(eigenvalues))]
  transfers between devices with their start and end apart: 4 -> 7, of which waited for: 1 -> 3; matrix products, arithmetic and copies ran while one was open for 6% -> 3% of each run, Pallas kernels for 0% -> 1%
where the time goes in v2:
time: 128 us; the launch traced here: 127 us
  starting transfers between devices  36 us (28%)
  blocking collectives  29.8 us (23%)
  waiting for transfers between devices  24.9 us (19%)
  between operations  13.6 us (11%)
  Pallas kernels  13.2 us (10%)
  local copies, waits for them, and re-layouts  9.05 us (7%)
    all_to_all x2, blocking collectives, swap_all(): return lax.all_to_all(block, axes, split_axis=0, concat_axis=0, tiled=True)  29.8 us
    all_to_all x2, waiting for transfers between devices, swap_all(): return lax.all_to_all(block, axes, split_axis=0, concat_axis=0, tiled=True)  22.5 us
    all_to_all x2, starting transfers between devices, swap_all(): return lax.all_to_all(block, axes, split_axis=0, concat_axis=0, tiled=True)  21.8 us
    pallas_call x3, Pallas kernels, local_call(): pl.pallas_call(kernel, out_shape=jax.ShapeDtypeStruct(out_shape, dtype),...  13.2 us
    ppermute x3, starting transfers between devices, shards(): lax.ppermute(grad_basis, 'x', [(p, (p + step) % 4) for p in range(4)])  10.5 us
    unnamed x23, local copies, waits for them, and re-layouts  5.85 us
    ppermute x1, starting transfers between devices, shards(): other = lax.ppermute(own[4:12], 'c', [(0, 1), (1, 0)])  3.66 us
  transfers between devices with their start and end apart: 7, of which 3 were waited for; matrix products, arithmetic and copies ran while one was open for 3% of the time, Pallas kernels for 1%

profile of v2, /device:TPU:1, one launch (start us, length us, event | category | flops | bytes accessed | tf_op | source)
XLA Modules:
  0.0 127.4 jit_solution(7504624514880507894)
XLA Ops:
  6.6 0.9 copy-done.1
  7.6 0.8 copy-done.4
  8.4 0.8 copy-done.5
  9.2 0.8 copy-done.6
  10.0 0.7 copy-done.7
  10.7 1.9 %shard_map.91 = bf16[64,17,4,128]{3,2,1,0:T(4,128)(2,1)} custom-call(s32[3]{0:T(128)S(1)} %pad_add_fusion.place, bf16[4,4096]{1,0:T(4,128)(2,1)S(1)} %copy-done.6, bf16[4,8192]{1,0:T(4,128)(2,1)S(1)} %copy-done.4, bf16[4,512]{1,0:T(4,128)(2,1)S(1)} %copy-done.7, bf16[4,8192]{1,0:T(4,128)(2,1)S(1)} %copy-done.5, f32[512,128]{1,0:T(8,128)S(1)} %copy-done.1), custom_call_target="tpu_custom_call" | custom-call | tf_op jit(solution)/shard_map/pallas_call | solution.py:119
  12.6 17.3 %all-to-all-start = ((bf16[64,17,4,128]{3,2,1,0:T(4,128)(2,1)}), bf16[64,17,4,128]{3,2,1,0:T(4,128)(2,1)S(1)}, u32[]{:S(2)}, u32[]{:S(2)}) async-start(bf16[64,17,4,128]{3,2,1,0:T(4,128)(2,1)} %shard_map.91), calls=%async_computation | async-start | bytes 2228224 | tf_op jit(solution)/shard_map/all_to_all | solution.py:21
  29.9 0.7 all-gather.3.cloned.1.call-update
  30.6 3.1 %collective-permute-start = (bf16[512,128]{1,0:T(8,128)(2,1)S(1)}, bf16[512,128]{1,0:T(8,128)(2,1)S(1)}, u32[]{:S(2)}, u32[]{:S(2)}) collective-permute-start(bf16[512,128]{1,0:T(8,128)(2,1)S(1)} %copy-done.3), channel_id=1, source_target_pairs={{0,8},{8,16},{16,24},{24,0},{1,9},{9,17},{17,25},{25,1},{2,10},{10... | collective-permute-start | bytes 393224 | tf_op jit(solution)/shard_map/ppermute | solution.py:149
  33.7 4.4 %collective-permute-start.1 = (bf16[512,128]{1,0:T(8,128)(2,1)S(1)}, bf16[512,128]{1,0:T(8,128)(2,1)S(1)}, u32[]{:S(2)}, u32[]{:S(2)}) collective-permute-start(bf16[512,128]{1,0:T(8,128)(2,1)S(1)} %copy-done.3), channel_id=1, source_target_pairs={{0,16},{8,24},{16,0},{24,8},{1,17},{9,25},{17,1},{25,9},{2,18},{10... | collective-permute-start | bytes 393224 | tf_op jit(solution)/shard_map/ppermute | solution.py:149
  38.1 3.1 %collective-permute-start.2 = (bf16[512,128]{1,0:T(8,128)(2,1)S(1)}, bf16[512,128]{1,0:T(8,128)(2,1)S(1)}, u32[]{:S(2)}, u32[]{:S(2)}) collective-permute-start(bf16[512,128]{1,0:T(8,128)(2,1)S(1)} %copy-done.3), channel_id=1, source_target_pairs={{0,24},{8,0},{16,8},{24,16},{1,25},{9,1},{17,9},{25,17},{2,26},{10... | collective-permute-start | bytes 393224 | tf_op jit(solution)/shard_map/ppermute | solution.py:149
  42.4 1.7 %collective-permute-done.2.basis3 = bf16[512,128]{1,0:T(8,128)(2,1)S(1)} collective-permute-done((bf16[512,128]{1,0:T(8,128)(2,1)S(1)}, bf16[512,128]{1,0:T(8,128)(2,1)S(1)}, u32[]{:S(2)}, u32[]{:S(2)}) %collective-permute-start.2) | collective-permute-done | bytes 131104 | tf_op jit(solution)/shard_map/ppermute | solution.py:149
  44.1 14.4 %all-to-all-done.got = bf16[64,17,4,128]{3,2,1,0:T(4,128)(2,1)S(1)} async-done(((bf16[64,17,4,128]{3,2,1,0:T(4,128)(2,1)}), bf16[64,17,4,128]{3,2,1,0:T(4,128)(2,1)S(1)}, u32[]{:S(2)}, u32[]{:S(2)}) %all-to-all-start) | async-done | bytes 1114144 | tf_op jit(solution)/shard_map/all_to_all | solution.py:21
  59.1 0.5 copy-done.8
  59.6 3.7 %collective-permute-start.3 = (bf16[8,256,128]{2,1,0:T(8,128)(2,1)S(1)}, bf16[8,256,128]{2,1,0:T(8,128)(2,1)S(1)}, u32[]{:S(2)}, u32[]{:S(2)}) collective-permute-start(bf16[8,256,128]{2,1,0:T(8,128)(2,1)S(1)} %bitcast.15), channel_id=1, source_target_pairs={{0,1},{1,0},{2,3},{3,2},{4,5},{5,4},{6,7},{7,6},{8,9},{9,8},{10,11... | collective-permute-start | bytes 1572872 | tf_op jit(solution)/shard_map/ppermute | solution.py:163
  63.3 1.5 %shard_map.92 = bf16[8,264,128]{2,1,0:T(8,128)(2,1)} custom-call(s32[3]{0:T(128)S(1)} %pad_add_fusion.place, bf16[64,17,4,128]{3,2,1,0:T(4,128)(2,1)S(1)} %all-to-all-done.got), custom_call_target="tpu_custom_call" | custom-call | tf_op jit(solution)/shard_map/pallas_call | solution.py:119
  64.8 4.5 %all-to-all-start.1 = ((bf16[8,264,128]{2,1,0:T(8,128)(2,1)}), bf16[8,264,128]{2,1,0:T(8,128)(2,1)S(1)}, u32[]{:S(2)}, u32[]{:S(2)}) async-start(bf16[8,264,128]{2,1,0:T(8,128)(2,1)} %shard_map.92), calls=%async_computation.1 | async-start | bytes 1081344 | tf_op jit(solution)/shard_map/all_to_all | solution.py:21
  69.3 1.5 %copy.20 = bf16[12,64,4,128]{3,2,1,0:T(4,128)(2,1)S(1)} copy(bf16[12,64,4,128]{3,2,0,1:T(4,128)(2,1)} %copy-done.8) | data formatting | bytes 1572864 | tf_op jit(solution)/shard_map/transpose | solution.py:162
  70.8 8.2 %all-to-all-done.1.queries = bf16[8,264,128]{2,1,0:T(8,128)(2,1)S(1)} async-done(((bf16[8,264,128]{2,1,0:T(8,128)(2,1)}), bf16[8,264,128]{2,1,0:T(8,128)(2,1)S(1)}, u32[]{:S(2)}, u32[]{:S(2)}) %all-to-all-start.1) | async-done | bytes 540704 | tf_op jit(solution)/shard_map/all_to_all | solution.py:21
  79.0 1.2 copy-done
  80.2 9.9 %shard_map.93 = f32[128,16]{1,0:T(8,128)S(1)} custom-call(s32[3]{0:T(128)S(1)} %pad_add_fusion.place, bf16[12,256,128]{2,1,0:T(8,128)(2,1)S(1)} %bitcast.12, bf16[8,256,128]{2,1,0:T(8,128)(2,1)S(1)} %collective-permute-done.3.other, bf16[8,264,128]{2,1,0:T(8,128)(2,1)S(1)} %all-to-all-done.1.queries, bf16[512,512]{1,0:T(8,128)(2,1)S(1)} %copy-done.2, ...), custom_call_target="tpu_custom_call" | custom-call | tf_op jit(solution)/shard_map/pallas_call | solution.py:119
  90.1 16.8 %all_to_all.20 = f32[32,4,16]{2,1,0:T(4,128)S(1)} all-to-all(f32[32,4,16]{2,1,0:T(4,128)S(1)} %bitcast.14), channel_id=1, replica_groups=mesh['zh'=2,'y'=8,'x'=4,'zl'=4,'c'=2] {'y','x'}, dimensions={0} | all-to-all | bytes 16384 | tf_op jit(solution)/shard_map/all_to_all | solution.py:21
  106.9 13.0 %all_to_all.21 = f32[16,2,16]{2,1,0:T(2,128)S(1)} all-to-all(f32[16,2,16]{2,1,0:T(2,128)S(1)} %bitcast.17), channel_id=1, replica_groups=mesh['zh'=2,'y'=8,'x'=4,'zl'=4,'c'=2] {'zh','zl','c'}, dimensions={0} | all-to-all | bytes 4096 | tf_op jit(solution)/shard_map/all_to_all | solution.py:21
  119.9 0.6 reduce_sum.19
  (36 shorter events, 2.0 us)
Async XLA Ops:
  6.6 1.0 copy-start.1
  7.6 0.8 copy-start.4
  8.4 0.8 copy-start.5
  9.2 0.8 copy-start.6
  10.0 0.7 copy-start.7
  12.5 18.0 %copy-start.3 = (bf16[512,128]{1,0:T(8,128)(2,1)S(1)}, bf16[512,128]{1,0:T(8,128)(2,1)}, u32[]{:S(2)}) copy-start(bf16[512,128]{1,0:T(8,128)(2,1)} %basis0) | copy-start | bytes 393220
  12.5 28.6 %copy-start.9 = (s32[2048]{0:T(1024)S(1)}, s32[2048]{0:T(1024)}, u32[]{:S(2)}) copy-start(s32[2048]{0:T(1024)} %param.16) | copy-start | bytes 24580
  12.6 29.5 %copy-start.10 = (s32[256]{0:T(256)S(1)}, s32[256]{0:T(256)}, u32[]{:S(2)}) copy-start(s32[256]{0:T(256)} %param.17) | copy-start | bytes 3076
  12.6 45.9 %all-to-all-start = ((bf16[64,17,4,128]{3,2,1,0:T(4,128)(2,1)}), bf16[64,17,4,128]{3,2,1,0:T(4,128)(2,1)S(1)}, u32[]{:S(2)}, u32[]{:S(2)}) async-start(bf16[64,17,4,128]{3,2,1,0:T(4,128)(2,1)} %shard_map.91), calls=%async_computation | async-start | bytes 2228224 | tf_op jit(solution)/shard_map/all_to_all | solution.py:21
  29.8 41.0 %all-gather.3.cloned.1.call-start = ((), (), s32[]{:S(2)}) async-start(), calls=%async_computation.4 | async-start | bytes 1310720 | tf_op jit(solution)/shard_map/all_gather | solution.py:148
  30.6 11.8 %collective-permute-start = (bf16[512,128]{1,0:T(8,128)(2,1)S(1)}, bf16[512,128]{1,0:T(8,128)(2,1)S(1)}, u32[]{:S(2)}, u32[]{:S(2)}) collective-permute-start(bf16[512,128]{1,0:T(8,128)(2,1)S(1)} %copy-done.3), channel_id=1, source_target_pairs={{0,8},{8,16},{16,24},{24,0},{1,9},{9,17},{17,25},{25,1},{2,10},{10... | collective-permute-start | bytes 393224 | tf_op jit(solution)/shard_map/ppermute | solution.py:149
  33.7 8.7 %collective-permute-start.1 = (bf16[512,128]{1,0:T(8,128)(2,1)S(1)}, bf16[512,128]{1,0:T(8,128)(2,1)S(1)}, u32[]{:S(2)}, u32[]{:S(2)}) collective-permute-start(bf16[512,128]{1,0:T(8,128)(2,1)S(1)} %copy-done.3), channel_id=1, source_target_pairs={{0,16},{8,24},{16,0},{24,8},{1,17},{9,25},{17,1},{25,9},{2,18},{10... | collective-permute-start | bytes 393224 | tf_op jit(solution)/shard_map/ppermute | solution.py:149
  38.1 6.0 %collective-permute-start.2 = (bf16[512,128]{1,0:T(8,128)(2,1)S(1)}, bf16[512,128]{1,0:T(8,128)(2,1)S(1)}, u32[]{:S(2)}, u32[]{:S(2)}) collective-permute-start(bf16[512,128]{1,0:T(8,128)(2,1)S(1)} %copy-done.3), channel_id=1, source_target_pairs={{0,24},{8,0},{16,8},{24,16},{1,25},{9,1},{17,9},{25,17},{2,26},{10... | collective-permute-start | bytes 393224 | tf_op jit(solution)/shard_map/ppermute | solution.py:149
  58.7 0.9 copy-start.8
  59.6 19.3 %collective-permute-start.3 = (bf16[8,256,128]{2,1,0:T(8,128)(2,1)S(1)}, bf16[8,256,128]{2,1,0:T(8,128)(2,1)S(1)}, u32[]{:S(2)}, u32[]{:S(2)}) collective-permute-start(bf16[8,256,128]{2,1,0:T(8,128)(2,1)S(1)} %bitcast.15), channel_id=1, source_target_pairs={{0,1},{1,0},{2,3},{3,2},{4,5},{5,4},{6,7},{7,6},{8,9},{9,8},{10,11... | collective-permute-start | bytes 1572872 | tf_op jit(solution)/shard_map/ppermute | solution.py:163
  64.8 14.2 %copy-start.2 = (bf16[512,512]{1,0:T(8,128)(2,1)S(1)}, bf16[512,512]{1,0:T(8,128)(2,1)}, u32[]{:S(2)}) copy-start(bf16[512,512]{1,0:T(8,128)(2,1)} %act_basis.1) | copy-start | bytes 1572868
  64.8 14.2 %all-to-all-start.1 = ((bf16[8,264,128]{2,1,0:T(8,128)(2,1)}), bf16[8,264,128]{2,1,0:T(8,128)(2,1)S(1)}, u32[]{:S(2)}, u32[]{:S(2)}) async-start(bf16[8,264,128]{2,1,0:T(8,128)(2,1)} %shard_map.92), calls=%async_computation.1 | async-start | bytes 1081344 | tf_op jit(solution)/shard_map/all_to_all | solution.py:21
  79.0 1.2 copy-start
Sparse Core Ops, SparseCore 0:
  32.8 29.5 all-gather.2

commit v3 on v2

v3 whole, which is shorter than its diff:
```python
import jax
import jax.numpy as jnp
import numpy as np
from jax import lax
from jax.experimental import pallas as pl
from jax.experimental.pallas import tpu as pltpu
from jax.sharding import Mesh, PartitionSpec as P

D = 4096
FF = 8192
QUERIES = 16
EXAMPLES = 128
BF = jnp.bfloat16
F32 = jnp.float32
DP = ("zh", "y", "x")
BLK = ("zl", "c")
SIZES = (2, 8, 4, 4, 2)


def swap_all(block, axes):
    return lax.all_to_all(block, axes, split_axis=0, concat_axis=0, tiled=True)


def three_parts(rows):
    high = rows.astype(BF).astype(F32)
    rest = rows - high
    mid = rest.astype(BF).astype(F32)
    return high, mid, rest - mid


def pack_kernel(copies, act, grad, query_act, query_grad, eigen, out):
    zl, c = lax.axis_index("zl"), lax.axis_index("c")
    for copy in copies:
        copy.wait()
    sums = jnp.sum(jnp.sum(eigen[...].reshape(64, 8, 128), axis=0), axis=0, keepdims=True)
    sums = jnp.concatenate([*three_parts(sums), jnp.zeros((1, 128), F32)], axis=0).astype(BF)
    for z in range(4):
        own = act[:, pl.ds(pl.multiple_of(z * 1024 + c * 512, 128), 512)]
        away = act[:, pl.ds(pl.multiple_of(z * 1024 + 512 - c * 512, 128), 512)]
        for m in range(16):
            to = m * 4 + z
            for t in range(4):
                part = slice(t * 128, t * 128 + 128)
                cols = slice(m * 512 + t * 128, m * 512 + t * 128 + 128)
                out[to, t] = own[:, part]
                out[to, 4 + t] = away[:, part]
                out[to, 8 + t] = grad[:, cols]
                out[to, 12 + t] = query_grad[:, cols]
            out[to, 16] = sums
    for m in range(16):
        for t in range(4):
            out[m * 4 + zl, 12 + t] = query_act[:, t * 128 : t * 128 + 128]


def relay_kernel(copies, got, out):
    zl, c = lax.axis_index("zl"), lax.axis_index("c")
    sums = jnp.sum(jnp.sum(got[:, 16].astype(F32), axis=0), axis=0, keepdims=True)
    sums = jnp.concatenate([*three_parts(sums), jnp.zeros((5, 128), F32)], axis=0).astype(BF)
    for core in range(2):
        source = zl + jnp.where(c == core, 0, 1 - 2 * (zl % 2))
        for t in range(4):
            for s in range(16):
                out[core, t * 64 + s * 4 : t * 64 + s * 4 + 4, :] = got[s * 4 + source, 12 + t]
        out[core, 256:264, :] = sums
        for x in range(1, 4):
            out[2 * x + core] = out[core]


def rotated(rows, by):
    return jnp.dot(rows, by, preferred_element_type=F32)


def ring_slot(x, step):
    return pl.multiple_of(lax.rem(x + 4 - step, 4) * 128, 128)


def turn_kernel(copies, own, other, act_basis, basis0, basis1, basis2, basis3, acts, grads, columns):
    x = lax.axis_index("x")
    for copy in copies:
        copy.wait()
    for step, part in enumerate((basis0, basis1, basis2, basis3)):
        columns[:, pl.ds(ring_slot(x, step), 128)] = part[...]

    def tiles(ref, first):
        return jnp.concatenate([ref[first + t] for t in range(4)], axis=1)

    acts[0:256, :] = rotated(tiles(own, 0), act_basis[...]).astype(BF)
    acts[256:512, :] = rotated(tiles(other, 0), act_basis[...]).astype(BF)
    grads[0:256, :] = rotated(tiles(own, 8), columns[...]).astype(BF).astype(F32)
    grads[256:512, :] = rotated(tiles(other, 4), columns[...]).astype(BF).astype(F32)


def score_kernel(
    copies, acts, grads, columns, queries, act_basis, ids, query_ids, eigen0, eigen1, eigen2, eigen3, out, scale
):
    c, x = lax.axis_index("c"), lax.axis_index("x")
    for copy in copies:
        copy.wait()
    total = 0.0
    for peer in range(8):
        total += jnp.sum(queries[peer, 256:264, :].astype(F32))
    damping = 0.1 * total / (D * FF)
    norm = float(D * FF) ** (-0.5)
    for step, part in enumerate((eigen0, eigen1, eigen2, eigen3)):
        scale[:, pl.ds(ring_slot(x, step), 128)] = norm / (part[...] + damping)

    def query_rows(core):
        rows = [
            jnp.concatenate([queries[2 * p + core, t * 64 : t * 64 + 64, :] for t in range(4)], axis=1)
            for p in range(4)
        ]
        return jnp.concatenate(rows, axis=0)

    query_turned = rotated(query_rows(c), act_basis[...]).T.astype(BF)
    query_cols = rotated(query_rows(1 - c), columns[...]).astype(BF)
    lane = lax.broadcasted_iota(jnp.int32, (512, QUERIES), 1)
    scores = jnp.zeros((512, QUERIES), F32)
    for q in range(QUERIES):
        chosen = (query_ids[...] == q).astype(F32).astype(BF)
        gram = rotated(query_turned * chosen, query_cols)
        precond = (gram * scale[...]).astype(BF)
        mixed = rotated(acts[...], precond)
        score = jnp.sum(mixed * grads[...], axis=1, keepdims=True)
        scores = jnp.where(lane == q, score, scores)
    row = lax.broadcasted_iota(jnp.int32, (EXAMPLES, 512), 0)
    chosen = (ids[...] == row).astype(F32)
    out[...] = jnp.dot(chosen, scores, precision=lax.Precision.HIGHEST, preferred_element_type=F32)


def local_call(kernel, mib, outs, near, far, scratch=()):
    count = len(far)

    def body(*refs):
        refs = list(refs)
        held, refs = refs[: len(near)], refs[len(near) :]
        sources, refs = refs[:count], refs[count:]
        results, refs = refs[: len(outs)], refs[len(outs) :]
        buffers, refs = refs[:count], refs[count:]
        copies = []
        if count:
            done, refs = refs[0], refs[1:]
            copies = [pltpu.make_async_copy(sources[k], buffers[k], done.at[k]) for k in range(count)]
        for copy in copies:
            copy.start()
        kernel(copies, *held, *buffers, *results, *refs)

    staged = [pltpu.VMEM(array.shape, array.dtype) for array in far]
    if count:
        staged.append(pltpu.SemaphoreType.DMA((count,)))
    vmem = pl.BlockSpec(memory_space=pltpu.VMEM)
    arrays = [pltpu.with_memory_space_constraint(array, pltpu.VMEM) for array in near]
    arrays += [pltpu.with_memory_space_constraint(array, pltpu.HBM) for array in far]
    return pl.pallas_call(
        body,
        out_shape=[jax.ShapeDtypeStruct(shape, dtype) for shape, dtype in outs],
        in_specs=[vmem] * len(near) + [pl.BlockSpec(memory_space=pltpu.HBM)] * count,
        out_specs=[vmem] * len(outs),
        scratch_shapes=staged + list(scratch),
        compiler_params=pltpu.CompilerParams(vmem_limit_bytes=mib << 20),
        cost_estimate=pl.CostEstimate(flops=1000, transcendentals=0, bytes_accessed=1000),
    )(*arrays)


def ring_parts(block):
    return [block] + [
        lax.ppermute(block, "x", [(p, (p + step) % 4) for p in range(4)]) for step in (1, 2, 3)
    ]


def shards(
    train_act,
    train_grad,
    query_act,
    query_grad,
    act_basis,
    grad_basis,
    eigenvalues,
    example_ids,
    query_ids,
):
    x = lax.axis_index("x")
    c = lax.axis_index("c")
    (message,) = local_call(
        pack_kernel,
        6,
        [((64, 17, 4, 128), BF)],
        (),
        (train_act, train_grad, query_act, query_grad, eigenvalues),
    )
    message, eigenvalues, grad_basis = lax.optimization_barrier((message, eigenvalues, grad_basis))
    eigens = ring_parts(eigenvalues)
    bases = ring_parts(grad_basis)
    got = swap_all(message, ("zh", "y", "zl"))

    ids = lax.dynamic_index_in_dim(example_ids.reshape(16, 4, 4, 2, 4), x, 1, keepdims=False)
    ids_own = lax.dynamic_index_in_dim(ids, c, 2, keepdims=False).reshape(1, 256)
    ids_other = lax.dynamic_index_in_dim(ids, 1 - c, 2, keepdims=False).reshape(1, 256)
    ids = jnp.concatenate([ids_own, ids_other], axis=1)
    ids = (ids % 64) // 2 * 4 + ids // 64 * 2 + ids % 2
    query_order = jnp.transpose(query_ids.reshape(16, 4, 4), (1, 0, 2)).reshape(1, 256)
    got, eigens, bases, ids, query_order = lax.optimization_barrier((got, eigens, bases, ids, query_order))

    (queries,) = local_call(relay_kernel, 6, [((8, 264, 128), BF)], (got,), ())
    queries, got = lax.optimization_barrier((queries, got))
    queries = swap_all(queries, ("x", "c"))
    own = jnp.transpose(got[:, 0:12], (1, 0, 2, 3)).reshape(12, 256, 128)
    other = lax.ppermute(own[4:12], "c", [(0, 1), (1, 0)])
    acts, grads, columns = local_call(
        turn_kernel,
        12,
        [((512, 512), BF), ((512, 512), F32), ((512, 512), BF)],
        (own, other),
        (act_basis, *bases),
    )
    (partial_scores,) = local_call(
        score_kernel,
        20,
        [((EXAMPLES, QUERIES), F32)],
        (acts, grads, columns, queries),
        (act_basis, ids, query_order, *eigens),
        (pltpu.VMEM((512, 512), F32),),
    )
    got = swap_all(partial_scores.reshape(32, 4, 16), ("y", "x"))
    sums = jnp.sum(got, axis=0).reshape(2, 1, 2, 16)
    got = swap_all(jnp.broadcast_to(sums, (2, 8, 2, 16)).reshape(16, 2, 16), ("zh", "zl", "c"))
    return jnp.sum(got, axis=0)


def solution(mesh):
    fine = Mesh(np.asarray(mesh.devices).reshape(SIZES), DP + BLK)
    placed = (
        P(DP + BLK, None),
        P(DP + BLK, None),
        P(DP, BLK),
        P(DP, None),
        P(BLK, None),
        P(None, DP),
        P(BLK, DP),
        P(),
        P(),
    )
    return jax.shard_map(
        shards, mesh=fine, in_specs=placed, out_specs=P(DP, None), check_vma=False
    )
```

time: 128 us -> 111 us (0.87)
  between operations: 13.6 us -> 0.3 us
  waiting for transfers between devices: 24.9 us -> 15.5 us
  starting transfers between devices: 36 us -> 42.6 us
  local copies, waits for them, and re-layouts: 9.05 us -> 3.46 us
  Pallas kernels: 13.2 us -> 15.7 us
  blocking collectives: 29.8 us -> 31.9 us
    all_to_all x2, waiting for transfers between devices: 22.5 us -> 7.31 us  [swap_all(): return lax.all_to_all(block, axes, split_axis=0, concat_axis=0, tiled=True)]
    ppermute x3 -> x6, starting transfers between devices: 10.5 us -> 17.9 us  [ring_parts(): lax.ppermute(block, 'x', [(p, (p + step) % 4) for p in range(4)])]
    ppermute x3 -> x6, waiting for transfers between devices: 1.71 us -> 8.16 us  [ring_parts(): lax.ppermute(block, 'x', [(p, (p + step) % 4) for p in range(4)])]
    unnamed x23 -> x21, local copies, waits for them, and re-layouts: 5.85 us -> 0.83 us
    pallas_call x3 -> x4, Pallas kernels: 13.2 us -> 15.7 us  [local_call(): pl.pallas_call(body, out_shape=[jax.ShapeDtypeStruct(shape, dtype) for sh...]
    all_to_all x2, blocking collectives: 29.8 us -> 31.9 us  [swap_all(): return lax.all_to_all(block, axes, split_axis=0, concat_axis=0, tiled=True)]
  transfers between devices with their start and end apart: 7 -> 9, of which waited for: 3 -> 2; matrix products, arithmetic and copies ran while one was open for 3% -> 2% of each run, Pallas kernels for 1% -> 2%
where the time goes in v3:
time: 111 us
  starting transfers between devices  42.6 us (38%)
  blocking collectives  31.9 us (29%)
  Pallas kernels  15.7 us (14%)
  waiting for transfers between devices  15.5 us (14%)
  local copies, waits for them, and re-layouts  3.46 us (3%)
  other arithmetic  1.25 us (1%)
    all_to_all x2, blocking collectives, swap_all(): return lax.all_to_all(block, axes, split_axis=0, concat_axis=0, tiled=True)  31.9 us
    all_to_all x2, starting transfers between devices, swap_all(): return lax.all_to_all(block, axes, split_axis=0, concat_axis=0, tiled=True)  21 us
    ppermute x6, starting transfers between devices, ring_parts(): lax.ppermute(block, 'x', [(p, (p + step) % 4) for p in range(4)])  17.9 us
    pallas_call x4, Pallas kernels, local_call(): pl.pallas_call(body, out_shape=[jax.ShapeDtypeStruct(shape, dtype) for sh...  15.7 us
    ppermute x6, waiting for transfers between devices, ring_parts(): lax.ppermute(block, 'x', [(p, (p + step) % 4) for p in range(4)])  8.16 us
    all_to_all x2, waiting for transfers between devices, swap_all(): return lax.all_to_all(block, axes, split_axis=0, concat_axis=0, tiled=True)  7.31 us
    ppermute x1, starting transfers between devices, shards(): other = lax.ppermute(own[4:12], 'c', [(0, 1), (1, 0)])  3.57 us
  transfers between devices with their start and end apart: 9, of which 2 were waited for; matrix products, arithmetic and copies ran while one was open for 2% of the time, Pallas kernels for 2%

profile of v3, /device:TPU:1, one launch (start us, length us, event | category | flops | bytes accessed | tf_op | source)
XLA Modules:
  0.0 110.5 jit_solution(4358922852507216730)
XLA Ops:
  0.0 2.4 %shard_map.91 = bf16[64,17,4,128]{3,2,1,0:T(4,128)(2,1)} custom-call(bf16[4,4096]{1,0:T(4,128)(2,1)} %refs_0_.1, bf16[4,8192]{1,0:T(4,128)(2,1)} %refs_1_.1, bf16[4,512]{1,0:T(4,128)(2,1)} %refs_2_.2, bf16[4,8192]{1,0:T(4,128)(2,1)} %refs_3_.1, f32[512,128]{1,0:T(8,128)} %refs_7_), custom_call_target="tpu_custom_call" | custom-call | flops 1000 | bytes 1000 | tf_op jit(solution)/shard_map/pallas_call | solution.py:153
  2.5 17.3 %all-to-all-start = ((bf16[64,17,4,128]{3,2,1,0:T(4,128)(2,1)}), bf16[64,17,4,128]{3,2,1,0:T(4,128)(2,1)S(1)}, u32[]{:S(2)}, u32[]{:S(2)}) async-start(bf16[64,17,4,128]{3,2,1,0:T(4,128)(2,1)} %shard_map.91), calls=%async_computation | async-start | bytes 2228224 | tf_op jit(solution)/shard_map/all_to_all | solution.py:21
  19.8 4.4 %collective-permute-start.5 = (bf16[512,128]{1,0:T(8,128)(2,1)S(1)}, bf16[512,128]{1,0:T(8,128)(2,1)S(1)}, u32[]{:S(2)}, u32[]{:S(2)}) collective-permute-start(bf16[512,128]{1,0:T(8,128)(2,1)S(1)} %copy-done.4), channel_id=1, source_target_pairs={{0,24},{8,0},{16,8},{24,16},{1,25},{9,1},{17,9},{25,17},{2,26},{10... | collective-permute-start | bytes 393224 | tf_op jit(solution)/shard_map/ppermute | solution.py:166
  24.2 2.4 %collective-permute-start.4 = (bf16[512,128]{1,0:T(8,128)(2,1)S(1)}, bf16[512,128]{1,0:T(8,128)(2,1)S(1)}, u32[]{:S(2)}, u32[]{:S(2)}) collective-permute-start(bf16[512,128]{1,0:T(8,128)(2,1)S(1)} %copy-done.4), channel_id=1, source_target_pairs={{0,16},{8,24},{16,0},{24,8},{1,17},{9,25},{17,1},{25,9},{2,18},{10... | collective-permute-start | bytes 393224 | tf_op jit(solution)/shard_map/ppermute | solution.py:166
  26.6 2.8 %collective-permute-start.2 = (f32[512,128]{1,0:T(8,128)S(1)}, f32[512,128]{1,0:T(8,128)S(1)}, u32[]{:S(2)}, u32[]{:S(2)}) collective-permute-start(f32[512,128]{1,0:T(8,128)S(1)} %copy-done), channel_id=1, source_target_pairs={{0,24},{8,0},{16,8},{24,16},{1,25},{9,1},{17,9},{25,17},{2,26},{10... | collective-permute-start | bytes 786440 | tf_op jit(solution)/shard_map/ppermute | solution.py:166
  29.4 3.5 %collective-permute-start.1 = (f32[512,128]{1,0:T(8,128)S(1)}, f32[512,128]{1,0:T(8,128)S(1)}, u32[]{:S(2)}, u32[]{:S(2)}) collective-permute-start(f32[512,128]{1,0:T(8,128)S(1)} %copy-done), channel_id=1, source_target_pairs={{0,16},{8,24},{16,0},{24,8},{1,17},{9,25},{17,1},{25,9},{2,18},{10... | collective-permute-start | bytes 786440 | tf_op jit(solution)/shard_map/ppermute | solution.py:166
  32.9 2.8 %collective-permute-start = (f32[512,128]{1,0:T(8,128)S(1)}, f32[512,128]{1,0:T(8,128)S(1)}, u32[]{:S(2)}, u32[]{:S(2)}) collective-permute-start(f32[512,128]{1,0:T(8,128)S(1)} %copy-done), channel_id=1, source_target_pairs={{0,8},{8,16},{16,24},{24,0},{1,9},{9,17},{17,25},{25,1},{2,10},{10... | collective-permute-start | bytes 786440 | tf_op jit(solution)/shard_map/ppermute | solution.py:166
  35.7 0.4 reshape.445
  36.7 0.7 reshape.447.refs_6_
  37.4 2.1 %collective-permute-start.3 = (bf16[512,128]{1,0:T(8,128)(2,1)S(1)}, bf16[512,128]{1,0:T(8,128)(2,1)S(1)}, u32[]{:S(2)}, u32[]{:S(2)}) collective-permute-start(bf16[512,128]{1,0:T(8,128)(2,1)S(1)} %copy-done.4), channel_id=1, source_target_pairs={{0,8},{8,16},{16,24},{24,0},{1,9},{9,17},{17,25},{25,1},{2,10},{10... | collective-permute-start | bytes 393224 | tf_op jit(solution)/shard_map/ppermute | solution.py:166
  39.5 0.6 fusion.refs_5_
  40.1 8.1 %collective-permute-done.3.refs_4_ = bf16[512,128]{1,0:T(8,128)(2,1)S(1)} collective-permute-done((bf16[512,128]{1,0:T(8,128)(2,1)S(1)}, bf16[512,128]{1,0:T(8,128)(2,1)S(1)}, u32[]{:S(2)}, u32[]{:S(2)}) %collective-permute-start.3) | collective-permute-done | bytes 131104 | tf_op jit(solution)/shard_map/ppermute | solution.py:166
  48.4 0.6 copy-done.7
  49.1 1.0 shard_map.92
  50.1 0.3 slice_bitcast_fusion
  50.8 3.6 %collective-permute-start.6 = (bf16[8,256,128]{2,1,0:T(8,128)(2,1)S(1)}, bf16[8,256,128]{2,1,0:T(8,128)(2,1)S(1)}, u32[]{:S(2)}, u32[]{:S(2)}) collective-permute-start(bf16[8,256,128]{2,1,0:T(8,128)(2,1)S(1)} %bitcast.10), channel_id=1, source_target_pairs={{0,1},{1,0},{2,3},{3,2},{4,5},{5,4},{6,7},{7,6},{8,9},{9,8},{10,11... | collective-permute-start | bytes 1572872 | tf_op jit(solution)/shard_map/ppermute | solution.py:207
  54.3 3.8 %all-to-all-start.1 = ((bf16[8,264,128]{2,1,0:T(8,128)(2,1)}), bf16[8,264,128]{2,1,0:T(8,128)(2,1)S(1)}, u32[]{:S(2)}, u32[]{:S(2)}) async-start(bf16[8,264,128]{2,1,0:T(8,128)(2,1)} %shard_map.92), calls=%async_computation.1 | async-start | bytes 1081344 | tf_op jit(solution)/shard_map/all_to_all | solution.py:21
  58.1 0.3 copy.20
  58.5 2.0 %shard_map.93 = (bf16[512,512]{1,0:T(8,128)(2,1)S(1)}, f32[512,512]{1,0:T(8,128)S(1)}, bf16[512,512]{1,0:T(8,128)(2,1)S(1)}) custom-call(bf16[12,256,128]{2,1,0:T(8,128)(2,1)S(1)} %bitcast.8, bf16[8,256,128]{2,1,0:T(8,128)(2,1)S(1)} %collective-permute-done.6.refs_1_, bf16[512,512]{1,0:T(8,128)(2,1)} %refs_4_.3, bf16[512,128]{1,0:T(8,128)(2,1)} %refs_3_.2, ...), custom_call_target="tpu_custom_call" | custom-call | flops 1000 | bytes 1000 | tf_op jit(solution)/shard_map/pallas_call | solution.py:153
  60.5 7.3 %all-to-all-done.1.refs_3_ = bf16[8,264,128]{2,1,0:T(8,128)(2,1)S(1)} async-done(((bf16[8,264,128]{2,1,0:T(8,128)(2,1)}), bf16[8,264,128]{2,1,0:T(8,128)(2,1)S(1)}, u32[]{:S(2)}, u32[]{:S(2)}) %all-to-all-start.1) | async-done | bytes 540704 | tf_op jit(solution)/shard_map/all_to_all | solution.py:21
  67.7 10.3 %shard_map.94 = f32[128,16]{1,0:T(8,128)S(1)} custom-call(bf16[512,512]{1,0:T(8,128)(2,1)S(1)} %get-tuple-element.33.refs_0_, f32[512,512]{1,0:T(8,128)S(1)} %get-tuple-element.34.refs_1_, bf16[512,512]{1,0:T(8,128)(2,1)S(1)} %get-tuple-element.35.refs_2_, bf16[8,264,128]{2,1,0:T(8,128)(2,1)S(1)} %all-to-all-done.1.refs_3_, bf16[512,512]{1,0:T(8,128)(2,1)} %refs_4_.3, ...), custom_call_target="tpu_custom_call" | custom-call | flops 1000 | bytes 1000 | tf_op jit(solution)/shard_map/pallas_call | solution.py:153
  78.0 16.8 %all_to_all.20 = f32[32,4,16]{2,1,0:T(4,128)S(1)} all-to-all(f32[32,4,16]{2,1,0:T(4,128)S(1)} %bitcast.9), channel_id=1, replica_groups=mesh['zh'=2,'y'=8,'x'=4,'zl'=4,'c'=2] {'y','x'}, dimensions={0} | all-to-all | bytes 16384 | tf_op jit(solution)/shard_map/all_to_all | solution.py:21
  94.9 15.1 %all_to_all.21 = f32[16,2,16]{2,1,0:T(2,128)S(1)} all-to-all(f32[16,2,16]{2,1,0:T(2,128)S(1)} %bitcast.12), channel_id=1, replica_groups=mesh['zh'=2,'y'=8,'x'=4,'zl'=4,'c'=2] {'zh','zl','c'}, dimensions={0} | all-to-all | bytes 4096 | tf_op jit(solution)/shard_map/all_to_all | solution.py:21
  110.0 0.6 reduce_sum.19
  (37 shorter events, 1.3 us)
Async XLA Ops:
  2.4 17.3 %copy-start.4 = (bf16[512,128]{1,0:T(8,128)(2,1)S(1)}, bf16[512,128]{1,0:T(8,128)(2,1)}, u32[]{:S(2)}) copy-start(bf16[512,128]{1,0:T(8,128)(2,1)} %refs_3_.2) | copy-start | bytes 393220
  2.4 24.2 %copy-start = (f32[512,128]{1,0:T(8,128)S(1)}, f32[512,128]{1,0:T(8,128)}, u32[]{:S(2)}) copy-start(f32[512,128]{1,0:T(8,128)} %refs_7_) | copy-start | bytes 786436
  2.4 33.2 %copy-start.8 = (s32[2048]{0:T(1024)S(1)}, s32[2048]{0:T(1024)}, u32[]{:S(2)}) copy-start(s32[2048]{0:T(1024)} %param.16) | copy-start | bytes 24580
  2.5 34.1 %copy-start.9 = (s32[256]{0:T(256)S(1)}, s32[256]{0:T(256)}, u32[]{:S(2)}) copy-start(s32[256]{0:T(256)} %param.17) | copy-start | bytes 3076
  2.5 45.9 %all-to-all-start = ((bf16[64,17,4,128]{3,2,1,0:T(4,128)(2,1)}), bf16[64,17,4,128]{3,2,1,0:T(4,128)(2,1)S(1)}, u32[]{:S(2)}, u32[]{:S(2)}) async-start(bf16[64,17,4,128]{3,2,1,0:T(4,128)(2,1)} %shard_map.91), calls=%async_computation | async-start | bytes 2228224 | tf_op jit(solution)/shard_map/all_to_all | solution.py:21
  19.8 17.6 %collective-permute-start.5 = (bf16[512,128]{1,0:T(8,128)(2,1)S(1)}, bf16[512,128]{1,0:T(8,128)(2,1)S(1)}, u32[]{:S(2)}, u32[]{:S(2)}) collective-permute-start(bf16[512,128]{1,0:T(8,128)(2,1)S(1)} %copy-done.4), channel_id=1, source_target_pairs={{0,24},{8,0},{16,8},{24,16},{1,25},{9,1},{17,9},{25,17},{2,26},{10... | collective-permute-start | bytes 393224 | tf_op jit(solution)/shard_map/ppermute | solution.py:166
  24.2 16.0 %collective-permute-start.4 = (bf16[512,128]{1,0:T(8,128)(2,1)S(1)}, bf16[512,128]{1,0:T(8,128)(2,1)S(1)}, u32[]{:S(2)}, u32[]{:S(2)}) collective-permute-start(bf16[512,128]{1,0:T(8,128)(2,1)S(1)} %copy-done.4), channel_id=1, source_target_pairs={{0,16},{8,24},{16,0},{24,8},{1,17},{9,25},{17,1},{25,9},{2,18},{10... | collective-permute-start | bytes 393224 | tf_op jit(solution)/shard_map/ppermute | solution.py:166
  26.6 21.7 %collective-permute-start.2 = (f32[512,128]{1,0:T(8,128)S(1)}, f32[512,128]{1,0:T(8,128)S(1)}, u32[]{:S(2)}, u32[]{:S(2)}) collective-permute-start(f32[512,128]{1,0:T(8,128)S(1)} %copy-done), channel_id=1, source_target_pairs={{0,24},{8,0},{16,8},{24,16},{1,25},{9,1},{17,9},{25,17},{2,26},{10... | collective-permute-start | bytes 786440 | tf_op jit(solution)/shard_map/ppermute | solution.py:166
  29.4 18.9 %collective-permute-start.1 = (f32[512,128]{1,0:T(8,128)S(1)}, f32[512,128]{1,0:T(8,128)S(1)}, u32[]{:S(2)}, u32[]{:S(2)}) collective-permute-start(f32[512,128]{1,0:T(8,128)S(1)} %copy-done), channel_id=1, source_target_pairs={{0,16},{8,24},{16,0},{24,8},{1,17},{9,25},{17,1},{25,9},{2,18},{10... | collective-permute-start | bytes 786440 | tf_op jit(solution)/shard_map/ppermute | solution.py:166
  32.9 15.4 %collective-permute-start = (f32[512,128]{1,0:T(8,128)S(1)}, f32[512,128]{1,0:T(8,128)S(1)}, u32[]{:S(2)}, u32[]{:S(2)}) collective-permute-start(f32[512,128]{1,0:T(8,128)S(1)} %copy-done), channel_id=1, source_target_pairs={{0,8},{8,16},{16,24},{24,0},{1,9},{9,17},{17,25},{25,1},{2,10},{10... | collective-permute-start | bytes 786440 | tf_op jit(solution)/shard_map/ppermute | solution.py:166
  37.4 21.0 %copy-start.5 = (bf16[512,128]{1,0:T(8,128)(2,1)}, bf16[512,128]{1,0:T(8,128)(2,1)S(1)}, u32[]{:S(2)}) copy-start(bf16[512,128]{1,0:T(8,128)(2,1)S(1)} %collective-permute-done.5.refs_6_) | copy-start | bytes 393220
  37.4 10.9 %collective-permute-start.3 = (bf16[512,128]{1,0:T(8,128)(2,1)S(1)}, bf16[512,128]{1,0:T(8,128)(2,1)S(1)}, u32[]{:S(2)}, u32[]{:S(2)}) collective-permute-start(bf16[512,128]{1,0:T(8,128)(2,1)S(1)} %copy-done.4), channel_id=1, source_target_pairs={{0,8},{8,16},{16,24},{24,0},{1,9},{9,17},{17,25},{25,1},{2,10},{10... | collective-permute-start | bytes 393224 | tf_op jit(solution)/shard_map/ppermute | solution.py:166
  40.1 18.3 %copy-start.6 = (bf16[512,128]{1,0:T(8,128)(2,1)}, bf16[512,128]{1,0:T(8,128)(2,1)S(1)}, u32[]{:S(2)}) copy-start(bf16[512,128]{1,0:T(8,128)(2,1)S(1)} %collective-permute-done.4.refs_5_) | copy-start | bytes 393220
  48.3 0.6 copy-start.7
  48.3 0.7 copy-start.1
  48.3 0.9 copy-start.2
  48.3 2.1 %copy-start.3 = (f32[512,128]{1,0:T(8,128)}, f32[512,128]{1,0:T(8,128)S(1)}, u32[]{:S(2)}) copy-start(f32[512,128]{1,0:T(8,128)S(1)} %collective-permute-done.refs_8_) | copy-start | bytes 786436
  50.8 7.7 %collective-permute-start.6 = (bf16[8,256,128]{2,1,0:T(8,128)(2,1)S(1)}, bf16[8,256,128]{2,1,0:T(8,128)(2,1)S(1)}, u32[]{:S(2)}, u32[]{:S(2)}) collective-permute-start(bf16[8,256,128]{2,1,0:T(8,128)(2,1)S(1)} %bitcast.10), channel_id=1, source_target_pairs={{0,1},{1,0},{2,3},{3,2},{4,5},{5,4},{6,7},{7,6},{8,9},{9,8},{10,11... | collective-permute-start | bytes 1572872 | tf_op jit(solution)/shard_map/ppermute | solution.py:207
  54.3 13.4 %all-to-all-start.1 = ((bf16[8,264,128]{2,1,0:T(8,128)(2,1)}), bf16[8,264,128]{2,1,0:T(8,128)(2,1)S(1)}, u32[]{:S(2)}, u32[]{:S(2)}) async-start(bf16[8,264,128]{2,1,0:T(8,128)(2,1)} %shard_map.92), calls=%async_computation.1 | async-start | bytes 1081344 | tf_op jit(solution)/shard_map/all_to_all | solution.py:21

commit v4 on v3

--- a/solution.py
+++ b/solution.py
@@ -74,35 +74,38 @@
     return pl.multiple_of(lax.rem(x + 4 - step, 4) * 128, 128)
 
 
-def turn_kernel(copies, own, other, act_basis, basis0, basis1, basis2, basis3, acts, grads, columns):
+def turn_kernel(
+    copies, own, other, act_basis, basis0, basis1, basis2, basis3, eigen0, eigen1, eigen2, eigen3,
+    acts, grads, columns, eigen
+):
     x = lax.axis_index("x")
     for copy in copies:
         copy.wait()
     for step, part in enumerate((basis0, basis1, basis2, basis3)):
         columns[:, pl.ds(ring_slot(x, step), 128)] = part[...]
+    for step, part in enumerate((eigen0, eigen1, eigen2, eigen3)):
+        eigen[:, pl.ds(ring_slot(x, step), 128)] = part[...]
 
     def tiles(ref, first):
         return jnp.concatenate([ref[first + t] for t in range(4)], axis=1)
 
     acts[0:256, :] = rotated(tiles(own, 0), act_basis[...]).astype(BF)
     acts[256:512, :] = rotated(tiles(other, 0), act_basis[...]).astype(BF)
-    grads[0:256, :] = rotated(tiles(own, 8), columns[...]).astype(BF).astype(F32)
-    grads[256:512, :] = rotated(tiles(other, 4), columns[...]).astype(BF).astype(F32)
+    grads[0:256, :] = rotated(tiles(own, 8), columns[...]).astype(BF)
+    grads[256:512, :] = rotated(tiles(other, 4), columns[...]).astype(BF)
 
 
 def score_kernel(
-    copies, acts, grads, columns, queries, act_basis, ids, query_ids, eigen0, eigen1, eigen2, eigen3, out, scale
+    copies, acts, grads_in, columns, eigen, queries, act_basis, query_ids, ids, out, scale, grads
 ):
-    c, x = lax.axis_index("c"), lax.axis_index("x")
-    for copy in copies:
-        copy.wait()
+    c = lax.axis_index("c")
     total = 0.0
     for peer in range(8):
         total += jnp.sum(queries[peer, 256:264, :].astype(F32))
     damping = 0.1 * total / (D * FF)
     norm = float(D * FF) ** (-0.5)
-    for step, part in enumerate((eigen0, eigen1, eigen2, eigen3)):
-        scale[:, pl.ds(ring_slot(x, step), 128)] = norm / (part[...] + damping)
+    scale[...] = norm / (eigen[...] + damping)
+    grads[...] = grads_in[...].astype(F32)
 
     def query_rows(core):
         rows = [
@@ -111,6 +114,8 @@
         ]
         return jnp.concatenate(rows, axis=0)
 
+    for copy in copies:
+        copy.wait()
     query_turned = rotated(query_rows(c), act_basis[...]).T.astype(BF)
     query_cols = rotated(query_rows(1 - c), columns[...]).astype(BF)
     lane = lax.broadcasted_iota(jnp.int32, (512, QUERIES), 1)
@@ -124,7 +129,9 @@
         scores = jnp.where(lane == q, score, scores)
     row = lax.broadcasted_iota(jnp.int32, (EXAMPLES, 512), 0)
     chosen = (ids[...] == row).astype(F32)
-    out[...] = jnp.dot(chosen, scores, precision=lax.Precision.HIGHEST, preferred_element_type=F32)
+    sums = jnp.dot(chosen, scores, precision=lax.Precision.HIGHEST, preferred_element_type=F32)
+    sums = [sums[part * 32 : part * 32 + 32, :] for part in range(4)]
+    out[...] = jnp.concatenate(sums + [jnp.zeros((32, 64), F32)], axis=1)
 
 
 def local_call(kernel, mib, outs, near, far, scratch=()):
@@ -161,10 +168,12 @@
     )(*arrays)
 
 
-def ring_parts(block):
-    return [block] + [
-        lax.ppermute(block, "x", [(p, (p + step) % 4) for p in range(4)]) for step in (1, 2, 3)
-    ]
+def ring_parts(block, way):
+    def moved(part, step):
+        return lax.ppermute(part, "x", [(p, (p + step) % 4) for p in range(4)])
+
+    one, three = moved(block, 1), moved(block, 3)
+    return [block, one, moved(one, 1) if way == 1 else moved(three, 3), three]
 
 
 def shards(
@@ -188,42 +197,42 @@
         (train_act, train_grad, query_act, query_grad, eigenvalues),
     )
     message, eigenvalues, grad_basis = lax.optimization_barrier((message, eigenvalues, grad_basis))
-    eigens = ring_parts(eigenvalues)
-    bases = ring_parts(grad_basis)
+    eigens = ring_parts(eigenvalues, 3)
+    bases = ring_parts(grad_basis, 1)
     got = swap_all(message, ("zh", "y", "zl"))
 
     ids = lax.dynamic_index_in_dim(example_ids.reshape(16, 4, 4, 2, 4), x, 1, keepdims=False)
     ids_own = lax.dynamic_index_in_dim(ids, c, 2, keepdims=False).reshape(1, 256)
     ids_other = lax.dynamic_index_in_dim(ids, 1 - c, 2, keepdims=False).reshape(1, 256)
     ids = jnp.concatenate([ids_own, ids_other], axis=1)
-    ids = (ids % 64) // 2 * 4 + ids // 64 * 2 + ids % 2
+    ids = ids // 64 * 64 + ids % 2 * 32 + ids % 64 // 2
     query_order = jnp.transpose(query_ids.reshape(16, 4, 4), (1, 0, 2)).reshape(1, 256)
     got, eigens, bases, ids, query_order = lax.optimization_barrier((got, eigens, bases, ids, query_order))
 
     (queries,) = local_call(relay_kernel, 6, [((8, 264, 128), BF)], (got,), ())
     queries, got = lax.optimization_barrier((queries, got))
     queries = swap_all(queries, ("x", "c"))
+    other = lax.ppermute(got, "c", [(0, 1), (1, 0)])
     own = jnp.transpose(got[:, 0:12], (1, 0, 2, 3)).reshape(12, 256, 128)
-    other = lax.ppermute(own[4:12], "c", [(0, 1), (1, 0)])
-    acts, grads, columns = local_call(
+    other = jnp.transpose(other[:, 4:12], (1, 0, 2, 3)).reshape(8, 256, 128)
+    held = local_call(
         turn_kernel,
         12,
-        [((512, 512), BF), ((512, 512), F32), ((512, 512), BF)],
+        [((512, 512), BF), ((512, 512), BF), ((512, 512), BF), ((512, 512), F32)],
         (own, other),
-        (act_basis, *bases),
+        (act_basis, *bases, *eigens),
     )
     (partial_scores,) = local_call(
         score_kernel,
         20,
-        [((EXAMPLES, QUERIES), F32)],
-        (acts, grads, columns, queries),
-        (act_basis, ids, query_order, *eigens),
-        (pltpu.VMEM((512, 512), F32),),
-    )
-    got = swap_all(partial_scores.reshape(32, 4, 16), ("y", "x"))
-    sums = jnp.sum(got, axis=0).reshape(2, 1, 2, 16)
-    got = swap_all(jnp.broadcast_to(sums, (2, 8, 2, 16)).reshape(16, 2, 16), ("zh", "zl", "c"))
-    return jnp.sum(got, axis=0)
+        [((32, 128), F32)],
+        (*held, queries),
+        (act_basis, query_order, ids),
+        (pltpu.VMEM((512, 512), F32), pltpu.VMEM((512, 512), F32)),
+    )
+    sums = jnp.sum(swap_all(partial_scores, ("y", "x")), axis=0, keepdims=True)
+    sums = jnp.sum(swap_all(jnp.broadcast_to(sums, (16, 128)), ("zh", "zl", "c")), axis=0)
+    return lax.dynamic_slice_in_dim(sums, lax.axis_index("zh") * 32, 32, 0).reshape(2, 16)
 
 
 def solution(mesh):

time: 111 us -> 109 us (0.982)
  blocking collectives: 31.9 us -> 16.5 us
  starting transfers between devices: 42.6 us -> 49.7 us
  waiting for transfers between devices: 15.5 us -> 21.3 us
    all_to_all x2 -> x1, blocking collectives: 31.9 us -> 16.5 us  [swap_all(): return lax.all_to_all(block, axes, split_axis=0, concat_axis=0, tiled=True)]
    all_to_all x2 -> x3, waiting for transfers between devices: 7.31 us -> 16.6 us  [swap_all(): return lax.all_to_all(block, axes, split_axis=0, concat_axis=0, tiled=True)]
    all_to_all x2 -> x3, starting transfers between devices: 21 us -> 27.9 us  [swap_all(): return lax.all_to_all(block, axes, split_axis=0, concat_axis=0, tiled=True)]
    ppermute x7, waiting for transfers between devices: 8.16 us -> 4.7 us  [the longest x6 4.7 us: moved(): return lax.ppermute(part, 'x', [(p, (p + step) % 4) for p in range(4)])]
  transfers between devices with their start and end apart: 9 -> 10, of which waited for: 2 -> 4; matrix products, arithmetic and copies ran while one was open for 2% -> 3% of each run, Pallas kernels for 2% -> 2%
where the time goes in v4:
time: 109 us; the launch traced here: 108 us
  starting transfers between devices  49.7 us (46%)
  waiting for transfers between devices  21.3 us (20%)
  blocking collectives  16.5 us (15%)
  Pallas kernels  15.8 us (14%)
  local copies, waits for them, and re-layouts  4 us (4%)
    all_to_all x3, starting transfers between devices, swap_all(): return lax.all_to_all(block, axes, split_axis=0, concat_axis=0, tiled=True)  27.9 us
    ppermute x6, starting transfers between devices, moved(): return lax.ppermute(part, 'x', [(p, (p + step) % 4) for p in range(4)])  18.1 us
    all_to_all x3, waiting for transfers between devices, swap_all(): return lax.all_to_all(block, axes, split_axis=0, concat_axis=0, tiled=True)  16.6 us
    all_to_all x1, blocking collectives, swap_all(): return lax.all_to_all(block, axes, split_axis=0, concat_axis=0, tiled=True)  16.5 us
    pallas_call x4, Pallas kernels, local_call(): pl.pallas_call(body, out_shape=[jax.ShapeDtypeStruct(shape, dtype) for sh...  15.8 us
    ppermute x6, waiting for transfers between devices, moved(): return lax.ppermute(part, 'x', [(p, (p + step) % 4) for p in range(4)])  4.7 us
    ppermute x1, starting transfers between devices, shards(): other = lax.ppermute(got, 'c', [(0, 1), (1, 0)])  3.66 us
  transfers between devices with their start and end apart: 10, of which 4 were waited for; matrix products, arithmetic and copies ran while one was open for 3% of the time, Pallas kernels for 2%

profile of v4, /device:TPU:1, one launch (start us, length us, event | category | flops | bytes accessed | tf_op | source)
XLA Modules:
  0.0 108.3 jit_solution(17781467968980544509)
XLA Ops:
  0.0 2.4 %shard_map.91 = bf16[64,17,4,128]{3,2,1,0:T(4,128)(2,1)} custom-call(bf16[4,4096]{1,0:T(4,128)(2,1)} %refs_0_.1, bf16[4,8192]{1,0:T(4,128)(2,1)} %refs_1_.1, bf16[4,512]{1,0:T(4,128)(2,1)} %refs_2_.2, bf16[4,8192]{1,0:T(4,128)(2,1)} %refs_3_.1, f32[512,128]{1,0:T(8,128)} %refs_7_), custom_call_target="tpu_custom_call" | custom-call | flops 1000 | bytes 1000 | tf_op jit(solution)/shard_map/pallas_call | solution.py:160
  2.5 17.3 %all-to-all-start = ((bf16[64,17,4,128]{3,2,1,0:T(4,128)(2,1)}), bf16[64,17,4,128]{3,2,1,0:T(4,128)(2,1)S(1)}, u32[]{:S(2)}, u32[]{:S(2)}) async-start(bf16[64,17,4,128]{3,2,1,0:T(4,128)(2,1)} %shard_map.91), calls=%async_computation | async-start | bytes 2228224 | tf_op jit(solution)/shard_map/all_to_all | solution.py:21
  19.8 4.4 %collective-permute-start.1 = (f32[512,128]{1,0:T(8,128)S(1)}, f32[512,128]{1,0:T(8,128)S(1)}, u32[]{:S(2)}, u32[]{:S(2)}) collective-permute-start(f32[512,128]{1,0:T(8,128)S(1)} %copy-done), channel_id=1, source_target_pairs={{0,24},{8,0},{16,8},{24,16},{1,25},{9,1},{17,9},{25,17},{2,26},{10... | collective-permute-start | bytes 786440 | tf_op jit(solution)/shard_map/ppermute | solution.py:173
  24.2 2.5 %collective-permute-start.5 = (bf16[512,128]{1,0:T(8,128)(2,1)S(1)}, bf16[512,128]{1,0:T(8,128)(2,1)S(1)}, u32[]{:S(2)}, u32[]{:S(2)}) collective-permute-start(bf16[512,128]{1,0:T(8,128)(2,1)S(1)} %copy-done.4), channel_id=1, source_target_pairs={{0,24},{8,0},{16,8},{24,16},{1,25},{9,1},{17,9},{25,17},{2,26},{10... | collective-permute-start | bytes 393224 | tf_op jit(solution)/shard_map/ppermute | solution.py:173
  26.6 2.8 %collective-permute-start.3 = (bf16[512,128]{1,0:T(8,128)(2,1)S(1)}, bf16[512,128]{1,0:T(8,128)(2,1)S(1)}, u32[]{:S(2)}, u32[]{:S(2)}) collective-permute-start(bf16[512,128]{1,0:T(8,128)(2,1)S(1)} %copy-done.4), channel_id=1, source_target_pairs={{0,8},{8,16},{16,24},{24,0},{1,9},{9,17},{17,25},{25,1},{2,10},{10... | collective-permute-start | bytes 393224 | tf_op jit(solution)/shard_map/ppermute | solution.py:173
  29.5 1.9 %collective-permute-start = (f32[512,128]{1,0:T(8,128)S(1)}, f32[512,128]{1,0:T(8,128)S(1)}, u32[]{:S(2)}, u32[]{:S(2)}) collective-permute-start(f32[512,128]{1,0:T(8,128)S(1)} %copy-done), channel_id=1, source_target_pairs={{0,8},{8,16},{16,24},{24,0},{1,9},{9,17},{17,25},{25,1},{2,10},{10... | collective-permute-start | bytes 786440 | tf_op jit(solution)/shard_map/ppermute | solution.py:173
  31.4 0.4 reshape.450
  32.3 4.6 %collective-permute-start.2 = (f32[512,128]{1,0:T(8,128)S(1)}, f32[512,128]{1,0:T(8,128)S(1)}, u32[]{:S(2)}, u32[]{:S(2)}) collective-permute-start(f32[512,128]{1,0:T(8,128)S(1)} %collective-permute-done.1.refs_10_), channel_id=1, source_target_pairs={{0,24},{8,0},{16,8},{24,16},{1,25},{9,1},{17,9},{25,17},{2,26},{10... | collective-permute-start | bytes 786440 | tf_op jit(solution)/shard_map/ppermute | solution.py:173
  37.1 0.7 reshape.452.refs_6_
  37.7 1.9 %collective-permute-start.4 = (bf16[512,128]{1,0:T(8,128)(2,1)S(1)}, bf16[512,128]{1,0:T(8,128)(2,1)S(1)}, u32[]{:S(2)}, u32[]{:S(2)}) collective-permute-start(bf16[512,128]{1,0:T(8,128)(2,1)S(1)} %collective-permute-done.3.refs_4_), channel_id=1, source_target_pairs={{0,8},{8,16},{16,24},{24,0},{1,9},{9,17},{17,25},{25,1},{2,10},{10... | collective-permute-start | bytes 393224 | tf_op jit(solution)/shard_map/ppermute | solution.py:173
  39.7 0.6 fusion.refs_7_
  40.3 4.7 %collective-permute-done.4.refs_5_ = bf16[512,128]{1,0:T(8,128)(2,1)S(1)} collective-permute-done((bf16[512,128]{1,0:T(8,128)(2,1)S(1)}, bf16[512,128]{1,0:T(8,128)(2,1)S(1)}, u32[]{:S(2)}, u32[]{:S(2)}) %collective-permute-start.4) | collective-permute-done | bytes 131104 | tf_op jit(solution)/shard_map/ppermute | solution.py:173
  45.0 3.4 %all-to-all-done.refs_0_ = bf16[64,17,4,128]{3,2,1,0:T(4,128)(2,1)S(1)} async-done(((bf16[64,17,4,128]{3,2,1,0:T(4,128)(2,1)}), bf16[64,17,4,128]{3,2,1,0:T(4,128)(2,1)S(1)}, u32[]{:S(2)}, u32[]{:S(2)}) %all-to-all-start) | async-done | bytes 1114144 | tf_op jit(solution)/shard_map/all_to_all | solution.py:21
  48.4 0.9 shard_map.92
  49.3 3.7 %collective-permute-start.6 = (bf16[64,17,4,128]{3,2,1,0:T(4,128)(2,1)S(1)}, bf16[64,17,4,128]{3,2,1,0:T(4,128)(2,1)S(1)}, u32[]{:S(2)}, u32[]{:S(2)}) collective-permute-start(bf16[64,17,4,128]{3,2,1,0:T(4,128)(2,1)S(1)} %all-to-all-done.refs_0_), channel_id=1, source_target_pairs={{0,1},{1,0},{2,3},{3,2},{4,5},{5,4},{6,7},{7,6},{8,9},{9,8},{10,11... | collective-permute-start | bytes 3342344 | tf_op jit(solution)/shard_map/ppermute | solution.py:215
  53.0 4.4 %all-to-all-start.1 = ((bf16[8,264,128]{2,1,0:T(8,128)(2,1)}), bf16[8,264,128]{2,1,0:T(8,128)(2,1)S(1)}, u32[]{:S(2)}, u32[]{:S(2)}) async-start(bf16[8,264,128]{2,1,0:T(8,128)(2,1)} %shard_map.92), calls=%async_computation.1 | async-start | bytes 1081344 | tf_op jit(solution)/shard_map/all_to_all | solution.py:21
  58.4 2.4 %shard_map.93 = (bf16[512,512]{1,0:T(8,128)(2,1)S(1)}, bf16[512,512]{1,0:T(8,128)(2,1)S(1)}, bf16[512,512]{1,0:T(8,128)(2,1)S(1)}, f32[512,512]{1,0:T(8,128)S(1)}) custom-call(bf16[12,256,128]{2,1,0:T(8,128)(2,1)S(1)} %bitcast.11, bf16[8,256,128]{2,1,0:T(8,128)(2,1)S(1)} %bitcast.12, bf16[512,512]{1,0:T(8,128)(2,1)} %refs_5_.1, bf16[512,128]{1,0:T(8,128)(2,1)} %refs_3_.2, ...), custom_call_target="tpu_custom_call" | custom-call | flops 1000 | bytes 1000 | tf_op jit(solution)/shard_map/pallas_call | solution.py:160
  60.9 6.2 %all-to-all-done.1.refs_4_ = bf16[8,264,128]{2,1,0:T(8,128)(2,1)S(1)} async-done(((bf16[8,264,128]{2,1,0:T(8,128)(2,1)}), bf16[8,264,128]{2,1,0:T(8,128)(2,1)S(1)}, u32[]{:S(2)}, u32[]{:S(2)}) %all-to-all-start.1) | async-done | bytes 540704 | tf_op jit(solution)/shard_map/all_to_all | solution.py:21
  67.1 10.0 %shard_map.94 = f32[32,128]{1,0:T(8,128)S(1)} custom-call(bf16[512,512]{1,0:T(8,128)(2,1)S(1)} %get-tuple-element.38.refs_0_, bf16[512,512]{1,0:T(8,128)(2,1)S(1)} %get-tuple-element.39.refs_1_, bf16[512,512]{1,0:T(8,128)(2,1)S(1)} %get-tuple-element.40.refs_2_, f32[512,512]{1,0:T(8,128)S(1)} %get-tuple-element.41.refs_3_, ...), custom_call_target="tpu_custom_call" | custom-call | flops 1000 | bytes 1000 | tf_op jit(solution)/shard_map/pallas_call | solution.py:160
  77.1 16.5 %all_to_all.25 = f32[32,1,128]{2,1,0:T(1,128)S(1)} all-to-all(f32[32,1,128]{2,1,0:T(1,128)S(1)} %bitcast.13), channel_id=1, replica_groups=mesh['zh'=2,'y'=8,'x'=4,'zl'=4,'c'=2] {'y','x'}, dimensions={0} | all-to-all | bytes 32768 | tf_op jit(solution)/shard_map/all_to_all | solution.py:21
  93.7 0.6 broadcast_in_dim.2
  94.3 6.2 %all-to-all-start.3 = ((f32[16,1,128]{2,1,0:T(1,128)}), f32[16,1,128]{2,1,0:T(1,128)S(1)}, u32[]{:S(2)}, u32[]{:S(2)}) async-start(f32[16,1,128]{2,1,0:T(1,128)} %broadcast_in_dim.2), calls=%async_computation.3 | async-start | bytes 16384 | tf_op jit(solution)/shard_map/all_to_all | solution.py:21
  100.5 7.0 %all-to-all-done.3 = f32[16,1,128]{2,1,0:T(1,128)S(1)} async-done(((f32[16,1,128]{2,1,0:T(1,128)}), f32[16,1,128]{2,1,0:T(1,128)S(1)}, u32[]{:S(2)}, u32[]{:S(2)}) %all-to-all-start.3) | async-done | bytes 8224 | tf_op jit(solution)/shard_map/all_to_all | solution.py:21
  107.6 0.6 reshape.455
  (40 shorter events, 1.8 us)
Async XLA Ops:
  2.4 17.3 %copy-start = (f32[512,128]{1,0:T(8,128)S(1)}, f32[512,128]{1,0:T(8,128)}, u32[]{:S(2)}) copy-start(f32[512,128]{1,0:T(8,128)} %refs_7_) | copy-start | bytes 786436
  2.4 21.7 %copy-start.4 = (bf16[512,128]{1,0:T(8,128)(2,1)S(1)}, bf16[512,128]{1,0:T(8,128)(2,1)}, u32[]{:S(2)}) copy-start(bf16[512,128]{1,0:T(8,128)(2,1)} %refs_3_.2) | copy-start | bytes 393220
  2.4 29.0 %copy-start.8 = (s32[2048]{0:T(1024)S(1)}, s32[2048]{0:T(1024)}, u32[]{:S(2)}) copy-start(s32[2048]{0:T(1024)} %param.16) | copy-start | bytes 24580
  2.5 34.5 %copy-start.9 = (s32[256]{0:T(256)S(1)}, s32[256]{0:T(256)}, u32[]{:S(2)}) copy-start(s32[256]{0:T(256)} %param.17) | copy-start | bytes 3076
  2.5 45.9 %all-to-all-start = ((bf16[64,17,4,128]{3,2,1,0:T(4,128)(2,1)}), bf16[64,17,4,128]{3,2,1,0:T(4,128)(2,1)S(1)}, u32[]{:S(2)}, u32[]{:S(2)}) async-start(bf16[64,17,4,128]{3,2,1,0:T(4,128)(2,1)} %shard_map.91), calls=%async_computation | async-start | bytes 2228224 | tf_op jit(solution)/shard_map/all_to_all | solution.py:21
  19.8 12.5 %collective-permute-start.1 = (f32[512,128]{1,0:T(8,128)S(1)}, f32[512,128]{1,0:T(8,128)S(1)}, u32[]{:S(2)}, u32[]{:S(2)}) collective-permute-start(f32[512,128]{1,0:T(8,128)S(1)} %copy-done), channel_id=1, source_target_pairs={{0,24},{8,0},{16,8},{24,16},{1,25},{9,1},{17,9},{25,17},{2,26},{10... | collective-permute-start | bytes 786440 | tf_op jit(solution)/shard_map/ppermute | solution.py:173
  24.2 16.1 %collective-permute-start.5 = (bf16[512,128]{1,0:T(8,128)(2,1)S(1)}, bf16[512,128]{1,0:T(8,128)(2,1)S(1)}, u32[]{:S(2)}, u32[]{:S(2)}) collective-permute-start(bf16[512,128]{1,0:T(8,128)(2,1)S(1)} %copy-done.4), channel_id=1, source_target_pairs={{0,24},{8,0},{16,8},{24,16},{1,25},{9,1},{17,9},{25,17},{2,26},{10... | collective-permute-start | bytes 393224 | tf_op jit(solution)/shard_map/ppermute | solution.py:173
  26.6 11.1 %collective-permute-start.3 = (bf16[512,128]{1,0:T(8,128)(2,1)S(1)}, bf16[512,128]{1,0:T(8,128)(2,1)S(1)}, u32[]{:S(2)}, u32[]{:S(2)}) collective-permute-start(bf16[512,128]{1,0:T(8,128)(2,1)S(1)} %copy-done.4), channel_id=1, source_target_pairs={{0,8},{8,16},{16,24},{24,0},{1,9},{9,17},{17,25},{25,1},{2,10},{10... | collective-permute-start | bytes 393224 | tf_op jit(solution)/shard_map/ppermute | solution.py:173
  29.5 15.5 %collective-permute-start = (f32[512,128]{1,0:T(8,128)S(1)}, f32[512,128]{1,0:T(8,128)S(1)}, u32[]{:S(2)}, u32[]{:S(2)}) collective-permute-start(f32[512,128]{1,0:T(8,128)S(1)} %copy-done), channel_id=1, source_target_pairs={{0,8},{8,16},{16,24},{24,0},{1,9},{9,17},{17,25},{25,1},{2,10},{10... | collective-permute-start | bytes 786440 | tf_op jit(solution)/shard_map/ppermute | solution.py:173
  32.3 20.7 %copy-start.1 = (f32[512,128]{1,0:T(8,128)}, f32[512,128]{1,0:T(8,128)S(1)}, u32[]{:S(2)}) copy-start(f32[512,128]{1,0:T(8,128)S(1)} %collective-permute-done.1.refs_10_) | copy-start | bytes 786436
  32.3 12.6 %collective-permute-start.2 = (f32[512,128]{1,0:T(8,128)S(1)}, f32[512,128]{1,0:T(8,128)S(1)}, u32[]{:S(2)}, u32[]{:S(2)}) collective-permute-start(f32[512,128]{1,0:T(8,128)S(1)} %collective-permute-done.1.refs_10_), channel_id=1, source_target_pairs={{0,24},{8,0},{16,8},{24,16},{1,25},{9,1},{17,9},{25,17},{2,26},{10... | collective-permute-start | bytes 786440 | tf_op jit(solution)/shard_map/ppermute | solution.py:173
  37.7 10.6 %copy-start.6 = (bf16[512,128]{1,0:T(8,128)(2,1)}, bf16[512,128]{1,0:T(8,128)(2,1)S(1)}, u32[]{:S(2)}) copy-start(bf16[512,128]{1,0:T(8,128)(2,1)S(1)} %collective-permute-done.3.refs_4_) | copy-start | bytes 393220
  37.7 7.2 %collective-permute-start.4 = (bf16[512,128]{1,0:T(8,128)(2,1)S(1)}, bf16[512,128]{1,0:T(8,128)(2,1)S(1)}, u32[]{:S(2)}, u32[]{:S(2)}) collective-permute-start(bf16[512,128]{1,0:T(8,128)(2,1)S(1)} %collective-permute-done.3.refs_4_), channel_id=1, source_target_pairs={{0,8},{8,16},{16,24},{24,0},{1,9},{9,17},{17,25},{25,1},{2,10},{10... | collective-permute-start | bytes 393224 | tf_op jit(solution)/shard_map/ppermute | solution.py:173
  40.3 8.1 %copy-start.5 = (bf16[512,128]{1,0:T(8,128)(2,1)}, bf16[512,128]{1,0:T(8,128)(2,1)S(1)}, u32[]{:S(2)}) copy-start(bf16[512,128]{1,0:T(8,128)(2,1)S(1)} %collective-permute-done.5.refs_6_) | copy-start | bytes 393220
  44.9 3.4 %copy-start.7 = (bf16[512,128]{1,0:T(8,128)(2,1)}, bf16[512,128]{1,0:T(8,128)(2,1)S(1)}, u32[]{:S(2)}) copy-start(bf16[512,128]{1,0:T(8,128)(2,1)S(1)} %collective-permute-done.4.refs_5_) | copy-start | bytes 393220
  45.0 8.0 %copy-start.2 = (f32[512,128]{1,0:T(8,128)}, f32[512,128]{1,0:T(8,128)S(1)}, u32[]{:S(2)}) copy-start(f32[512,128]{1,0:T(8,128)S(1)} %collective-permute-done.refs_8_) | copy-start | bytes 786436
  45.0 8.0 %copy-start.3 = (f32[512,128]{1,0:T(8,128)}, f32[512,128]{1,0:T(8,128)S(1)}, u32[]{:S(2)}) copy-start(f32[512,128]{1,0:T(8,128)S(1)} %collective-permute-done.2.refs_9_) | copy-start | bytes 786436
  49.3 8.7 %collective-permute-start.6 = (bf16[64,17,4,128]{3,2,1,0:T(4,128)(2,1)S(1)}, bf16[64,17,4,128]{3,2,1,0:T(4,128)(2,1)S(1)}, u32[]{:S(2)}, u32[]{:S(2)}) collective-permute-start(bf16[64,17,4,128]{3,2,1,0:T(4,128)(2,1)S(1)} %all-to-all-done.refs_0_), channel_id=1, source_target_pairs={{0,1},{1,0},{2,3},{3,2},{4,5},{5,4},{6,7},{7,6},{8,9},{9,8},{10,11... | collective-permute-start | bytes 3342344 | tf_op jit(solution)/shard_map/ppermute | solution.py:215
  53.0 14.1 %all-to-all-start.1 = ((bf16[8,264,128]{2,1,0:T(8,128)(2,1)}), bf16[8,264,128]{2,1,0:T(8,128)(2,1)S(1)}, u32[]{:S(2)}, u32[]{:S(2)}) async-start(bf16[8,264,128]{2,1,0:T(8,128)(2,1)} %shard_map.92), calls=%async_computation.1 | async-start | bytes 1081344 | tf_op jit(solution)/shard_map/all_to_all | solution.py:21
  94.3 13.3 %all-to-all-start.3 = ((f32[16,1,128]{2,1,0:T(1,128)}), f32[16,1,128]{2,1,0:T(1,128)S(1)}, u32[]{:S(2)}, u32[]{:S(2)}) async-start(f32[16,1,128]{2,1,0:T(1,128)} %broadcast_in_dim.2), calls=%async_computation.3 | async-start | bytes 16384 | tf_op jit(solution)/shard_map/all_to_all | solution.py:21

commit v5 on v4

--- a/solution.py
+++ b/solution.py
@@ -37,8 +37,8 @@
     for z in range(4):
         own = act[:, pl.ds(pl.multiple_of(z * 1024 + c * 512, 128), 512)]
         away = act[:, pl.ds(pl.multiple_of(z * 1024 + 512 - c * 512, 128), 512)]
-        for m in range(16):
-            to = m * 4 + z
+        for k in range(16):
+            to, m = k * 4 + z, k % 2 * 8 + k // 2
             for t in range(4):
                 part = slice(t * 128, t * 128 + 128)
                 cols = slice(m * 512 + t * 128, m * 512 + t * 128 + 128)
@@ -60,10 +60,10 @@
         source = zl + jnp.where(c == core, 0, 1 - 2 * (zl % 2))
         for t in range(4):
             for s in range(16):
-                out[core, t * 64 + s * 4 : t * 64 + s * 4 + 4, :] = got[s * 4 + source, 12 + t]
-        out[core, 256:264, :] = sums
+                out[4 * core, t * 64 + s * 4 : t * 64 + s * 4 + 4, :] = got[s * 4 + source, 12 + t]
+        out[4 * core, 256:264, :] = sums
         for x in range(1, 4):
-            out[2 * x + core] = out[core]
+            out[4 * core + x] = out[4 * core]
 
 
 def rotated(rows, by):
@@ -84,15 +84,18 @@
     for step, part in enumerate((basis0, basis1, basis2, basis3)):
         columns[:, pl.ds(ring_slot(x, step), 128)] = part[...]
     for step, part in enumerate((eigen0, eigen1, eigen2, eigen3)):
-        eigen[:, pl.ds(ring_slot(x, step), 128)] = part[...]
+        eigen[pl.ds(ring_slot(x, step), 128), :] = part[...].T
 
     def tiles(ref, first):
         return jnp.concatenate([ref[first + t] for t in range(4)], axis=1)
 
-    acts[0:256, :] = rotated(tiles(own, 0), act_basis[...]).astype(BF)
-    acts[256:512, :] = rotated(tiles(other, 0), act_basis[...]).astype(BF)
-    grads[0:256, :] = rotated(tiles(own, 8), columns[...]).astype(BF)
-    grads[256:512, :] = rotated(tiles(other, 4), columns[...]).astype(BF)
+    def turned(rows, by):
+        return rotated(rows, by).T.astype(BF)
+
+    acts[:, 0:256] = turned(tiles(own, 0), act_basis[...])
+    acts[:, 256:512] = turned(tiles(other, 0), act_basis[...])
+    grads[:, 0:256] = turned(tiles(own, 8), columns[...])
+    grads[:, 256:512] = turned(tiles(other, 4), columns[...])
 
 
 def score_kernel(
@@ -109,27 +112,33 @@
 
     def query_rows(core):
         rows = [
-            jnp.concatenate([queries[2 * p + core, t * 64 : t * 64 + 64, :] for t in range(4)], axis=1)
+            jnp.concatenate([queries[4 * core + p, t * 64 : t * 64 + 64, :] for t in range(4)], axis=1)
             for p in range(4)
         ]
         return jnp.concatenate(rows, axis=0)
 
     for copy in copies:
         copy.wait()
-    query_turned = rotated(query_rows(c), act_basis[...]).T.astype(BF)
-    query_cols = rotated(query_rows(1 - c), columns[...]).astype(BF)
-    lane = lax.broadcasted_iota(jnp.int32, (512, QUERIES), 1)
-    scores = jnp.zeros((512, QUERIES), F32)
+    query_act = rotated(query_rows(c), act_basis[...]).astype(BF)
+    query_turned = rotated(query_rows(1 - c), columns[...]).T.astype(BF)
+    row = lax.broadcasted_iota(jnp.int32, (QUERIES, 512), 0)
+    scores = jnp.zeros((QUERIES, 512), F32)
     for q in range(QUERIES):
         chosen = (query_ids[...] == q).astype(F32).astype(BF)
-        gram = rotated(query_turned * chosen, query_cols)
+        gram = rotated(query_turned * chosen, query_act)
         precond = (gram * scale[...]).astype(BF)
-        mixed = rotated(acts[...], precond)
-        score = jnp.sum(mixed * grads[...], axis=1, keepdims=True)
-        scores = jnp.where(lane == q, score, scores)
+        mixed = rotated(precond, acts[...])
+        score = jnp.sum(mixed * grads[...], axis=0, keepdims=True)
+        scores = jnp.where(row == q, score, scores)
     row = lax.broadcasted_iota(jnp.int32, (EXAMPLES, 512), 0)
     chosen = (ids[...] == row).astype(F32)
-    sums = jnp.dot(chosen, scores, precision=lax.Precision.HIGHEST, preferred_element_type=F32)
+    sums = lax.dot_general(
+        chosen,
+        scores,
+        (((1,), (1,)), ((), ())),
+        precision=lax.Precision.HIGHEST,
+        preferred_element_type=F32,
+    )
     sums = [sums[part * 32 : part * 32 + 32, :] for part in range(4)]
     out[...] = jnp.concatenate(sums + [jnp.zeros((32, 64), F32)], axis=1)
 
@@ -199,19 +208,20 @@
     message, eigenvalues, grad_basis = lax.optimization_barrier((message, eigenvalues, grad_basis))
     eigens = ring_parts(eigenvalues, 3)
     bases = ring_parts(grad_basis, 1)
-    got = swap_all(message, ("zh", "y", "zl"))
-
-    ids = lax.dynamic_index_in_dim(example_ids.reshape(16, 4, 4, 2, 4), x, 1, keepdims=False)
-    ids_own = lax.dynamic_index_in_dim(ids, c, 2, keepdims=False).reshape(1, 256)
-    ids_other = lax.dynamic_index_in_dim(ids, 1 - c, 2, keepdims=False).reshape(1, 256)
+    got = swap_all(message, ("y", "zh", "zl"))
+
+    ids = lax.dynamic_index_in_dim(example_ids.reshape(2, 8, 4, 4, 2, 4), x, 2, keepdims=False)
+    ids = jnp.transpose(ids, (1, 0, 2, 3, 4))
+    ids_own = lax.dynamic_index_in_dim(ids, c, 3, keepdims=False).reshape(1, 256)
+    ids_other = lax.dynamic_index_in_dim(ids, 1 - c, 3, keepdims=False).reshape(1, 256)
     ids = jnp.concatenate([ids_own, ids_other], axis=1)
     ids = ids // 64 * 64 + ids % 2 * 32 + ids % 64 // 2
-    query_order = jnp.transpose(query_ids.reshape(16, 4, 4), (1, 0, 2)).reshape(1, 256)
+    query_order = jnp.transpose(query_ids.reshape(2, 8, 4, 4), (2, 1, 0, 3)).reshape(1, 256)
     got, eigens, bases, ids, query_order = lax.optimization_barrier((got, eigens, bases, ids, query_order))
 
     (queries,) = local_call(relay_kernel, 6, [((8, 264, 128), BF)], (got,), ())
     queries, got = lax.optimization_barrier((queries, got))
-    queries = swap_all(queries, ("x", "c"))
+    queries = swap_all(queries, ("c", "x"))
     other = lax.ppermute(got, "c", [(0, 1), (1, 0)])
     own = jnp.transpose(got[:, 0:12], (1, 0, 2, 3)).reshape(12, 256, 128)
     other = jnp.transpose(other[:, 4:12], (1, 0, 2, 3)).reshape(8, 256, 128)

time: 109 us -> 108 us (level)
  starting transfers between devices: 49.7 us -> 53.1 us
  blocking collectives: 16.5 us -> 14.1 us
  waiting for transfers between devices: 21.3 us -> 20.1 us
    all_to_all x1, blocking collectives: 16.5 us -> 14.1 us  [swap_all(): return lax.all_to_all(block, axes, split_axis=0, concat_axis=0, tiled=True)]
    ppermute x1, starting transfers between devices: 3.66 us -> 5.79 us  [shards(): other = lax.ppermute(got, 'c', [(0, 1), (1, 0)])]
    all_to_all x3, starting transfers between devices: 27.9 us -> 29.3 us  [swap_all(): return lax.all_to_all(block, axes, split_axis=0, concat_axis=0, tiled=True)]
    all_to_all x3, waiting for transfers between devices: 16.6 us -> 15.5 us  [swap_all(): return lax.all_to_all(block, axes, split_axis=0, concat_axis=0, tiled=True)]
where the time goes in v5:
time: 108 us
  starting transfers between devices  53.1 us (49%)
  waiting for transfers between devices  20.1 us (19%)
  Pallas kernels  14.8 us (14%)
  blocking collectives  14.1 us (13%)
  local copies, waits for them, and re-layouts  4.41 us (4%)
    all_to_all x3, starting transfers between devices, swap_all(): return lax.all_to_all(block, axes, split_axis=0, concat_axis=0, tiled=True)  29.3 us
    ppermute x6, starting transfers between devices, moved(): return lax.ppermute(part, 'x', [(p, (p + step) % 4) for p in range(4)])  18.1 us
    all_to_all x3, waiting for transfers between devices, swap_all(): return lax.all_to_all(block, axes, split_axis=0, concat_axis=0, tiled=True)  15.5 us
    pallas_call x4, Pallas kernels, local_call(): pl.pallas_call(body, out_shape=[jax.ShapeDtypeStruct(shape, dtype) for sh...  14.8 us
    all_to_all x1, blocking collectives, swap_all(): return lax.all_to_all(block, axes, split_axis=0, concat_axis=0, tiled=True)  14.1 us
    ppermute x1, starting transfers between devices, shards(): other = lax.ppermute(got, 'c', [(0, 1), (1, 0)])  5.79 us
    ppermute x6, waiting for transfers between devices, moved(): return lax.ppermute(part, 'x', [(p, (p + step) % 4) for p in range(4)])  4.68 us
  transfers between devices with their start and end apart: 10, of which 4 were waited for; matrix products, arithmetic and copies ran while one was open for 3% of the time, Pallas kernels for 2%

profile of v5, /device:TPU:1, one launch (start us, length us, event | category | flops | bytes accessed | tf_op | source)
XLA Modules:
  0.0 107.6 jit_solution(8673975124656675183)
XLA Ops:
  0.0 2.4 %shard_map.91 = bf16[64,17,4,128]{3,2,1,0:T(4,128)(2,1)} custom-call(bf16[4,4096]{1,0:T(4,128)(2,1)} %refs_0_.1, bf16[4,8192]{1,0:T(4,128)(2,1)} %refs_1_.1, bf16[4,512]{1,0:T(4,128)(2,1)} %refs_2_.2, bf16[4,8192]{1,0:T(4,128)(2,1)} %refs_3_.1, f32[512,128]{1,0:T(8,128)} %refs_7_), custom_call_target="tpu_custom_call" | custom-call | flops 1000 | bytes 1000 | tf_op jit(solution)/shard_map/pallas_call | solution.py:169
  2.5 17.3 %all-to-all-start = ((bf16[64,17,4,128]{3,2,1,0:T(4,128)(2,1)}), bf16[64,17,4,128]{3,2,1,0:T(4,128)(2,1)S(1)}, u32[]{:S(2)}, u32[]{:S(2)}) async-start(bf16[64,17,4,128]{3,2,1,0:T(4,128)(2,1)} %shard_map.91), calls=%async_computation | async-start | bytes 2228224 | tf_op jit(solution)/shard_map/all_to_all | solution.py:21
  19.8 4.4 %collective-permute-start.1 = (f32[512,128]{1,0:T(8,128)S(1)}, f32[512,128]{1,0:T(8,128)S(1)}, u32[]{:S(2)}, u32[]{:S(2)}) collective-permute-start(f32[512,128]{1,0:T(8,128)S(1)} %copy-done), channel_id=1, source_target_pairs={{0,24},{8,0},{16,8},{24,16},{1,25},{9,1},{17,9},{25,17},{2,26},{10... | collective-permute-start | bytes 786440 | tf_op jit(solution)/shard_map/ppermute | solution.py:182
  24.2 2.5 %collective-permute-start.5 = (bf16[512,128]{1,0:T(8,128)(2,1)S(1)}, bf16[512,128]{1,0:T(8,128)(2,1)S(1)}, u32[]{:S(2)}, u32[]{:S(2)}) collective-permute-start(bf16[512,128]{1,0:T(8,128)(2,1)S(1)} %copy-done.4), channel_id=1, source_target_pairs={{0,24},{8,0},{16,8},{24,16},{1,25},{9,1},{17,9},{25,17},{2,26},{10... | collective-permute-start | bytes 393224 | tf_op jit(solution)/shard_map/ppermute | solution.py:182
  26.6 2.8 %collective-permute-start.3 = (bf16[512,128]{1,0:T(8,128)(2,1)S(1)}, bf16[512,128]{1,0:T(8,128)(2,1)S(1)}, u32[]{:S(2)}, u32[]{:S(2)}) collective-permute-start(bf16[512,128]{1,0:T(8,128)(2,1)S(1)} %copy-done.4), channel_id=1, source_target_pairs={{0,8},{8,16},{16,24},{24,0},{1,9},{9,17},{17,25},{25,1},{2,10},{10... | collective-permute-start | bytes 393224 | tf_op jit(solution)/shard_map/ppermute | solution.py:182
  29.5 1.9 %collective-permute-start = (f32[512,128]{1,0:T(8,128)S(1)}, f32[512,128]{1,0:T(8,128)S(1)}, u32[]{:S(2)}, u32[]{:S(2)}) collective-permute-start(f32[512,128]{1,0:T(8,128)S(1)} %copy-done), channel_id=1, source_target_pairs={{0,8},{8,16},{16,24},{24,0},{1,9},{9,17},{17,25},{25,1},{2,10},{10... | collective-permute-start | bytes 786440 | tf_op jit(solution)/shard_map/ppermute | solution.py:182
  31.4 0.4 reshape.452
  32.7 4.6 %collective-permute-start.2 = (f32[512,128]{1,0:T(8,128)S(1)}, f32[512,128]{1,0:T(8,128)S(1)}, u32[]{:S(2)}, u32[]{:S(2)}) collective-permute-start(f32[512,128]{1,0:T(8,128)S(1)} %collective-permute-done.1.refs_10_), channel_id=1, source_target_pairs={{0,24},{8,0},{16,8},{24,16},{1,25},{9,1},{17,9},{25,17},{2,26},{10... | collective-permute-start | bytes 786440 | tf_op jit(solution)/shard_map/ppermute | solution.py:182
  37.5 0.7 reshape.456.refs_6_
  38.2 1.9 %collective-permute-start.4 = (bf16[512,128]{1,0:T(8,128)(2,1)S(1)}, bf16[512,128]{1,0:T(8,128)(2,1)S(1)}, u32[]{:S(2)}, u32[]{:S(2)}) collective-permute-start(bf16[512,128]{1,0:T(8,128)(2,1)S(1)} %collective-permute-done.3.refs_4_), channel_id=1, source_target_pairs={{0,8},{8,16},{16,24},{24,0},{1,9},{9,17},{17,25},{25,1},{2,10},{10... | collective-permute-start | bytes 393224 | tf_op jit(solution)/shard_map/ppermute | solution.py:182
  40.1 0.6 fusion.refs_7_
  40.7 4.7 %collective-permute-done.4.refs_5_ = bf16[512,128]{1,0:T(8,128)(2,1)S(1)} collective-permute-done((bf16[512,128]{1,0:T(8,128)(2,1)S(1)}, bf16[512,128]{1,0:T(8,128)(2,1)S(1)}, u32[]{:S(2)}, u32[]{:S(2)}) %collective-permute-start.4) | collective-permute-done | bytes 131104 | tf_op jit(solution)/shard_map/ppermute | solution.py:182
  45.4 2.4 %all-to-all-done.refs_0_ = bf16[64,17,4,128]{3,2,1,0:T(4,128)(2,1)S(1)} async-done(((bf16[64,17,4,128]{3,2,1,0:T(4,128)(2,1)}), bf16[64,17,4,128]{3,2,1,0:T(4,128)(2,1)S(1)}, u32[]{:S(2)}, u32[]{:S(2)}) %all-to-all-start) | async-done | bytes 1114144 | tf_op jit(solution)/shard_map/all_to_all | solution.py:21
  47.8 0.9 shard_map.92
  48.7 5.8 %collective-permute-start.6 = (bf16[64,17,4,128]{3,2,1,0:T(4,128)(2,1)S(1)}, bf16[64,17,4,128]{3,2,1,0:T(4,128)(2,1)S(1)}, u32[]{:S(2)}, u32[]{:S(2)}) collective-permute-start(bf16[64,17,4,128]{3,2,1,0:T(4,128)(2,1)S(1)} %all-to-all-done.refs_0_), channel_id=1, source_target_pairs={{0,1},{1,0},{2,3},{3,2},{4,5},{5,4},{6,7},{7,6},{8,9},{9,8},{10,11... | collective-permute-start | bytes 3342344 | tf_op jit(solution)/shard_map/ppermute | solution.py:225
  54.6 4.4 %all-to-all-start.1 = ((bf16[8,264,128]{2,1,0:T(8,128)(2,1)}), bf16[8,264,128]{2,1,0:T(8,128)(2,1)S(1)}, u32[]{:S(2)}, u32[]{:S(2)}) async-start(bf16[8,264,128]{2,1,0:T(8,128)(2,1)} %shard_map.92), calls=%async_computation.1 | async-start | bytes 1081344 | tf_op jit(solution)/shard_map/all_to_all | solution.py:21
  60.0 2.5 %shard_map.93 = (bf16[512,512]{1,0:T(8,128)(2,1)S(1)}, bf16[512,512]{1,0:T(8,128)(2,1)S(1)}, bf16[512,512]{1,0:T(8,128)(2,1)S(1)}, f32[512,512]{1,0:T(8,128)S(1)}) custom-call(bf16[12,256,128]{2,1,0:T(8,128)(2,1)S(1)} %bitcast.21, bf16[8,256,128]{2,1,0:T(8,128)(2,1)S(1)} %bitcast.22, bf16[512,512]{1,0:T(8,128)(2,1)} %refs_5_.1, bf16[512,128]{1,0:T(8,128)(2,1)} %refs_3_.2, ...), custom_call_target="tpu_custom_call" | custom-call | flops 1000 | bytes 1000 | tf_op jit(solution)/shard_map/pallas_call | solution.py:169
  62.5 6.0 %all-to-all-done.1.refs_4_ = bf16[8,264,128]{2,1,0:T(8,128)(2,1)S(1)} async-done(((bf16[8,264,128]{2,1,0:T(8,128)(2,1)}), bf16[8,264,128]{2,1,0:T(8,128)(2,1)S(1)}, u32[]{:S(2)}, u32[]{:S(2)}) %all-to-all-start.1) | async-done | bytes 540704 | tf_op jit(solution)/shard_map/all_to_all | solution.py:21
  68.6 9.0 %shard_map.94 = f32[32,128]{1,0:T(8,128)S(1)} custom-call(bf16[512,512]{1,0:T(8,128)(2,1)S(1)} %get-tuple-element.38.refs_0_, bf16[512,512]{1,0:T(8,128)(2,1)S(1)} %get-tuple-element.39.refs_1_, bf16[512,512]{1,0:T(8,128)(2,1)S(1)} %get-tuple-element.40.refs_2_, f32[512,512]{1,0:T(8,128)S(1)} %get-tuple-element.41.refs_3_, ...), custom_call_target="tpu_custom_call" | custom-call | flops 1000 | bytes 1000 | tf_op jit(solution)/shard_map/pallas_call | solution.py:169
  77.5 14.1 %all_to_all.25 = f32[32,1,128]{2,1,0:T(1,128)S(1)} all-to-all(f32[32,1,128]{2,1,0:T(1,128)S(1)} %bitcast.23), channel_id=1, replica_groups=mesh['zh'=2,'y'=8,'x'=4,'zl'=4,'c'=2] {'y','x'}, dimensions={0} | all-to-all | bytes 32768 | tf_op jit(solution)/shard_map/all_to_all | solution.py:21
  91.6 0.6 broadcast_in_dim.2
  92.2 7.6 %all-to-all-start.3 = ((f32[16,1,128]{2,1,0:T(1,128)}), f32[16,1,128]{2,1,0:T(1,128)S(1)}, u32[]{:S(2)}, u32[]{:S(2)}) async-start(f32[16,1,128]{2,1,0:T(1,128)} %broadcast_in_dim.2), calls=%async_computation.3 | async-start | bytes 16384 | tf_op jit(solution)/shard_map/all_to_all | solution.py:21
  99.8 7.0 %all-to-all-done.3 = f32[16,1,128]{2,1,0:T(1,128)S(1)} async-done(((f32[16,1,128]{2,1,0:T(1,128)}), f32[16,1,128]{2,1,0:T(1,128)S(1)}, u32[]{:S(2)}, u32[]{:S(2)}) %all-to-all-start.3) | async-done | bytes 8224 | tf_op jit(solution)/shard_map/all_to_all | solution.py:21
  106.9 0.6 reshape.459
  (44 shorter events, 2.2 us)
Async XLA Ops:
  2.4 17.3 %copy-start = (f32[512,128]{1,0:T(8,128)S(1)}, f32[512,128]{1,0:T(8,128)}, u32[]{:S(2)}) copy-start(f32[512,128]{1,0:T(8,128)} %refs_7_) | copy-start | bytes 786436
  2.4 21.7 %copy-start.4 = (bf16[512,128]{1,0:T(8,128)(2,1)S(1)}, bf16[512,128]{1,0:T(8,128)(2,1)}, u32[]{:S(2)}) copy-start(bf16[512,128]{1,0:T(8,128)(2,1)} %refs_3_.2) | copy-start | bytes 393220
  2.5 29.0 %copy-start.8 = (s32[2048]{0:T(1024)S(1)}, s32[2048]{0:T(1024)}, u32[]{:S(2)}) copy-start(s32[2048]{0:T(1024)} %param.16) | copy-start | bytes 24580
  2.5 34.9 %copy-start.9 = (s32[256]{0:T(256)S(1)}, s32[256]{0:T(256)}, u32[]{:S(2)}) copy-start(s32[256]{0:T(256)} %param.17) | copy-start | bytes 3076
  2.5 45.3 %all-to-all-start = ((bf16[64,17,4,128]{3,2,1,0:T(4,128)(2,1)}), bf16[64,17,4,128]{3,2,1,0:T(4,128)(2,1)S(1)}, u32[]{:S(2)}, u32[]{:S(2)}) async-start(bf16[64,17,4,128]{3,2,1,0:T(4,128)(2,1)} %shard_map.91), calls=%async_computation | async-start | bytes 2228224 | tf_op jit(solution)/shard_map/all_to_all | solution.py:21
  19.8 12.9 %collective-permute-start.1 = (f32[512,128]{1,0:T(8,128)S(1)}, f32[512,128]{1,0:T(8,128)S(1)}, u32[]{:S(2)}, u32[]{:S(2)}) collective-permute-start(f32[512,128]{1,0:T(8,128)S(1)} %copy-done), channel_id=1, source_target_pairs={{0,24},{8,0},{16,8},{24,16},{1,25},{9,1},{17,9},{25,17},{2,26},{10... | collective-permute-start | bytes 786440 | tf_op jit(solution)/shard_map/ppermute | solution.py:182
  24.2 16.5 %collective-permute-start.5 = (bf16[512,128]{1,0:T(8,128)(2,1)S(1)}, bf16[512,128]{1,0:T(8,128)(2,1)S(1)}, u32[]{:S(2)}, u32[]{:S(2)}) collective-permute-start(bf16[512,128]{1,0:T(8,128)(2,1)S(1)} %copy-done.4), channel_id=1, source_target_pairs={{0,24},{8,0},{16,8},{24,16},{1,25},{9,1},{17,9},{25,17},{2,26},{10... | collective-permute-start | bytes 393224 | tf_op jit(solution)/shard_map/ppermute | solution.py:182
  26.6 11.5 %collective-permute-start.3 = (bf16[512,128]{1,0:T(8,128)(2,1)S(1)}, bf16[512,128]{1,0:T(8,128)(2,1)S(1)}, u32[]{:S(2)}, u32[]{:S(2)}) collective-permute-start(bf16[512,128]{1,0:T(8,128)(2,1)S(1)} %copy-done.4), channel_id=1, source_target_pairs={{0,8},{8,16},{16,24},{24,0},{1,9},{9,17},{17,25},{25,1},{2,10},{10... | collective-permute-start | bytes 393224 | tf_op jit(solution)/shard_map/ppermute | solution.py:182
  29.5 15.9 %collective-permute-start = (f32[512,128]{1,0:T(8,128)S(1)}, f32[512,128]{1,0:T(8,128)S(1)}, u32[]{:S(2)}, u32[]{:S(2)}) collective-permute-start(f32[512,128]{1,0:T(8,128)S(1)} %copy-done), channel_id=1, source_target_pairs={{0,8},{8,16},{16,24},{24,0},{1,9},{9,17},{17,25},{25,1},{2,10},{10... | collective-permute-start | bytes 786440 | tf_op jit(solution)/shard_map/ppermute | solution.py:182
  32.7 21.8 %copy-start.1 = (f32[512,128]{1,0:T(8,128)}, f32[512,128]{1,0:T(8,128)S(1)}, u32[]{:S(2)}) copy-start(f32[512,128]{1,0:T(8,128)S(1)} %collective-permute-done.1.refs_10_) | copy-start | bytes 786436
  32.7 12.7 %collective-permute-start.2 = (f32[512,128]{1,0:T(8,128)S(1)}, f32[512,128]{1,0:T(8,128)S(1)}, u32[]{:S(2)}, u32[]{:S(2)}) collective-permute-start(f32[512,128]{1,0:T(8,128)S(1)} %collective-permute-done.1.refs_10_), channel_id=1, source_target_pairs={{0,24},{8,0},{16,8},{24,16},{1,25},{9,1},{17,9},{25,17},{2,26},{10... | collective-permute-start | bytes 786440 | tf_op jit(solution)/shard_map/ppermute | solution.py:182
  38.2 9.6 %copy-start.6 = (bf16[512,128]{1,0:T(8,128)(2,1)}, bf16[512,128]{1,0:T(8,128)(2,1)S(1)}, u32[]{:S(2)}) copy-start(bf16[512,128]{1,0:T(8,128)(2,1)S(1)} %collective-permute-done.3.refs_4_) | copy-start | bytes 393220
  38.2 7.2 %collective-permute-start.4 = (bf16[512,128]{1,0:T(8,128)(2,1)S(1)}, bf16[512,128]{1,0:T(8,128)(2,1)S(1)}, u32[]{:S(2)}, u32[]{:S(2)}) collective-permute-start(bf16[512,128]{1,0:T(8,128)(2,1)S(1)} %collective-permute-done.3.refs_4_), channel_id=1, source_target_pairs={{0,8},{8,16},{16,24},{24,0},{1,9},{9,17},{17,25},{25,1},{2,10},{10... | collective-permute-start | bytes 393224 | tf_op jit(solution)/shard_map/ppermute | solution.py:182
  40.7 7.1 %copy-start.5 = (bf16[512,128]{1,0:T(8,128)(2,1)}, bf16[512,128]{1,0:T(8,128)(2,1)S(1)}, u32[]{:S(2)}) copy-start(bf16[512,128]{1,0:T(8,128)(2,1)S(1)} %collective-permute-done.5.refs_6_) | copy-start | bytes 393220
  45.4 2.4 %copy-start.7 = (bf16[512,128]{1,0:T(8,128)(2,1)}, bf16[512,128]{1,0:T(8,128)(2,1)S(1)}, u32[]{:S(2)}) copy-start(bf16[512,128]{1,0:T(8,128)(2,1)S(1)} %collective-permute-done.4.refs_5_) | copy-start | bytes 393220
  45.4 9.2 %copy-start.2 = (f32[512,128]{1,0:T(8,128)}, f32[512,128]{1,0:T(8,128)S(1)}, u32[]{:S(2)}) copy-start(f32[512,128]{1,0:T(8,128)S(1)} %collective-permute-done.refs_8_) | copy-start | bytes 786436
  45.4 9.2 %copy-start.3 = (f32[512,128]{1,0:T(8,128)}, f32[512,128]{1,0:T(8,128)S(1)}, u32[]{:S(2)}) copy-start(f32[512,128]{1,0:T(8,128)S(1)} %collective-permute-done.2.refs_9_) | copy-start | bytes 786436
  48.7 10.9 %collective-permute-start.6 = (bf16[64,17,4,128]{3,2,1,0:T(4,128)(2,1)S(1)}, bf16[64,17,4,128]{3,2,1,0:T(4,128)(2,1)S(1)}, u32[]{:S(2)}, u32[]{:S(2)}) collective-permute-start(bf16[64,17,4,128]{3,2,1,0:T(4,128)(2,1)S(1)} %all-to-all-done.refs_0_), channel_id=1, source_target_pairs={{0,1},{1,0},{2,3},{3,2},{4,5},{5,4},{6,7},{7,6},{8,9},{9,8},{10,11... | collective-permute-start | bytes 3342344 | tf_op jit(solution)/shard_map/ppermute | solution.py:225
  54.6 14.0 %all-to-all-start.1 = ((bf16[8,264,128]{2,1,0:T(8,128)(2,1)}), bf16[8,264,128]{2,1,0:T(8,128)(2,1)S(1)}, u32[]{:S(2)}, u32[]{:S(2)}) async-start(bf16[8,264,128]{2,1,0:T(8,128)(2,1)} %shard_map.92), calls=%async_computation.1 | async-start | bytes 1081344 | tf_op jit(solution)/shard_map/all_to_all | solution.py:21
  92.2 14.6 %all-to-all-start.3 = ((f32[16,1,128]{2,1,0:T(1,128)}), f32[16,1,128]{2,1,0:T(1,128)S(1)}, u32[]{:S(2)}, u32[]{:S(2)}) async-start(f32[16,1,128]{2,1,0:T(1,128)} %broadcast_in_dim.2), calls=%async_computation.3 | async-start | bytes 16384 | tf_op jit(solution)/shard_map/all_to_all | solution.py:21

commit v6 on v5

--- a/solution.py
+++ b/solution.py
@@ -139,8 +139,7 @@
         precision=lax.Precision.HIGHEST,
         preferred_element_type=F32,
     )
-    sums = [sums[part * 32 : part * 32 + 32, :] for part in range(4)]
-    out[...] = jnp.concatenate(sums + [jnp.zeros((32, 64), F32)], axis=1)
+    out[...] = jnp.concatenate([sums[part * 8 : part * 8 + 8, :] for part in range(16)], axis=1)
 
 
 def local_call(kernel, mib, outs, near, far, scratch=()):
@@ -215,7 +214,7 @@
     ids_own = lax.dynamic_index_in_dim(ids, c, 3, keepdims=False).reshape(1, 256)
     ids_other = lax.dynamic_index_in_dim(ids, 1 - c, 3, keepdims=False).reshape(1, 256)
     ids = jnp.concatenate([ids_own, ids_other], axis=1)
-    ids = ids // 64 * 64 + ids % 2 * 32 + ids % 64 // 2
+    ids = ids // 64 * 64 + ids % 8 * 8 + ids % 64 // 8
     query_order = jnp.transpose(query_ids.reshape(2, 8, 4, 4), (2, 1, 0, 3)).reshape(1, 256)
     got, eigens, bases, ids, query_order = lax.optimization_barrier((got, eigens, bases, ids, query_order))
 
@@ -235,14 +234,16 @@
     (partial_scores,) = local_call(
         score_kernel,
         20,
-        [((32, 128), F32)],
+        [((8, 256), F32)],
         (*held, queries),
         (act_basis, query_order, ids),
         (pltpu.VMEM((512, 512), F32), pltpu.VMEM((512, 512), F32)),
     )
-    sums = jnp.sum(swap_all(partial_scores, ("y", "x")), axis=0, keepdims=True)
-    sums = jnp.sum(swap_all(jnp.broadcast_to(sums, (16, 128)), ("zh", "zl", "c")), axis=0)
-    return lax.dynamic_slice_in_dim(sums, lax.axis_index("zh") * 32, 32, 0).reshape(2, 16)
+    partial_scores = jnp.concatenate([partial_scores, partial_scores], axis=0)
+    sums = jnp.sum(swap_all(partial_scores, ("c", "y")), axis=0, keepdims=True)
+    sums = jnp.sum(swap_all(jnp.broadcast_to(sums, (32, 256)), ("zh", "zl", "x")), axis=0)
+    place = lax.axis_index("zh") * 128 + x * 32
+    return lax.dynamic_slice_in_dim(sums, place, 32, 0).reshape(2, 16)
 
 
 def solution(mesh):

time: 108 us -> 107 us (level)
  blocking collectives: 14.1 us -> 12 us
  waiting for transfers between devices: 20.1 us -> 21.8 us
    all_to_all x1, blocking collectives: 14.1 us -> 12 us  [swap_all(): return lax.all_to_all(block, axes, split_axis=0, concat_axis=0, tiled=True)]
    all_to_all x3, waiting for transfers between devices: 15.5 us -> 17.1 us  [swap_all(): return lax.all_to_all(block, axes, split_axis=0, concat_axis=0, tiled=True)]
where the time goes in v6:
time: 107 us; the launch traced here: 106 us
  starting transfers between devices  52.2 us (49%)
  waiting for transfers between devices  21.8 us (20%)
  Pallas kernels  14.8 us (14%)
  blocking collectives  12 us (11%)
  local copies, waits for them, and re-layouts  4.46 us (4%)
    all_to_all x3, starting transfers between devices, swap_all(): return lax.all_to_all(block, axes, split_axis=0, concat_axis=0, tiled=True)  28.3 us
    ppermute x6, starting transfers between devices, moved(): return lax.ppermute(part, 'x', [(p, (p + step) % 4) for p in range(4)])  18.1 us
    all_to_all x3, waiting for transfers between devices, swap_all(): return lax.all_to_all(block, axes, split_axis=0, concat_axis=0, tiled=True)  17.1 us
    pallas_call x4, Pallas kernels, local_call(): pl.pallas_call(body, out_shape=[jax.ShapeDtypeStruct(shape, dtype) for sh...  14.8 us
    all_to_all x1, blocking collectives, swap_all(): return lax.all_to_all(block, axes, split_axis=0, concat_axis=0, tiled=True)  12 us
    ppermute x1, starting transfers between devices, shards(): other = lax.ppermute(got, 'c', [(0, 1), (1, 0)])  5.79 us
    ppermute x6, waiting for transfers between devices, moved(): return lax.ppermute(part, 'x', [(p, (p + step) % 4) for p in range(4)])  4.68 us
  transfers between devices with their start and end apart: 10, of which 4 were waited for; matrix products, arithmetic and copies ran while one was open for 3% of the time, Pallas kernels for 2%

profile of v6, /device:TPU:1, one launch (start us, length us, event | category | flops | bytes accessed | tf_op | source)
XLA Modules:
  0.0 106.3 jit_solution(6438018715495835612)
XLA Ops:
  0.0 2.4 %shard_map.91 = bf16[64,17,4,128]{3,2,1,0:T(4,128)(2,1)} custom-call(bf16[4,4096]{1,0:T(4,128)(2,1)} %refs_0_.1, bf16[4,8192]{1,0:T(4,128)(2,1)} %refs_1_.1, bf16[4,512]{1,0:T(4,128)(2,1)} %refs_2_.2, bf16[4,8192]{1,0:T(4,128)(2,1)} %refs_3_.1, f32[512,128]{1,0:T(8,128)} %refs_7_), custom_call_target="tpu_custom_call" | custom-call | flops 1000 | bytes 1000 | tf_op jit(solution)/shard_map/pallas_call | solution.py:168
  2.5 17.3 %all-to-all-start = ((bf16[64,17,4,128]{3,2,1,0:T(4,128)(2,1)}), bf16[64,17,4,128]{3,2,1,0:T(4,128)(2,1)S(1)}, u32[]{:S(2)}, u32[]{:S(2)}) async-start(bf16[64,17,4,128]{3,2,1,0:T(4,128)(2,1)} %shard_map.91), calls=%async_computation | async-start | bytes 2228224 | tf_op jit(solution)/shard_map/all_to_all | solution.py:21
  19.8 4.4 %collective-permute-start.1 = (f32[512,128]{1,0:T(8,128)S(1)}, f32[512,128]{1,0:T(8,128)S(1)}, u32[]{:S(2)}, u32[]{:S(2)}) collective-permute-start(f32[512,128]{1,0:T(8,128)S(1)} %copy-done), channel_id=1, source_target_pairs={{0,24},{8,0},{16,8},{24,16},{1,25},{9,1},{17,9},{25,17},{2,26},{10... | collective-permute-start | bytes 786440 | tf_op jit(solution)/shard_map/ppermute | solution.py:181
  24.2 2.5 %collective-permute-start.5 = (bf16[512,128]{1,0:T(8,128)(2,1)S(1)}, bf16[512,128]{1,0:T(8,128)(2,1)S(1)}, u32[]{:S(2)}, u32[]{:S(2)}) collective-permute-start(bf16[512,128]{1,0:T(8,128)(2,1)S(1)} %copy-done.4), channel_id=1, source_target_pairs={{0,24},{8,0},{16,8},{24,16},{1,25},{9,1},{17,9},{25,17},{2,26},{10... | collective-permute-start | bytes 393224 | tf_op jit(solution)/shard_map/ppermute | solution.py:181
  26.6 2.8 %collective-permute-start.3 = (bf16[512,128]{1,0:T(8,128)(2,1)S(1)}, bf16[512,128]{1,0:T(8,128)(2,1)S(1)}, u32[]{:S(2)}, u32[]{:S(2)}) collective-permute-start(bf16[512,128]{1,0:T(8,128)(2,1)S(1)} %copy-done.4), channel_id=1, source_target_pairs={{0,8},{8,16},{16,24},{24,0},{1,9},{9,17},{17,25},{25,1},{2,10},{10... | collective-permute-start | bytes 393224 | tf_op jit(solution)/shard_map/ppermute | solution.py:181
  29.5 1.9 %collective-permute-start = (f32[512,128]{1,0:T(8,128)S(1)}, f32[512,128]{1,0:T(8,128)S(1)}, u32[]{:S(2)}, u32[]{:S(2)}) collective-permute-start(f32[512,128]{1,0:T(8,128)S(1)} %copy-done), channel_id=1, source_target_pairs={{0,8},{8,16},{16,24},{24,0},{1,9},{9,17},{17,25},{25,1},{2,10},{10... | collective-permute-start | bytes 786440 | tf_op jit(solution)/shard_map/ppermute | solution.py:181
  31.4 0.4 reshape.452
  32.7 4.6 %collective-permute-start.2 = (f32[512,128]{1,0:T(8,128)S(1)}, f32[512,128]{1,0:T(8,128)S(1)}, u32[]{:S(2)}, u32[]{:S(2)}) collective-permute-start(f32[512,128]{1,0:T(8,128)S(1)} %collective-permute-done.1.refs_10_), channel_id=1, source_target_pairs={{0,24},{8,0},{16,8},{24,16},{1,25},{9,1},{17,9},{25,17},{2,26},{10... | collective-permute-start | bytes 786440 | tf_op jit(solution)/shard_map/ppermute | solution.py:181
  37.5 0.7 reshape.456.refs_6_
  38.2 1.9 %collective-permute-start.4 = (bf16[512,128]{1,0:T(8,128)(2,1)S(1)}, bf16[512,128]{1,0:T(8,128)(2,1)S(1)}, u32[]{:S(2)}, u32[]{:S(2)}) collective-permute-start(bf16[512,128]{1,0:T(8,128)(2,1)S(1)} %collective-permute-done.3.refs_4_), channel_id=1, source_target_pairs={{0,8},{8,16},{16,24},{24,0},{1,9},{9,17},{17,25},{25,1},{2,10},{10... | collective-permute-start | bytes 393224 | tf_op jit(solution)/shard_map/ppermute | solution.py:181
  40.1 0.6 fusion.refs_7_
  40.7 4.7 %collective-permute-done.4.refs_5_ = bf16[512,128]{1,0:T(8,128)(2,1)S(1)} collective-permute-done((bf16[512,128]{1,0:T(8,128)(2,1)S(1)}, bf16[512,128]{1,0:T(8,128)(2,1)S(1)}, u32[]{:S(2)}, u32[]{:S(2)}) %collective-permute-start.4) | collective-permute-done | bytes 131104 | tf_op jit(solution)/shard_map/ppermute | solution.py:181
  45.4 2.4 %all-to-all-done.refs_0_ = bf16[64,17,4,128]{3,2,1,0:T(4,128)(2,1)S(1)} async-done(((bf16[64,17,4,128]{3,2,1,0:T(4,128)(2,1)}), bf16[64,17,4,128]{3,2,1,0:T(4,128)(2,1)S(1)}, u32[]{:S(2)}, u32[]{:S(2)}) %all-to-all-start) | async-done | bytes 1114144 | tf_op jit(solution)/shard_map/all_to_all | solution.py:21
  47.8 0.9 shard_map.92
  48.7 5.8 %collective-permute-start.6 = (bf16[64,17,4,128]{3,2,1,0:T(4,128)(2,1)S(1)}, bf16[64,17,4,128]{3,2,1,0:T(4,128)(2,1)S(1)}, u32[]{:S(2)}, u32[]{:S(2)}) collective-permute-start(bf16[64,17,4,128]{3,2,1,0:T(4,128)(2,1)S(1)} %all-to-all-done.refs_0_), channel_id=1, source_target_pairs={{0,1},{1,0},{2,3},{3,2},{4,5},{5,4},{6,7},{7,6},{8,9},{9,8},{10,11... | collective-permute-start | bytes 3342344 | tf_op jit(solution)/shard_map/ppermute | solution.py:224
  54.6 4.4 %all-to-all-start.1 = ((bf16[8,264,128]{2,1,0:T(8,128)(2,1)}), bf16[8,264,128]{2,1,0:T(8,128)(2,1)S(1)}, u32[]{:S(2)}, u32[]{:S(2)}) async-start(bf16[8,264,128]{2,1,0:T(8,128)(2,1)} %shard_map.92), calls=%async_computation.1 | async-start | bytes 1081344 | tf_op jit(solution)/shard_map/all_to_all | solution.py:21
  60.0 2.5 %shard_map.93 = (bf16[512,512]{1,0:T(8,128)(2,1)S(1)}, bf16[512,512]{1,0:T(8,128)(2,1)S(1)}, bf16[512,512]{1,0:T(8,128)(2,1)S(1)}, f32[512,512]{1,0:T(8,128)S(1)}) custom-call(bf16[12,256,128]{2,1,0:T(8,128)(2,1)S(1)} %bitcast.19, bf16[8,256,128]{2,1,0:T(8,128)(2,1)S(1)} %bitcast.20, bf16[512,512]{1,0:T(8,128)(2,1)} %refs_5_.1, bf16[512,128]{1,0:T(8,128)(2,1)} %refs_3_.2, ...), custom_call_target="tpu_custom_call" | custom-call | flops 1000 | bytes 1000 | tf_op jit(solution)/shard_map/pallas_call | solution.py:168
  62.5 6.0 %all-to-all-done.1.refs_4_ = bf16[8,264,128]{2,1,0:T(8,128)(2,1)S(1)} async-done(((bf16[8,264,128]{2,1,0:T(8,128)(2,1)}), bf16[8,264,128]{2,1,0:T(8,128)(2,1)S(1)}, u32[]{:S(2)}, u32[]{:S(2)}) %all-to-all-start.1) | async-done | bytes 540704 | tf_op jit(solution)/shard_map/all_to_all | solution.py:21
  68.6 9.0 %shard_map.94 = f32[8,256]{1,0:T(8,128)S(1)} custom-call(bf16[512,512]{1,0:T(8,128)(2,1)S(1)} %get-tuple-element.38.refs_0_, bf16[512,512]{1,0:T(8,128)(2,1)S(1)} %get-tuple-element.39.refs_1_, bf16[512,512]{1,0:T(8,128)(2,1)S(1)} %get-tuple-element.40.refs_2_, f32[512,512]{1,0:T(8,128)S(1)} %get-tuple-element.41.refs_3_, ...), custom_call_target="tpu_custom_call" | custom-call | flops 1000 | bytes 1000 | tf_op jit(solution)/shard_map/pallas_call | solution.py:168
  77.6 12.0 %all_to_all.25 = f32[16,1,256]{2,1,0:T(1,128)S(1)} all-to-all(f32[16,1,256]{2,1,0:T(1,128)S(1)} %copy.45), channel_id=1, replica_groups=mesh['zh'=2,'y'=8,'x'=4,'zl'=4,'c'=2] {'c','y'}, dimensions={0} | all-to-all | bytes 32768 | tf_op jit(solution)/shard_map/all_to_all | solution.py:21
  89.6 0.6 broadcast_in_dim.2
  90.3 6.6 %all-to-all-start.3 = ((f32[32,1,256]{2,1,0:T(1,128)}), f32[32,1,256]{2,1,0:T(1,128)S(1)}, u32[]{:S(2)}, u32[]{:S(2)}) async-start(f32[32,1,256]{2,1,0:T(1,128)} %broadcast_in_dim.2), calls=%async_computation.3 | async-start | bytes 65536 | tf_op jit(solution)/shard_map/all_to_all | solution.py:21
  96.9 8.7 %all-to-all-done.3 = f32[32,1,256]{2,1,0:T(1,128)S(1)} async-done(((f32[32,1,256]{2,1,0:T(1,128)}), f32[32,1,256]{2,1,0:T(1,128)S(1)}, u32[]{:S(2)}, u32[]{:S(2)}) %all-to-all-start.3) | async-done | bytes 32800 | tf_op jit(solution)/shard_map/all_to_all | solution.py:21
  105.7 0.6 reshape.459
  (46 shorter events, 2.2 us)
Async XLA Ops:
  2.4 17.3 %copy-start = (f32[512,128]{1,0:T(8,128)S(1)}, f32[512,128]{1,0:T(8,128)}, u32[]{:S(2)}) copy-start(f32[512,128]{1,0:T(8,128)} %refs_7_) | copy-start | bytes 786436
  2.4 21.7 %copy-start.4 = (bf16[512,128]{1,0:T(8,128)(2,1)S(1)}, bf16[512,128]{1,0:T(8,128)(2,1)}, u32[]{:S(2)}) copy-start(bf16[512,128]{1,0:T(8,128)(2,1)} %refs_3_.2) | copy-start | bytes 393220
  2.5 29.0 %copy-start.8 = (s32[2048]{0:T(1024)S(1)}, s32[2048]{0:T(1024)}, u32[]{:S(2)}) copy-start(s32[2048]{0:T(1024)} %param.16) | copy-start | bytes 24580
  2.5 34.9 %copy-start.9 = (s32[256]{0:T(256)S(1)}, s32[256]{0:T(256)}, u32[]{:S(2)}) copy-start(s32[256]{0:T(256)} %param.17) | copy-start | bytes 3076
  2.5 45.3 %all-to-all-start = ((bf16[64,17,4,128]{3,2,1,0:T(4,128)(2,1)}), bf16[64,17,4,128]{3,2,1,0:T(4,128)(2,1)S(1)}, u32[]{:S(2)}, u32[]{:S(2)}) async-start(bf16[64,17,4,128]{3,2,1,0:T(4,128)(2,1)} %shard_map.91), calls=%async_computation | async-start | bytes 2228224 | tf_op jit(solution)/shard_map/all_to_all | solution.py:21
  19.8 12.9 %collective-permute-start.1 = (f32[512,128]{1,0:T(8,128)S(1)}, f32[512,128]{1,0:T(8,128)S(1)}, u32[]{:S(2)}, u32[]{:S(2)}) collective-permute-start(f32[512,128]{1,0:T(8,128)S(1)} %copy-done), channel_id=1, source_target_pairs={{0,24},{8,0},{16,8},{24,16},{1,25},{9,1},{17,9},{25,17},{2,26},{10... | collective-permute-start | bytes 786440 | tf_op jit(solution)/shard_map/ppermute | solution.py:181
  24.2 16.5 %collective-permute-start.5 = (bf16[512,128]{1,0:T(8,128)(2,1)S(1)}, bf16[512,128]{1,0:T(8,128)(2,1)S(1)}, u32[]{:S(2)}, u32[]{:S(2)}) collective-permute-start(bf16[512,128]{1,0:T(8,128)(2,1)S(1)} %copy-done.4), channel_id=1, source_target_pairs={{0,24},{8,0},{16,8},{24,16},{1,25},{9,1},{17,9},{25,17},{2,26},{10... | collective-permute-start | bytes 393224 | tf_op jit(solution)/shard_map/ppermute | solution.py:181
  26.6 11.5 %collective-permute-start.3 = (bf16[512,128]{1,0:T(8,128)(2,1)S(1)}, bf16[512,128]{1,0:T(8,128)(2,1)S(1)}, u32[]{:S(2)}, u32[]{:S(2)}) collective-permute-start(bf16[512,128]{1,0:T(8,128)(2,1)S(1)} %copy-done.4), channel_id=1, source_target_pairs={{0,8},{8,16},{16,24},{24,0},{1,9},{9,17},{17,25},{25,1},{2,10},{10... | collective-permute-start | bytes 393224 | tf_op jit(solution)/shard_map/ppermute | solution.py:181
  29.5 15.9 %collective-permute-start = (f32[512,128]{1,0:T(8,128)S(1)}, f32[512,128]{1,0:T(8,128)S(1)}, u32[]{:S(2)}, u32[]{:S(2)}) collective-permute-start(f32[512,128]{1,0:T(8,128)S(1)} %copy-done), channel_id=1, source_target_pairs={{0,8},{8,16},{16,24},{24,0},{1,9},{9,17},{17,25},{25,1},{2,10},{10... | collective-permute-start | bytes 786440 | tf_op jit(solution)/shard_map/ppermute | solution.py:181
  32.7 21.8 %copy-start.1 = (f32[512,128]{1,0:T(8,128)}, f32[512,128]{1,0:T(8,128)S(1)}, u32[]{:S(2)}) copy-start(f32[512,128]{1,0:T(8,128)S(1)} %collective-permute-done.1.refs_10_) | copy-start | bytes 786436
  32.7 12.7 %collective-permute-start.2 = (f32[512,128]{1,0:T(8,128)S(1)}, f32[512,128]{1,0:T(8,128)S(1)}, u32[]{:S(2)}, u32[]{:S(2)}) collective-permute-start(f32[512,128]{1,0:T(8,128)S(1)} %collective-permute-done.1.refs_10_), channel_id=1, source_target_pairs={{0,24},{8,0},{16,8},{24,16},{1,25},{9,1},{17,9},{25,17},{2,26},{10... | collective-permute-start | bytes 786440 | tf_op jit(solution)/shard_map/ppermute | solution.py:181
  38.2 9.6 %copy-start.6 = (bf16[512,128]{1,0:T(8,128)(2,1)}, bf16[512,128]{1,0:T(8,128)(2,1)S(1)}, u32[]{:S(2)}) copy-start(bf16[512,128]{1,0:T(8,128)(2,1)S(1)} %collective-permute-done.3.refs_4_) | copy-start | bytes 393220
  38.2 7.2 %collective-permute-start.4 = (bf16[512,128]{1,0:T(8,128)(2,1)S(1)}, bf16[512,128]{1,0:T(8,128)(2,1)S(1)}, u32[]{:S(2)}, u32[]{:S(2)}) collective-permute-start(bf16[512,128]{1,0:T(8,128)(2,1)S(1)} %collective-permute-done.3.refs_4_), channel_id=1, source_target_pairs={{0,8},{8,16},{16,24},{24,0},{1,9},{9,17},{17,25},{25,1},{2,10},{10... | collective-permute-start | bytes 393224 | tf_op jit(solution)/shard_map/ppermute | solution.py:181
  40.7 7.1 %copy-start.5 = (bf16[512,128]{1,0:T(8,128)(2,1)}, bf16[512,128]{1,0:T(8,128)(2,1)S(1)}, u32[]{:S(2)}) copy-start(bf16[512,128]{1,0:T(8,128)(2,1)S(1)} %collective-permute-done.5.refs_6_) | copy-start | bytes 393220
  45.4 2.4 %copy-start.7 = (bf16[512,128]{1,0:T(8,128)(2,1)}, bf16[512,128]{1,0:T(8,128)(2,1)S(1)}, u32[]{:S(2)}) copy-start(bf16[512,128]{1,0:T(8,128)(2,1)S(1)} %collective-permute-done.4.refs_5_) | copy-start | bytes 393220
  45.4 9.2 %copy-start.2 = (f32[512,128]{1,0:T(8,128)}, f32[512,128]{1,0:T(8,128)S(1)}, u32[]{:S(2)}) copy-start(f32[512,128]{1,0:T(8,128)S(1)} %collective-permute-done.refs_8_) | copy-start | bytes 786436
  45.4 9.2 %copy-start.3 = (f32[512,128]{1,0:T(8,128)}, f32[512,128]{1,0:T(8,128)S(1)}, u32[]{:S(2)}) copy-start(f32[512,128]{1,0:T(8,128)S(1)} %collective-permute-done.2.refs_9_) | copy-start | bytes 786436
  48.7 10.9 %collective-permute-start.6 = (bf16[64,17,4,128]{3,2,1,0:T(4,128)(2,1)S(1)}, bf16[64,17,4,128]{3,2,1,0:T(4,128)(2,1)S(1)}, u32[]{:S(2)}, u32[]{:S(2)}) collective-permute-start(bf16[64,17,4,128]{3,2,1,0:T(4,128)(2,1)S(1)} %all-to-all-done.refs_0_), channel_id=1, source_target_pairs={{0,1},{1,0},{2,3},{3,2},{4,5},{5,4},{6,7},{7,6},{8,9},{9,8},{10,11... | collective-permute-start | bytes 3342344 | tf_op jit(solution)/shard_map/ppermute | solution.py:224
  54.6 14.0 %all-to-all-start.1 = ((bf16[8,264,128]{2,1,0:T(8,128)(2,1)}), bf16[8,264,128]{2,1,0:T(8,128)(2,1)S(1)}, u32[]{:S(2)}, u32[]{:S(2)}) async-start(bf16[8,264,128]{2,1,0:T(8,128)(2,1)} %shard_map.92), calls=%async_computation.1 | async-start | bytes 1081344 | tf_op jit(solution)/shard_map/all_to_all | solution.py:21
  90.3 15.3 %all-to-all-start.3 = ((f32[32,1,256]{2,1,0:T(1,128)}), f32[32,1,256]{2,1,0:T(1,128)S(1)}, u32[]{:S(2)}, u32[]{:S(2)}) async-start(f32[32,1,256]{2,1,0:T(1,128)} %broadcast_in_dim.2), calls=%async_computation.3 | async-start | bytes 65536 | tf_op jit(solution)/shard_map/all_to_all | solution.py:21

commit v7 on v6

--- a/solution.py
+++ b/solution.py
@@ -38,7 +38,7 @@
         own = act[:, pl.ds(pl.multiple_of(z * 1024 + c * 512, 128), 512)]
         away = act[:, pl.ds(pl.multiple_of(z * 1024 + 512 - c * 512, 128), 512)]
         for k in range(16):
-            to, m = k * 4 + z, k % 2 * 8 + k // 2
+            to, m = k * 4 + z, k
             for t in range(4):
                 part = slice(t * 128, t * 128 + 128)
                 cols = slice(m * 512 + t * 128, m * 512 + t * 128 + 128)
@@ -207,15 +207,14 @@
     message, eigenvalues, grad_basis = lax.optimization_barrier((message, eigenvalues, grad_basis))
     eigens = ring_parts(eigenvalues, 3)
     bases = ring_parts(grad_basis, 1)
-    got = swap_all(message, ("y", "zh", "zl"))
+    got = swap_all(message, ("zh", "y", "zl"))
 
     ids = lax.dynamic_index_in_dim(example_ids.reshape(2, 8, 4, 4, 2, 4), x, 2, keepdims=False)
-    ids = jnp.transpose(ids, (1, 0, 2, 3, 4))
     ids_own = lax.dynamic_index_in_dim(ids, c, 3, keepdims=False).reshape(1, 256)
     ids_other = lax.dynamic_index_in_dim(ids, 1 - c, 3, keepdims=False).reshape(1, 256)
     ids = jnp.concatenate([ids_own, ids_other], axis=1)
     ids = ids // 64 * 64 + ids % 8 * 8 + ids % 64 // 8
-    query_order = jnp.transpose(query_ids.reshape(2, 8, 4, 4), (2, 1, 0, 3)).reshape(1, 256)
+    query_order = jnp.transpose(query_ids.reshape(2, 8, 4, 4), (2, 0, 1, 3)).reshape(1, 256)
     got, eigens, bases, ids, query_order = lax.optimization_barrier((got, eigens, bases, ids, query_order))
 
     (queries,) = local_call(relay_kernel, 6, [((8, 264, 128), BF)], (got,), ())

time: 107 us -> 107 us (level)
  starting transfers between devices: 52.2 us -> 48.7 us
  blocking collectives: 12 us -> 14.6 us
    all_to_all x1, blocking collectives: 12 us -> 14.6 us  [swap_all(): return lax.all_to_all(block, axes, split_axis=0, concat_axis=0, tiled=True)]
    ppermute x1, starting transfers between devices: 5.79 us -> 3.66 us  [shards(): other = lax.ppermute(got, 'c', [(0, 1), (1, 0)])]
    all_to_all x3, starting transfers between devices: 28.3 us -> 27 us  [swap_all(): return lax.all_to_all(block, axes, split_axis=0, concat_axis=0, tiled=True)]
where the time goes in v7:
time: 107 us; the launch traced here: 106 us
  starting transfers between devices  48.7 us (46%)
  waiting for transfers between devices  22.7 us (21%)
  Pallas kernels  14.8 us (14%)
  blocking collectives  14.6 us (14%)
  local copies, waits for them, and re-layouts  4.04 us (4%)
    all_to_all x3, starting transfers between devices, swap_all(): return lax.all_to_all(block, axes, split_axis=0, concat_axis=0, tiled=True)  27 us
    ppermute x6, starting transfers between devices, moved(): return lax.ppermute(part, 'x', [(p, (p + step) % 4) for p in range(4)])  18.1 us
    all_to_all x3, waiting for transfers between devices, swap_all(): return lax.all_to_all(block, axes, split_axis=0, concat_axis=0, tiled=True)  18 us
    pallas_call x4, Pallas kernels, local_call(): pl.pallas_call(body, out_shape=[jax.ShapeDtypeStruct(shape, dtype) for sh...  14.8 us
    all_to_all x1, blocking collectives, swap_all(): return lax.all_to_all(block, axes, split_axis=0, concat_axis=0, tiled=True)  14.6 us
    ppermute x6, waiting for transfers between devices, moved(): return lax.ppermute(part, 'x', [(p, (p + step) % 4) for p in range(4)])  4.7 us
    ppermute x1, starting transfers between devices, shards(): other = lax.ppermute(got, 'c', [(0, 1), (1, 0)])  3.66 us
  transfers between devices with their start and end apart: 10, of which 4 were waited for; matrix products, arithmetic and copies ran while one was open for 3% of the time, Pallas kernels for 2%

profile of v7, /device:TPU:1, one launch (start us, length us, event | category | flops | bytes accessed | tf_op | source)
XLA Modules:
  0.0 105.9 jit_solution(8208223190892493707)
XLA Ops:
  0.0 2.4 %shard_map.91 = bf16[64,17,4,128]{3,2,1,0:T(4,128)(2,1)} custom-call(bf16[4,4096]{1,0:T(4,128)(2,1)} %refs_0_.1, bf16[4,8192]{1,0:T(4,128)(2,1)} %refs_1_.1, bf16[4,512]{1,0:T(4,128)(2,1)} %refs_2_.2, bf16[4,8192]{1,0:T(4,128)(2,1)} %refs_3_.1, f32[512,128]{1,0:T(8,128)} %refs_7_), custom_call_target="tpu_custom_call" | custom-call | flops 1000 | bytes 1000 | tf_op jit(solution)/shard_map/pallas_call | solution.py:168
  2.5 17.3 %all-to-all-start = ((bf16[64,17,4,128]{3,2,1,0:T(4,128)(2,1)}), bf16[64,17,4,128]{3,2,1,0:T(4,128)(2,1)S(1)}, u32[]{:S(2)}, u32[]{:S(2)}) async-start(bf16[64,17,4,128]{3,2,1,0:T(4,128)(2,1)} %shard_map.91), calls=%async_computation | async-start | bytes 2228224 | tf_op jit(solution)/shard_map/all_to_all | solution.py:21
  19.8 4.4 %collective-permute-start.1 = (f32[512,128]{1,0:T(8,128)S(1)}, f32[512,128]{1,0:T(8,128)S(1)}, u32[]{:S(2)}, u32[]{:S(2)}) collective-permute-start(f32[512,128]{1,0:T(8,128)S(1)} %copy-done), channel_id=1, source_target_pairs={{0,24},{8,0},{16,8},{24,16},{1,25},{9,1},{17,9},{25,17},{2,26},{10... | collective-permute-start | bytes 786440 | tf_op jit(solution)/shard_map/ppermute | solution.py:181
  24.2 2.5 %collective-permute-start.5 = (bf16[512,128]{1,0:T(8,128)(2,1)S(1)}, bf16[512,128]{1,0:T(8,128)(2,1)S(1)}, u32[]{:S(2)}, u32[]{:S(2)}) collective-permute-start(bf16[512,128]{1,0:T(8,128)(2,1)S(1)} %copy-done.4), channel_id=1, source_target_pairs={{0,24},{8,0},{16,8},{24,16},{1,25},{9,1},{17,9},{25,17},{2,26},{10... | collective-permute-start | bytes 393224 | tf_op jit(solution)/shard_map/ppermute | solution.py:181
  26.6 2.8 %collective-permute-start.3 = (bf16[512,128]{1,0:T(8,128)(2,1)S(1)}, bf16[512,128]{1,0:T(8,128)(2,1)S(1)}, u32[]{:S(2)}, u32[]{:S(2)}) collective-permute-start(bf16[512,128]{1,0:T(8,128)(2,1)S(1)} %copy-done.4), channel_id=1, source_target_pairs={{0,8},{8,16},{16,24},{24,0},{1,9},{9,17},{17,25},{25,1},{2,10},{10... | collective-permute-start | bytes 393224 | tf_op jit(solution)/shard_map/ppermute | solution.py:181
  29.5 1.9 %collective-permute-start = (f32[512,128]{1,0:T(8,128)S(1)}, f32[512,128]{1,0:T(8,128)S(1)}, u32[]{:S(2)}, u32[]{:S(2)}) collective-permute-start(f32[512,128]{1,0:T(8,128)S(1)} %copy-done), channel_id=1, source_target_pairs={{0,8},{8,16},{16,24},{24,0},{1,9},{9,17},{17,25},{25,1},{2,10},{10... | collective-permute-start | bytes 786440 | tf_op jit(solution)/shard_map/ppermute | solution.py:181
  31.4 0.4 reshape.450
  32.3 4.6 %collective-permute-start.2 = (f32[512,128]{1,0:T(8,128)S(1)}, f32[512,128]{1,0:T(8,128)S(1)}, u32[]{:S(2)}, u32[]{:S(2)}) collective-permute-start(f32[512,128]{1,0:T(8,128)S(1)} %collective-permute-done.1.refs_10_), channel_id=1, source_target_pairs={{0,24},{8,0},{16,8},{24,16},{1,25},{9,1},{17,9},{25,17},{2,26},{10... | collective-permute-start | bytes 786440 | tf_op jit(solution)/shard_map/ppermute | solution.py:181
  37.1 0.7 reshape.452.refs_6_
  37.7 1.9 %collective-permute-start.4 = (bf16[512,128]{1,0:T(8,128)(2,1)S(1)}, bf16[512,128]{1,0:T(8,128)(2,1)S(1)}, u32[]{:S(2)}, u32[]{:S(2)}) collective-permute-start(bf16[512,128]{1,0:T(8,128)(2,1)S(1)} %collective-permute-done.3.refs_4_), channel_id=1, source_target_pairs={{0,8},{8,16},{16,24},{24,0},{1,9},{9,17},{17,25},{25,1},{2,10},{10... | collective-permute-start | bytes 393224 | tf_op jit(solution)/shard_map/ppermute | solution.py:181
  39.7 0.6 fusion.refs_7_
  40.3 4.7 %collective-permute-done.4.refs_5_ = bf16[512,128]{1,0:T(8,128)(2,1)S(1)} collective-permute-done((bf16[512,128]{1,0:T(8,128)(2,1)S(1)}, bf16[512,128]{1,0:T(8,128)(2,1)S(1)}, u32[]{:S(2)}, u32[]{:S(2)}) %collective-permute-start.4) | collective-permute-done | bytes 131104 | tf_op jit(solution)/shard_map/ppermute | solution.py:181
  45.0 3.4 %all-to-all-done.refs_0_ = bf16[64,17,4,128]{3,2,1,0:T(4,128)(2,1)S(1)} async-done(((bf16[64,17,4,128]{3,2,1,0:T(4,128)(2,1)}), bf16[64,17,4,128]{3,2,1,0:T(4,128)(2,1)S(1)}, u32[]{:S(2)}, u32[]{:S(2)}) %all-to-all-start) | async-done | bytes 1114144 | tf_op jit(solution)/shard_map/all_to_all | solution.py:21
  48.4 0.9 shard_map.92
  49.3 3.7 %collective-permute-start.6 = (bf16[64,17,4,128]{3,2,1,0:T(4,128)(2,1)S(1)}, bf16[64,17,4,128]{3,2,1,0:T(4,128)(2,1)S(1)}, u32[]{:S(2)}, u32[]{:S(2)}) collective-permute-start(bf16[64,17,4,128]{3,2,1,0:T(4,128)(2,1)S(1)} %all-to-all-done.refs_0_), channel_id=1, source_target_pairs={{0,1},{1,0},{2,3},{3,2},{4,5},{5,4},{6,7},{7,6},{8,9},{9,8},{10,11... | collective-permute-start | bytes 3342344 | tf_op jit(solution)/shard_map/ppermute | solution.py:223
  53.0 4.4 %all-to-all-start.1 = ((bf16[8,264,128]{2,1,0:T(8,128)(2,1)}), bf16[8,264,128]{2,1,0:T(8,128)(2,1)S(1)}, u32[]{:S(2)}, u32[]{:S(2)}) async-start(bf16[8,264,128]{2,1,0:T(8,128)(2,1)} %shard_map.92), calls=%async_computation.1 | async-start | bytes 1081344 | tf_op jit(solution)/shard_map/all_to_all | solution.py:21
  58.4 2.5 %shard_map.93 = (bf16[512,512]{1,0:T(8,128)(2,1)S(1)}, bf16[512,512]{1,0:T(8,128)(2,1)S(1)}, bf16[512,512]{1,0:T(8,128)(2,1)S(1)}, f32[512,512]{1,0:T(8,128)S(1)}) custom-call(bf16[12,256,128]{2,1,0:T(8,128)(2,1)S(1)} %bitcast.11, bf16[8,256,128]{2,1,0:T(8,128)(2,1)S(1)} %bitcast.12, bf16[512,512]{1,0:T(8,128)(2,1)} %refs_5_.1, bf16[512,128]{1,0:T(8,128)(2,1)} %refs_3_.2, ...), custom_call_target="tpu_custom_call" | custom-call | flops 1000 | bytes 1000 | tf_op jit(solution)/shard_map/pallas_call | solution.py:168
  61.0 6.0 %all-to-all-done.1.refs_4_ = bf16[8,264,128]{2,1,0:T(8,128)(2,1)S(1)} async-done(((bf16[8,264,128]{2,1,0:T(8,128)(2,1)}), bf16[8,264,128]{2,1,0:T(8,128)(2,1)S(1)}, u32[]{:S(2)}, u32[]{:S(2)}) %all-to-all-start.1) | async-done | bytes 540704 | tf_op jit(solution)/shard_map/all_to_all | solution.py:21
  67.0 9.0 %shard_map.94 = f32[8,256]{1,0:T(8,128)S(1)} custom-call(bf16[512,512]{1,0:T(8,128)(2,1)S(1)} %get-tuple-element.38.refs_0_, bf16[512,512]{1,0:T(8,128)(2,1)S(1)} %get-tuple-element.39.refs_1_, bf16[512,512]{1,0:T(8,128)(2,1)S(1)} %get-tuple-element.40.refs_2_, f32[512,512]{1,0:T(8,128)S(1)} %get-tuple-element.41.refs_3_, ...), custom_call_target="tpu_custom_call" | custom-call | flops 1000 | bytes 1000 | tf_op jit(solution)/shard_map/pallas_call | solution.py:168
  76.0 14.6 %all_to_all.25 = f32[16,1,256]{2,1,0:T(1,128)S(1)} all-to-all(f32[16,1,256]{2,1,0:T(1,128)S(1)} %copy.26), channel_id=1, replica_groups=mesh['zh'=2,'y'=8,'x'=4,'zl'=4,'c'=2] {'c','y'}, dimensions={0} | all-to-all | bytes 32768 | tf_op jit(solution)/shard_map/all_to_all | solution.py:21
  90.6 0.6 broadcast_in_dim.2
  91.2 5.3 %all-to-all-start.3 = ((f32[32,1,256]{2,1,0:T(1,128)}), f32[32,1,256]{2,1,0:T(1,128)S(1)}, u32[]{:S(2)}, u32[]{:S(2)}) async-start(f32[32,1,256]{2,1,0:T(1,128)} %broadcast_in_dim.2), calls=%async_computation.3 | async-start | bytes 65536 | tf_op jit(solution)/shard_map/all_to_all | solution.py:21
  96.5 8.6 %all-to-all-done.3 = f32[32,1,256]{2,1,0:T(1,128)S(1)} async-done(((f32[32,1,256]{2,1,0:T(1,128)}), f32[32,1,256]{2,1,0:T(1,128)S(1)}, u32[]{:S(2)}, u32[]{:S(2)}) %all-to-all-start.3) | async-done | bytes 32800 | tf_op jit(solution)/shard_map/all_to_all | solution.py:21
  105.3 0.6 reshape.455
  (42 shorter events, 1.8 us)
Async XLA Ops:
  2.4 17.3 %copy-start = (f32[512,128]{1,0:T(8,128)S(1)}, f32[512,128]{1,0:T(8,128)}, u32[]{:S(2)}) copy-start(f32[512,128]{1,0:T(8,128)} %refs_7_) | copy-start | bytes 786436
  2.4 21.7 %copy-start.4 = (bf16[512,128]{1,0:T(8,128)(2,1)S(1)}, bf16[512,128]{1,0:T(8,128)(2,1)}, u32[]{:S(2)}) copy-start(bf16[512,128]{1,0:T(8,128)(2,1)} %refs_3_.2) | copy-start | bytes 393220
  2.4 29.0 %copy-start.8 = (s32[2048]{0:T(1024)S(1)}, s32[2048]{0:T(1024)}, u32[]{:S(2)}) copy-start(s32[2048]{0:T(1024)} %param.16) | copy-start | bytes 24580
  2.5 34.5 %copy-start.9 = (s32[256]{0:T(256)S(1)}, s32[256]{0:T(256)}, u32[]{:S(2)}) copy-start(s32[256]{0:T(256)} %param.17) | copy-start | bytes 3076
  2.5 45.9 %all-to-all-start = ((bf16[64,17,4,128]{3,2,1,0:T(4,128)(2,1)}), bf16[64,17,4,128]{3,2,1,0:T(4,128)(2,1)S(1)}, u32[]{:S(2)}, u32[]{:S(2)}) async-start(bf16[64,17,4,128]{3,2,1,0:T(4,128)(2,1)} %shard_map.91), calls=%async_computation | async-start | bytes 2228224 | tf_op jit(solution)/shard_map/all_to_all | solution.py:21
  19.8 12.5 %collective-permute-start.1 = (f32[512,128]{1,0:T(8,128)S(1)}, f32[512,128]{1,0:T(8,128)S(1)}, u32[]{:S(2)}, u32[]{:S(2)}) collective-permute-start(f32[512,128]{1,0:T(8,128)S(1)} %copy-done), channel_id=1, source_target_pairs={{0,24},{8,0},{16,8},{24,16},{1,25},{9,1},{17,9},{25,17},{2,26},{10... | collective-permute-start | bytes 786440 | tf_op jit(solution)/shard_map/ppermute | solution.py:181
  24.2 16.1 %collective-permute-start.5 = (bf16[512,128]{1,0:T(8,128)(2,1)S(1)}, bf16[512,128]{1,0:T(8,128)(2,1)S(1)}, u32[]{:S(2)}, u32[]{:S(2)}) collective-permute-start(bf16[512,128]{1,0:T(8,128)(2,1)S(1)} %copy-done.4), channel_id=1, source_target_pairs={{0,24},{8,0},{16,8},{24,16},{1,25},{9,1},{17,9},{25,17},{2,26},{10... | collective-permute-start | bytes 393224 | tf_op jit(solution)/shard_map/ppermute | solution.py:181
  26.6 11.1 %collective-permute-start.3 = (bf16[512,128]{1,0:T(8,128)(2,1)S(1)}, bf16[512,128]{1,0:T(8,128)(2,1)S(1)}, u32[]{:S(2)}, u32[]{:S(2)}) collective-permute-start(bf16[512,128]{1,0:T(8,128)(2,1)S(1)} %copy-done.4), channel_id=1, source_target_pairs={{0,8},{8,16},{16,24},{24,0},{1,9},{9,17},{17,25},{25,1},{2,10},{10... | collective-permute-start | bytes 393224 | tf_op jit(solution)/shard_map/ppermute | solution.py:181
  29.5 15.5 %collective-permute-start = (f32[512,128]{1,0:T(8,128)S(1)}, f32[512,128]{1,0:T(8,128)S(1)}, u32[]{:S(2)}, u32[]{:S(2)}) collective-permute-start(f32[512,128]{1,0:T(8,128)S(1)} %copy-done), channel_id=1, source_target_pairs={{0,8},{8,16},{16,24},{24,0},{1,9},{9,17},{17,25},{25,1},{2,10},{10... | collective-permute-start | bytes 786440 | tf_op jit(solution)/shard_map/ppermute | solution.py:181
  32.3 20.7 %copy-start.1 = (f32[512,128]{1,0:T(8,128)}, f32[512,128]{1,0:T(8,128)S(1)}, u32[]{:S(2)}) copy-start(f32[512,128]{1,0:T(8,128)S(1)} %collective-permute-done.1.refs_10_) | copy-start | bytes 786436
  32.3 12.6 %collective-permute-start.2 = (f32[512,128]{1,0:T(8,128)S(1)}, f32[512,128]{1,0:T(8,128)S(1)}, u32[]{:S(2)}, u32[]{:S(2)}) collective-permute-start(f32[512,128]{1,0:T(8,128)S(1)} %collective-permute-done.1.refs_10_), channel_id=1, source_target_pairs={{0,24},{8,0},{16,8},{24,16},{1,25},{9,1},{17,9},{25,17},{2,26},{10... | collective-permute-start | bytes 786440 | tf_op jit(solution)/shard_map/ppermute | solution.py:181
  37.7 10.6 %copy-start.6 = (bf16[512,128]{1,0:T(8,128)(2,1)}, bf16[512,128]{1,0:T(8,128)(2,1)S(1)}, u32[]{:S(2)}) copy-start(bf16[512,128]{1,0:T(8,128)(2,1)S(1)} %collective-permute-done.3.refs_4_) | copy-start | bytes 393220
  37.7 7.2 %collective-permute-start.4 = (bf16[512,128]{1,0:T(8,128)(2,1)S(1)}, bf16[512,128]{1,0:T(8,128)(2,1)S(1)}, u32[]{:S(2)}, u32[]{:S(2)}) collective-permute-start(bf16[512,128]{1,0:T(8,128)(2,1)S(1)} %collective-permute-done.3.refs_4_), channel_id=1, source_target_pairs={{0,8},{8,16},{16,24},{24,0},{1,9},{9,17},{17,25},{25,1},{2,10},{10... | collective-permute-start | bytes 393224 | tf_op jit(solution)/shard_map/ppermute | solution.py:181
  40.3 8.1 %copy-start.5 = (bf16[512,128]{1,0:T(8,128)(2,1)}, bf16[512,128]{1,0:T(8,128)(2,1)S(1)}, u32[]{:S(2)}) copy-start(bf16[512,128]{1,0:T(8,128)(2,1)S(1)} %collective-permute-done.5.refs_6_) | copy-start | bytes 393220
  44.9 3.4 %copy-start.7 = (bf16[512,128]{1,0:T(8,128)(2,1)}, bf16[512,128]{1,0:T(8,128)(2,1)S(1)}, u32[]{:S(2)}) copy-start(bf16[512,128]{1,0:T(8,128)(2,1)S(1)} %collective-permute-done.4.refs_5_) | copy-start | bytes 393220
  45.0 8.0 %copy-start.2 = (f32[512,128]{1,0:T(8,128)}, f32[512,128]{1,0:T(8,128)S(1)}, u32[]{:S(2)}) copy-start(f32[512,128]{1,0:T(8,128)S(1)} %collective-permute-done.refs_8_) | copy-start | bytes 786436
  45.0 8.0 %copy-start.3 = (f32[512,128]{1,0:T(8,128)}, f32[512,128]{1,0:T(8,128)S(1)}, u32[]{:S(2)}) copy-start(f32[512,128]{1,0:T(8,128)S(1)} %collective-permute-done.2.refs_9_) | copy-start | bytes 786436
  49.3 8.7 %collective-permute-start.6 = (bf16[64,17,4,128]{3,2,1,0:T(4,128)(2,1)S(1)}, bf16[64,17,4,128]{3,2,1,0:T(4,128)(2,1)S(1)}, u32[]{:S(2)}, u32[]{:S(2)}) collective-permute-start(bf16[64,17,4,128]{3,2,1,0:T(4,128)(2,1)S(1)} %all-to-all-done.refs_0_), channel_id=1, source_target_pairs={{0,1},{1,0},{2,3},{3,2},{4,5},{5,4},{6,7},{7,6},{8,9},{9,8},{10,11... | collective-permute-start | bytes 3342344 | tf_op jit(solution)/shard_map/ppermute | solution.py:223
  53.0 14.0 %all-to-all-start.1 = ((bf16[8,264,128]{2,1,0:T(8,128)(2,1)}), bf16[8,264,128]{2,1,0:T(8,128)(2,1)S(1)}, u32[]{:S(2)}, u32[]{:S(2)}) async-start(bf16[8,264,128]{2,1,0:T(8,128)(2,1)} %shard_map.92), calls=%async_computation.1 | async-start | bytes 1081344 | tf_op jit(solution)/shard_map/all_to_all | solution.py:21
  91.2 13.9 %all-to-all-start.3 = ((f32[32,1,256]{2,1,0:T(1,128)}), f32[32,1,256]{2,1,0:T(1,128)S(1)}, u32[]{:S(2)}, u32[]{:S(2)}) async-start(f32[32,1,256]{2,1,0:T(1,128)} %broadcast_in_dim.2), calls=%async_computation.3 | async-start | bytes 65536 | tf_op jit(solution)/shard_map/all_to_all | solution.py:21
